TPU v7x, 32 devices: a whole 2x2x4 slice. The times are simulated.
32 devices in a mesh: dp: 4 (over y, x), ctx: 2 (over core), mp: 4 (over z).
Axes of the slice: x: 2, y: 2, z: 4, core: 2. Of those that a mesh axis runs over, the one named last changes fastest.
Arguments:
- inputs: bfloat16 [12, 1024, 1536], P('dp', ('ctx', 'mp')), may hold values from -6 to 6
- w_query: bfloat16 [1536, 1536], P(('dp', 'ctx'), 'mp'), may hold values from -0.21875 to 0.21875
- w_key: bfloat16 [1536, 1536], P(('dp', 'ctx'), 'mp'), may hold values from -0.21875 to 0.21875
- w_value: bfloat16 [1536, 1536], P(('dp', 'ctx'), 'mp'), may hold values from -0.15625 to 0.15625
- w_out: bfloat16 [1536, 1536], P('mp', ('dp', 'ctx')), may hold values from -0.875 to 0.875
- w_up: bfloat16 [1536, 8, 768], P(('dp', 'ctx'), None, 'mp'), may hold values from -0.15625 to 0.15625
- w_down: bfloat16 [8, 768, 1536], P(None, 'mp', ('dp', 'ctx')), may hold values from -0.15625 to 0.15625
- gain_attn: bfloat16 [1536], P(('dp', 'ctx')), may hold values from 0.099609375 to 1.8984375
- gain_ffn: bfloat16 [1536], P(('dp', 'ctx')), may hold values from 0.099609375 to 1.8984375
- cotangent: bfloat16 [12, 1024, 1536], P('dp', ('ctx', 'mp')), may hold values from -6 to 6
Outputs:
- outputs: bfloat16 [12, 1024, 1536], P('dp', ('ctx', 'mp'))
- input_grads: float32 [12, 1024, 1536], P('dp', ('ctx', 'mp'))
- grad_query: float32 [1536, 1536], P(('dp', 'ctx'), 'mp')
- grad_key: float32 [1536, 1536], P(('dp', 'ctx'), 'mp')
- grad_value: float32 [1536, 1536], P(('dp', 'ctx'), 'mp')
- grad_out: float32 [1536, 1536], P('mp', ('dp', 'ctx'))
- grad_up: float32 [1536, 8, 768], P(('dp', 'ctx'), None, 'mp')
- grad_down: float32 [8, 768, 1536], P(None, 'mp', ('dp', 'ctx'))
- grad_gain_attn: float32 [1536], P(('dp', 'ctx'))
- grad_gain_ffn: float32 [1536], P(('dp', 'ctx'))
All inputs are finite; a program needn't handle non-finite values.
Results may differ from a plain program's by a relative error of at most 0.015.
Values may be sent and summed in bfloat16 or wider, within the bound.
No kernel may reach another device: no remote copies, remote signals or barrier semaphores. Data moves between devices by JAX's collectives and lax.ppermute only.
A program may use at most 256 MiB of HBM per device.

v0:
```python
import jax
import jax.numpy as jnp
from jax import lax
from jax.sharding import PartitionSpec as P

HEAD = 128


EPSILON = 1e-06
NEGATIVE = -1e30


def from_behind(shard, axis, by):
    devices = lax.axis_size(axis)
    pairs = [(i, i + by) for i in range(devices) if 0 <= i + by < devices]
    return lax.ppermute(shard, axis, pairs)


def normalize(values, gain_vec):
    inv_rms = lax.rsqrt(jnp.mean(values * values, axis=-1, keepdims=True) + EPSILON)
    return values * inv_rms * gain_vec


def unit_rows(values):
    return values * lax.rsqrt(jnp.mean(values * values, axis=-1, keepdims=True) + EPSILON)


def norm_back(values, gain_vec, grad_normed):
    inv_rms = lax.rsqrt(jnp.mean(values * values, axis=-1, keepdims=True) + EPSILON)
    weighted = grad_normed * gain_vec
    return inv_rms * weighted - values * (inv_rms * inv_rms * inv_rms) * jnp.mean(
        weighted * values, axis=-1, keepdims=True
    )


def rotation(positions, head_size):
    half_size = head_size // 2
    frequency = 10000.0 ** (-jnp.arange(half_size, dtype=jnp.float32) / half_size)
    angles = positions.astype(jnp.float32)[:, None] * frequency[None, :]
    return (jnp.cos(angles)[:, None, :], jnp.sin(angles)[:, None, :])


def rotate(values, cosine, sine_part):
    half_size = values.shape[-1] // 2
    leading = values[..., :half_size]
    trailing = values[..., half_size:]
    return jnp.concatenate(
        [leading * cosine - trailing * sine_part, trailing * cosine + leading * sine_part], axis=-1
    )


def gelu_tanh(values):
    return jax.nn.gelu(values, approximate=True)


def local(inputs, w_query, w_key, w_value, w_out, w_up, w_down, gain_attn, gain_ffn, cotangent):
    query_full, key_full, value_full, out_full, up_full, down_full, gain_a_low, gain_f_low = (
        lax.all_gather(w_query, ("dp", "ctx"), axis=0, tiled=True),
        lax.all_gather(w_key, ("dp", "ctx"), axis=0, tiled=True),
        lax.all_gather(w_value, ("dp", "ctx"), axis=0, tiled=True),
        lax.all_gather(w_out, ("dp", "ctx"), axis=1, tiled=True),
        lax.all_gather(w_up, ("dp", "ctx"), axis=0, tiled=True),
        lax.all_gather(w_down, ("dp", "ctx"), axis=2, tiled=True),
        lax.all_gather(gain_attn, ("dp", "ctx"), axis=0, tiled=True),
        lax.all_gather(gain_ffn, ("dp", "ctx"), axis=0, tiled=True),
    )
    gain_first = gain_a_low.astype(jnp.float32)
    gain_second = gain_f_low.astype(jnp.float32)
    inputs_all, cotangent_all = (
        lax.all_gather(inputs, "mp", axis=1, tiled=True),
        lax.all_gather(cotangent, "mp", axis=1, tiled=True),
    )
    count = inputs_all.shape[0]
    length_half = inputs_all.shape[1]
    width = inputs_all.shape[2]
    shard_len = inputs.shape[1]
    total_rows = count * length_half
    mp_count = lax.axis_size("mp")
    mp_index = lax.axis_index("mp")
    ctx_index = lax.axis_index("ctx")
    head_count = query_full.shape[1] // HEAD
    factor = HEAD ** (-0.5)
    positions = ctx_index * length_half + jnp.arange(length_half, dtype=jnp.int32)
    cosine, sine_part = rotation(positions, HEAD)
    inputs_f = inputs_all.astype(jnp.float32)
    flat_first = normalize(inputs_f, gain_first).astype(jnp.bfloat16).reshape(total_rows, width)

    def project(matrix):
        return jnp.dot(flat_first, matrix, preferred_element_type=jnp.float32).reshape(
            count, length_half, head_count, HEAD
        )

    query_rows = rotate(project(query_full), cosine, sine_part).astype(jnp.bfloat16)
    key_rows = rotate(project(key_full), cosine, sine_part).astype(jnp.bfloat16)
    value_rows = project(value_full).astype(jnp.bfloat16)
    early_keys, early_values = from_behind((key_rows, value_rows), "ctx", 1)
    row_ids = jnp.arange(length_half)[:, None]
    col_ids = jnp.arange(2 * length_half)[None, :]
    visible = jnp.where(col_ids < length_half, ctx_index >= 1, col_ids - length_half <= row_ids)

    def scores_of(query_one, keys_all):
        raw_scores = (
            jnp.einsum("qhd,khd->hqk", query_one, keys_all, preferred_element_type=jnp.float32)
            * factor
        )
        return jnp.where(visible[None], raw_scores, NEGATIVE)

    def attend(package):
        query_one, key_one, value_one, key_early, value_early = package
        keys_all = jnp.concatenate([key_early, key_one], 0)
        values_all = jnp.concatenate([value_early, value_one], 0)
        scores = scores_of(query_one, keys_all)
        largest = jnp.max(scores, axis=-1, keepdims=True)
        exponent = jnp.exp(scores - largest)
        totals = jnp.sum(exponent, axis=-1, keepdims=True)
        softened = exponent / totals
        mixed_one = jnp.einsum(
            "hqk,khd->qhd",
            softened.astype(jnp.bfloat16),
            values_all,
            preferred_element_type=jnp.float32,
        )
        return (mixed_one.astype(jnp.bfloat16), (largest + jnp.log(totals))[..., 0])

    mixed_rows, log_totals = lax.map(
        attend, (query_rows, key_rows, value_rows, early_keys, early_values)
    )
    mixed_flat = mixed_rows.reshape(total_rows, head_count * HEAD)
    attended = lax.psum(jnp.dot(mixed_flat, out_full, preferred_element_type=jnp.float32), "mp")
    hidden_state = inputs_f + attended.reshape(count, length_half, width)
    normed_second = (
        normalize(hidden_state, gain_second).astype(jnp.bfloat16).reshape(total_rows, width)
    )
    cot_flat = cotangent_all.reshape(total_rows, width)
    block_width = up_full.shape[2]
    block_total = up_full.shape[1]

    def ffn_both(rows, grad_rows, blocks):
        used = blocks * block_width
        up_part = up_full[:, :blocks].reshape(width, used)
        down_part = down_full[:blocks].reshape(used, width)
        upped = jnp.dot(rows, up_part, preferred_element_type=jnp.float32)
        activated, gelu_pull = jax.vjp(gelu_tanh, upped)
        activated_low = activated.astype(jnp.bfloat16)
        result = jnp.dot(activated_low, down_part, preferred_element_type=jnp.float32)
        grad_act = jnp.einsum("rd,wd->rw", grad_rows, down_part, preferred_element_type=jnp.float32)
        grad_upped = gelu_pull(grad_act)[0].astype(jnp.bfloat16)
        grad_down_part = jnp.einsum(
            "rw,rd->wd", activated_low, grad_rows, preferred_element_type=jnp.float32
        )
        grad_up_part = jnp.einsum("rd,rw->dw", rows, grad_upped, preferred_element_type=jnp.float32)
        grad_in = jnp.einsum("rw,dw->rd", grad_upped, up_part, preferred_element_type=jnp.float32)
        grad_up_pad = jnp.pad(
            grad_up_part.reshape(width, blocks, block_width),
            ((0, 0), (0, block_total - blocks), (0, 0)),
        )
        grad_down_pad = jnp.pad(
            grad_down_part.reshape(blocks, block_width, width),
            ((0, block_total - blocks), (0, 0), (0, 0)),
        )
        return (result, grad_in, grad_up_pad, grad_down_pad)

    def make_branch(blocks):

        def branch_run(rows, grad_rows):
            return ffn_both(rows, grad_rows, blocks)

        return branch_run

    grain = lax.axis_index("dp") % 4
    ffn_part, grad_second_part, grad_up_sum, grad_down_sum = lax.switch(
        grain, [make_branch(2**grain_level) for grain_level in range(4)], normed_second, cot_flat
    )
    grad_second_part = grad_second_part.reshape(count, length_half, width)
    gain_second_part = jnp.sum(grad_second_part * unit_rows(hidden_state), axis=(0, 1))
    ffn_shard, grad_second_shard, gain_second_sum = (
        lax.psum_scatter(
            ffn_part.reshape(count, length_half, width), "mp", scatter_dimension=1, tiled=True
        ),
        lax.psum_scatter(grad_second_part, "mp", scatter_dimension=1, tiled=True),
        lax.psum_scatter(
            jnp.broadcast_to(gain_second_part, (mp_count, width)),
            "mp",
            scatter_dimension=0,
            tiled=True,
        ),
    )
    gain_second_grad = gain_second_sum[0]
    hidden_shard = lax.dynamic_slice_in_dim(hidden_state, mp_index * shard_len, shard_len, 1)
    outputs = (hidden_shard + ffn_shard).astype(jnp.bfloat16)
    grad_hidden_shard = cotangent.astype(jnp.float32) + norm_back(
        hidden_shard, gain_second, grad_second_shard
    )
    grad_hidden_low = lax.all_gather(
        grad_hidden_shard.astype(jnp.bfloat16), "mp", axis=1, tiled=True
    ).reshape(total_rows, width)
    grad_out_w = jnp.einsum(
        "rc,rd->cd", mixed_flat, grad_hidden_low, preferred_element_type=jnp.float32
    )
    grad_mixed = jnp.einsum(
        "rd,cd->rc", grad_hidden_low, out_full, preferred_element_type=jnp.float32
    )
    grad_mixed = grad_mixed.astype(jnp.bfloat16).reshape(count, length_half, head_count, HEAD)

    def attend_back(package):
        query_one, key_one, value_one, key_early, value_early, log_one, grad_one = package
        keys_all = jnp.concatenate([key_early, key_one], 0)
        values_all = jnp.concatenate([value_early, value_one], 0)
        scores = scores_of(query_one, keys_all)
        softened = jnp.exp(scores - log_one[..., None])
        grad_soft = jnp.einsum(
            "qhd,khd->hqk", grad_one, values_all, preferred_element_type=jnp.float32
        )
        grad_values = jnp.einsum(
            "hqk,qhd->khd",
            softened.astype(jnp.bfloat16),
            grad_one,
            preferred_element_type=jnp.float32,
        )
        inner = jnp.sum(grad_soft * softened, axis=-1, keepdims=True)
        grad_scores = (softened * (grad_soft - inner)).astype(jnp.bfloat16)
        grad_queries = (
            jnp.einsum("hqk,khd->qhd", grad_scores, keys_all, preferred_element_type=jnp.float32)
            * factor
        )
        grad_keys = (
            jnp.einsum("hqk,qhd->khd", grad_scores, query_one, preferred_element_type=jnp.float32)
            * factor
        )
        return (
            grad_queries,
            grad_keys[length_half:],
            grad_keys[:length_half],
            grad_values[length_half:],
            grad_values[:length_half],
        )

    grad_queries, grad_key_own, grad_key_early, grad_value_own, grad_value_early = lax.map(
        attend_back,
        (query_rows, key_rows, value_rows, early_keys, early_values, log_totals, grad_mixed),
    )
    key_back, value_back = (
        from_behind(grad_key_early.astype(jnp.bfloat16), "ctx", -1).astype(grad_key_early.dtype),
        from_behind(grad_value_early.astype(jnp.bfloat16), "ctx", -1).astype(
            grad_value_early.dtype
        ),
    )
    grad_query_low = (
        rotate(grad_queries, cosine, -sine_part).astype(jnp.bfloat16).reshape(total_rows, -1)
    )
    grad_key_low = (
        rotate(grad_key_own + key_back, cosine, -sine_part)
        .astype(jnp.bfloat16)
        .reshape(total_rows, -1)
    )
    grad_value_low = (grad_value_own + value_back).astype(jnp.bfloat16).reshape(total_rows, -1)
    grad_query_w = jnp.einsum(
        "rd,rc->dc", flat_first, grad_query_low, preferred_element_type=jnp.float32
    )
    grad_key_w = jnp.einsum(
        "rd,rc->dc", flat_first, grad_key_low, preferred_element_type=jnp.float32
    )
    grad_value_w = jnp.einsum(
        "rd,rc->dc", flat_first, grad_value_low, preferred_element_type=jnp.float32
    )
    grad_first_part = jnp.einsum(
        "rc,dc->rd", grad_query_low, query_full, preferred_element_type=jnp.float32
    )
    grad_first_part = grad_first_part + jnp.einsum(
        "rc,dc->rd", grad_key_low, key_full, preferred_element_type=jnp.float32
    )
    grad_first_part = grad_first_part + jnp.einsum(
        "rc,dc->rd", grad_value_low, value_full, preferred_element_type=jnp.float32
    )
    grad_first_part = grad_first_part.reshape(count, length_half, width)
    gain_first_part = jnp.sum(grad_first_part * unit_rows(inputs_f), axis=(0, 1))
    grad_first_shard, gain_first_sum = (
        lax.psum_scatter(
            grad_first_part.astype(jnp.bfloat16), "mp", scatter_dimension=1, tiled=True
        ).astype(jnp.float32),
        lax.psum_scatter(
            jnp.broadcast_to(gain_first_part, (mp_count, width)).astype(jnp.bfloat16),
            "mp",
            scatter_dimension=0,
            tiled=True,
        ).astype(jnp.float32),
    )
    input_grads = grad_hidden_shard + norm_back(
        inputs.astype(jnp.float32), gain_first, grad_first_shard
    )
    (
        grad_query_out,
        grad_key_out,
        grad_value_out,
        grad_out_out,
        grad_up_out,
        grad_down_out,
        gain_attn_out,
        gain_ffn_out,
    ) = (
        lax.psum_scatter(grad_query_w, ("dp", "ctx"), scatter_dimension=0, tiled=True),
        lax.psum_scatter(grad_key_w, ("dp", "ctx"), scatter_dimension=0, tiled=True),
        lax.psum_scatter(grad_value_w, ("dp", "ctx"), scatter_dimension=0, tiled=True),
        lax.psum_scatter(grad_out_w, ("dp", "ctx"), scatter_dimension=1, tiled=True),
        lax.psum_scatter(grad_up_sum, ("dp", "ctx"), scatter_dimension=0, tiled=True),
        lax.psum_scatter(grad_down_sum, ("dp", "ctx"), scatter_dimension=2, tiled=True),
        lax.psum_scatter(gain_first_sum[0], ("dp", "ctx"), scatter_dimension=0, tiled=True),
        lax.psum_scatter(gain_second_grad, ("dp", "ctx"), scatter_dimension=0, tiled=True),
    )
    return (
        outputs,
        input_grads,
        grad_query_out,
        grad_key_out,
        grad_value_out,
        grad_out_out,
        grad_up_out,
        grad_down_out,
        gain_attn_out,
        gain_ffn_out,
    )


def solution(mesh):
    in_specs = (
        P("dp", ("ctx", "mp"), None),
        P(("dp", "ctx"), "mp"),
        P(("dp", "ctx"), "mp"),
        P(("dp", "ctx"), "mp"),
        P("mp", ("dp", "ctx")),
        P(("dp", "ctx"), None, "mp"),
        P(None, "mp", ("dp", "ctx")),
        P(("dp", "ctx")),
        P(("dp", "ctx")),
        P("dp", ("ctx", "mp"), None),
    )
    out_specs = (
        P("dp", ("ctx", "mp"), None),
        P("dp", ("ctx", "mp"), None),
        P(("dp", "ctx"), "mp"),
        P(("dp", "ctx"), "mp"),
        P(("dp", "ctx"), "mp"),
        P("mp", ("dp", "ctx")),
        P(("dp", "ctx"), None, "mp"),
        P(None, "mp", ("dp", "ctx")),
        P(("dp", "ctx")),
        P(("dp", "ctx")),
    )
    return jax.shard_map(local, mesh=mesh, in_specs=in_specs, out_specs=out_specs, check_vma=False)
```

profile of v0, /device:TPU:0, one launch (start us, length us, event | category | flops | bytes accessed | tf_op | source)
XLA Modules:
  0.0 1783.5 jit_solution(12301022891588044339)
XLA Ops:
  13.7 15.5 all-reduce.13
  38.4 24.4 %all-gather.14.cloned.1.call-done = bf16[1536,384]{1,0:T(8,128)(2,1)} async-done(((bf16[192,384]{1,0:T(8,128)(2,1)}), bf16[1536,384]{1,0:T(8,128)(2,1)}) %all-gather.14.cloned.1.call-update) | async-done | bytes 1179664 | tf_op jit(solution)/shard_map/all_gather | solution.py:58
  64.4 24.4 %all-gather.12.cloned.1.call-done = bf16[1536,384]{1,0:T(8,128)(2,1)} async-done(((bf16[192,384]{1,0:T(8,128)(2,1)}), bf16[1536,384]{1,0:T(8,128)(2,1)}) %all-gather.12.cloned.1.call-update) | async-done | bytes 1179664 | tf_op jit(solution)/shard_map/all_gather | solution.py:60
  91.2 88.5 %all-gather.10.cloned.1.call-done = bf16[3,512,1536]{2,1,0:T(8,128)(2,1)} async-done(((bf16[3,128,1536]{2,1,0:T(8,128)(2,1)}), bf16[3,512,1536]{2,1,0:T(8,128)(2,1)}) %all-gather.10.cloned.1.call-update) | async-done | bytes 4718608 | tf_op jit(solution)/shard_map/all_gather | solution.py:70
  207.8 42.8 %while.32 = (s32[]{:T(128)}, bf16[3,512,3,128]{1,3,2,0:T(8,128)(2,1)}, f32[3,3,512]{2,1,0:T(4,128)}, bf16[3,512,3,128]{3,1,2,0:T(8,128)(2,1)}, bf16[3,512,3,128]...) while((s32[]{:T(128)}, ...), condition=%wide.region_4.5_spmd.clone, body=%wide.region_1.4_spmd.clone.sunk | while | flops 828570112 | bytes 53273240 | solution.py:125
  254.4 8.0 fusion.133
  266.0 320.0 %all-reduce.16.cloned.1.call-done = f32[3,512,1536]{2,1,0:T(8,128)} async-done(((f32[3,512,1536]{2,1,0:T(8,128)}), f32[3,512,1536]{2,1,0:T(8,128)}) %all-reduce.16.cloned.1.call-update) | async-done | bytes 9437200 | tf_op jit(solution)/shard_map/psum | solution.py:129
  585.9 10.6 multiply_reduce_fusion.2
  597.2 6.7 multiply_convert_fusion.13
  603.9 72.0 %all-gather.24.cloned.1.call-done = bf16[3,512,1536]{2,1,0:T(8,128)(2,1)} async-done(((bf16[3,128,1536]{2,1,0:T(8,128)(2,1)}), bf16[3,512,1536]{2,1,0:T(8,128)(2,1)}) %all-gather.24.cloned.1.call-update) | async-done | bytes 4718608 | tf_op jit(solution)/shard_map/all_gather | solution.py:71
  675.9 46.5 %all-gather.22.cloned.1.call-done = bf16[8,192,1536]{1,0,2:T(8,128)(2,1)} async-done(((bf16[8,192,192]{1,0,2:T(8,128)(2,1)}), bf16[8,192,1536]{1,0,2:T(8,128)(2,1)}) %all-gather.22.cloned.1.call-update) | async-done | bytes 4718608 | tf_op jit(solution)/shard_map/all_gather | solution.py:63
  722.4 47.4 %all-gather.20.cloned.1.call-done = bf16[1536,8,192]{2,1,0:T(8,128)(2,1)} async-done(((bf16[192,8,192]{2,1,0:T(8,128)(2,1)}), bf16[1536,8,192]{2,1,0:T(8,128)(2,1)}) %all-gather.20.cloned.1.call-update) | async-done | bytes 4718608 | tf_op jit(solution)/shard_map/all_gather | solution.py:62
  769.9 72.1 %conditional.1 = (f32[1536,1536]{1,0:T(8,128)}, f32[1536,1536]{1,0:T(8,128)}, f32[1536,8,192]{0,2,1:T(8,128)}, f32[8,192,1536]{2,1,0:T(8,128)}) conditional(s32[]{:T(128)} %clamp.3, (bf16[1536,8,192]{2,1,0:T(8,128)(2,1)}, bf16[1536,1536]{1,0:T(8,128)(2,1)}, bf16[8,192,1536]{1,0,2:T(8,128)(2,1)}, ...), branch_computations={%region_7.8_spmd, %region_8.9_spmd, %region_9.10_spmd, %region_10.... | conditional | flops 43576197120 | bytes 273678624 | solution.py:171
  770.0 8.8 copy.70
  782.9 8.8 copy.71
  842.0 203.9 %reduce-scatter.14.cloned.1.call-done = f32[3,128,1536]{2,1,0:T(8,128)} async-done(((f32[3,512,1536]{2,1,0:T(8,128)}), f32[3,128,1536]{2,1,0:T(8,128)}) %reduce-scatter.14.cloned.1.call-update) | async-done | bytes 2359312 | tf_op jit(solution)/shard_map/reduce_scatter | solution.py:180
  1053.0 12.9 copy.90
  1066.0 13.1 reshape.343
  1079.1 64.2 %all-gather.26.cloned.1.call-done = bf16[3,512,1536]{2,1,0:T(8,128)(2,1)} async-done(((bf16[3,128,1536]{2,1,0:T(8,128)(2,1)}), bf16[3,512,1536]{2,1,0:T(8,128)(2,1)}) %all-gather.26.cloned.1.call-update) | async-done | bytes 4718608 | tf_op jit(solution)/shard_map/all_gather | solution.py:194
  1152.0 52.4 %while.33 = (s32[]{:T(128)}, f32[3,512,3,128]{1,3,2,0:T(8,128)}, f32[3,512,3,128]{1,3,2,0:T(8,128)}, bf16[3,512,3,128]{1,3,2,0:T(8,128)(2,1)}, f32[3,512,3,128]{...) while((s32[]{:T(128)}, f32[3,512,3,128]{1,3,2,0:T(8,128)}, ...), condition=%wide.region_18.19_spmd.clone, body=%wide.region_16.18_spmd.clone.sunk | while | flops 2043214336 | bytes 65065664 | solution.py:238
  1245.0 12.9 copy.85
  1258.4 7.0 fusion.131
  1288.1 7.4 multiply_reduce_fusion.1
  1295.5 19.1 %all-reduce.10 = f32[4,1536]{1,0:T(4,128)S(1)} all-reduce(f32[4,1536]{1,0:T(4,128)S(1)} %broadcast_in_dim.98), channel_id=13, replica_groups=mesh['dp'=4,'ctx'=2,'mp'=4] {'mp'}, use_global_device_ids=true, to_apply=%region_31.32.clone | all-reduce | flops 6144 | bytes 49152
  1326.6 17.6 all-reduce.8
  1346.2 23.9 %all-reduce.12 = (f32[1536]{0:T(1024)}, f32[1536]{0:T(1024)}) all-reduce(f32[1536]{0:T(1024)} %fusion.144, f32[1536]{0:T(1024)} %dynamic-slice_reduce_fusion), channel_id=12, replica_groups=mesh['dp'=4,'ctx'=2,'mp'=4] {'dp','ctx'}, use_global_device_ids=true, to_apply=%region_29.30.clone | all-reduce | flops 3072 | bytes 24576
  1375.8 117.7 %reduce-scatter.12.cloned.1.call-done = f32[3,128,1536]{2,1,0:T(8,128)} async-done(((f32[3,512,1536]{2,1,0:T(8,128)}), f32[3,128,1536]{2,1,0:T(8,128)}) %reduce-scatter.12.cloned.1.call-update) | async-done | bytes 2359312 | tf_op jit(solution)/shard_map/reduce_scatter | solution.py:177
  1498.7 92.1 %reduce-scatter.26.cloned.1.call-done = f32[192,8,192]{2,1,0:T(8,128)} async-done(((f32[1536,8,192]{2,1,0:T(8,128)}), f32[192,8,192]{2,1,0:T(8,128)}) %reduce-scatter.26.cloned.1.call-update) | async-done | bytes 1179664 | tf_op jit(solution)/shard_map/reduce_scatter | solution.py:305
  1590.7 46.3 %reduce-scatter.24.cloned.1.call-done = f32[384,192]{0,1:T(8,128)} async-done(((f32[384,1536]{0,1:T(8,128)}), f32[384,192]{0,1:T(8,128)}) %reduce-scatter.24.cloned.1.call-update) | async-done | bytes 294928 | tf_op jit(solution)/shard_map/reduce_scatter | solution.py:304
  1637.0 46.7 %reduce-scatter.22.cloned.1.call-done = f32[192,384]{1,0:T(8,128)} async-done(((f32[1536,384]{1,0:T(8,128)}), f32[192,384]{1,0:T(8,128)}) %reduce-scatter.22.cloned.1.call-update) | async-done | bytes 294928 | tf_op jit(solution)/shard_map/reduce_scatter | solution.py:303
  1683.7 46.3 %reduce-scatter.20.cloned.1.call-done = f32[192,384]{1,0:T(8,128)} async-done(((f32[1536,384]{1,0:T(8,128)}), f32[192,384]{1,0:T(8,128)}) %reduce-scatter.20.cloned.1.call-update) | async-done | bytes 294928 | tf_op jit(solution)/shard_map/reduce_scatter | solution.py:302
  1730.0 46.8 %reduce-scatter.18.cloned.1.call-done = f32[192,384]{1,0:T(8,128)} async-done(((f32[1536,384]{1,0:T(8,128)}), f32[192,384]{1,0:T(8,128)}) %reduce-scatter.18.cloned.1.call-update) | async-done | bytes 294928 | tf_op jit(solution)/shard_map/reduce_scatter | solution.py:301
  (285 shorter events, 286.2 us)
Async XLA Ops:
  7.2 29.7 %all-gather.16.cloned.1.call-start = ((), (), s32[]{:S(2)}) async-start(), calls=%async_computation.12 | async-start | bytes 1327104 | tf_op jit(solution)/shard_map/all_gather | solution.py:59
  7.9 54.9 %all-gather.14.cloned.1.call-start = ((), (), s32[]{:S(2)}) async-start(), calls=%async_computation.11 | async-start | bytes 1327104 | tf_op jit(solution)/shard_map/all_gather | solution.py:58
  8.7 80.2 %all-gather.12.cloned.1.call-start = ((), (), s32[]{:S(2)}) async-start(), calls=%async_computation.10 | async-start | bytes 1327104 | tf_op jit(solution)/shard_map/all_gather | solution.py:60
  9.4 170.3 %all-gather.10.cloned.1.call-start = ((), (), s32[]{:S(2)}) async-start(), calls=%async_computation.9 | async-start | bytes 5898240 | tf_op jit(solution)/shard_map/all_gather | solution.py:70
  10.0 244.5 %all-gather.18.cloned.1.call-start = ((), (), s32[]{:S(2)}) async-start(), calls=%async_computation.13 | async-start | bytes 1327104 | tf_op jit(solution)/shard_map/all_gather | solution.py:61
  29.3 153.9 %copy-start.25 = (f32[1536]{0:T(1024)}, f32[1536]{0:T(1024)S(1)}, u32[]{:S(2)}) copy-start(f32[1536]{0:T(1024)S(1)} %convert_element_type.148) | copy-start | bytes 18436
  30.5 158.2 %copy-start.14 = (f32[512,64]{0,1:T(8,128)}, f32[512,64]{0,1:T(8,128)S(1)}, u32[]{:S(2)}) copy-start(f32[512,64]{0,1:T(8,128)S(1)} %get-tuple-element.456) | copy-start | bytes 393220
  190.4 14.9 collective-permute-start.1
  197.0 10.7 collective-permute-start
  199.4 386.5 %all-reduce.16.cloned.1.call-start = ((), (), s32[]{:S(2)}) async-start(), calls=%async_computation.14 | async-start | bytes 18874368 | tf_op jit(solution)/shard_map/psum | solution.py:129
  262.5 413.5 %all-gather.24.cloned.1.call-start = ((), (), s32[]{:S(2)}) async-start(), calls=%async_computation.17 | async-start | bytes 5898240 | tf_op jit(solution)/shard_map/all_gather | solution.py:71
  263.2 459.2 %all-gather.22.cloned.1.call-start = ((), (), s32[]{:S(2)}) async-start(), calls=%async_computation.16 | async-start | bytes 7077888 | tf_op jit(solution)/shard_map/all_gather | solution.py:63
  265.1 504.7 %all-gather.20.cloned.1.call-start = ((), (), s32[]{:S(2)}) async-start(), calls=%async_computation.15 | async-start | bytes 7077888 | tf_op jit(solution)/shard_map/all_gather | solution.py:62
  265.9 780.0 %reduce-scatter.14.cloned.1.call-start = ((), (), s32[]{:S(2)}) async-start(), calls=%async_computation.19 | async-start | bytes 11796480 | tf_op jit(solution)/shard_map/reduce_scatter | solution.py:180
  266.0 330.6 %copy-start.22 = (f32[1536]{0:T(1024)}, f32[1536]{0:T(1024)S(1)}, u32[]{:S(2)}) copy-start(f32[1536]{0:T(1024)S(1)} %convert_element_type.152) | copy-start | bytes 18436
  841.9 204.0 %copy-start.23 = (f32[1536]{0:T(1024)S(1)}, f32[1536]{0:T(1024)}, u32[]{:S(2)}) copy-start(f32[1536]{0:T(1024)} %copy-done.22) | copy-start | bytes 18436
  842.0 301.4 %all-gather.26.cloned.1.call-start = ((), (), s32[]{:S(2)}) async-start(), calls=%async_computation.20 | async-start | bytes 5898240 | tf_op jit(solution)/shard_map/all_gather | solution.py:194
  842.0 207.6 %copy-start.8 = (bf16[3,128,1536]{2,1,0:T(8,128)(2,1)S(1)}, bf16[3,128,1536]{2,1,0:T(8,128)(2,1)}, u32[]{:S(2)}) copy-start(bf16[3,128,1536]{2,1,0:T(8,128)(2,1)} %param.27) | copy-start | bytes 3538948
  1052.9 262.9 %reduce-scatter.28.cloned.1.call-start = ((), (), s32[]{:S(2)}) async-start(), calls=%async_computation.27 | async-start | bytes 10616832
  1079.1 64.3 %copy-start.16 = (bf16[384,1536]{0,1:T(8,128)(2,1)S(1)}, bf16[384,1536]{0,1:T(8,128)(2,1)}, u32[]{:S(2)}) copy-start(bf16[384,1536]{0,1:T(8,128)(2,1)} %all-gather.18.cloned.1.call-done) | copy-start | bytes 3538948
  1079.1 293.7 %reduce-scatter.16.cloned.1.call-start = ((), (), s32[]{:S(2)}) async-start(), calls=%async_computation.21 | async-start | bytes 5898240 | tf_op jit(solution)/shard_map/reduce_scatter | solution.py:278
  1204.4 4.7 collective-permute-start.3
  1205.7 6.6 collective-permute-start.2
  1244.4 249.2 %reduce-scatter.12.cloned.1.call-start = ((), (), s32[]{:S(2)}) async-start(), calls=%async_computation.18 | async-start | bytes 11796480 | tf_op jit(solution)/shard_map/reduce_scatter | solution.py:177
  1245.0 345.8 %reduce-scatter.26.cloned.1.call-start = ((), (), s32[]{:S(2)}) async-start(), calls=%async_computation.26 | async-start | bytes 14155776 | tf_op jit(solution)/shard_map/reduce_scatter | solution.py:305
  1257.9 379.1 %reduce-scatter.24.cloned.1.call-start = ((), (), s32[]{:S(2)}) async-start(), calls=%async_computation.25 | async-start | bytes 2654208 | tf_op jit(solution)/shard_map/reduce_scatter | solution.py:304
  1265.4 418.3 %reduce-scatter.22.cloned.1.call-start = ((), (), s32[]{:S(2)}) async-start(), calls=%async_computation.24 | async-start | bytes 2654208 | tf_op jit(solution)/shard_map/reduce_scatter | solution.py:303
  1271.9 458.1 %reduce-scatter.20.cloned.1.call-start = ((), (), s32[]{:S(2)}) async-start(), calls=%async_computation.23 | async-start | bytes 2654208 | tf_op jit(solution)/shard_map/reduce_scatter | solution.py:302
  1278.4 498.4 %reduce-scatter.18.cloned.1.call-start = ((), (), s32[]{:S(2)}) async-start(), calls=%async_computation.22 | async-start | bytes 2654208 | tf_op jit(solution)/shard_map/reduce_scatter | solution.py:301
  1319.5 53.2 %copy-start.26 = (f32[1536]{0:T(1024)S(1)}, f32[1536]{0:T(1024)}, u32[]{:S(2)}) copy-start(f32[1536]{0:T(1024)} %copy-done.25) | copy-start | bytes 18436
  1326.0 167.5 %copy-start.6 = (f32[3,128,1536]{2,1,0:T(8,128)S(1)}, f32[3,128,1536]{2,1,0:T(8,128)}, u32[]{:S(2)}) copy-start(f32[3,128,1536]{2,1,0:T(8,128)} %reduce-scatter.14.cloned.1.call-done) | copy-start | bytes 7077892
  1326.0 167.5 %copy-start.24 = (f32[1536]{0:T(1024)S(1)}, f32[1536]{0:T(1024)}, u32[]{:S(2)}) copy-start(f32[1536]{0:T(1024)} %copy-done.22) | copy-start | bytes 18436
  (33 other events, 202.9 us)
Sparse Core Ops, SparseCore 0:
  9.9 26.9 all-gather.15
  38.8 24.0 all-gather.13
  64.7 24.0 all-gather.11
  90.3 89.3 all-gather.9
  199.5 22.5 all-gather.17
  262.6 323.2 all-reduce.15
  587.5 88.3 all-gather.23
  678.4 43.9 all-gather.21
  724.3 45.5 all-gather.19
  842.1 203.8 reduce-scatter.13
  1053.1 90.2 all-gather.25
  1146.7 74.9 reduce-scatter.27
  1244.5 84.9 reduce-scatter.15
  1331.7 161.8 reduce-scatter.11
  1497.4 93.2 reduce-scatter.25
  1594.5 42.5 reduce-scatter.23
  1641.2 42.4 reduce-scatter.21
  1687.5 42.4 reduce-scatter.19
  1734.3 42.4 reduce-scatter.17
where the time goes:
time: 1790 us; the launch traced here: 1780 us
  waiting for transfers between devices  1300 us (73%)
  local copies, waits for them, and re-layouts  144 us (8%)
  matrix products  128 us (7%)
  other arithmetic  87.2 us (5%)
  blocking collectives  76.1 us (4%)
  loops' own time  21.7 us (1%)
    psum x1, waiting for transfers between devices, local(): lax.psum(jnp.dot(mixed_flat, out_full, preferred_element_type=jnp.float32...  320 us
    reduce_scatter x1, waiting for transfers between devices, local(): lax.psum_scatter(grad_second_part, 'mp', scatter_dimension=1, tiled=True)  204 us
    reduce_scatter x1, waiting for transfers between devices, local(): lax.psum_scatter(ffn_part.reshape(count, length_half, width), 'mp', scatt...  118 us
    reduce_scatter x1, waiting for transfers between devices, local(): lax.psum_scatter(grad_up_sum, ('dp', 'ctx'), scatter_dimension=0, tiled=T...  92.1 us
    all_gather x1, waiting for transfers between devices, local(): lax.all_gather(inputs, 'mp', axis=1, tiled=True)  88.5 us
    unnamed x4, blocking collectives  76.1 us
    all_gather x1, waiting for transfers between devices, local(): lax.all_gather(cotangent, 'mp', axis=1, tiled=True)  72 us
    all_gather x1, waiting for transfers between devices, local(): lax.all_gather(grad_hidden_shard.astype(jnp.bfloat16), 'mp', axis=1, tile...  64.2 us
  transfers between devices with their start and end apart: 23, of which 17 were waited for; matrix products, arithmetic and copies ran while one was open for 15% of the time, Pallas kernels for 0%

commit v1 on v0

v1 whole, which is shorter than its diff:
```python
import jax
import jax.numpy as jnp
from jax import lax
from jax.sharding import PartitionSpec as P

HEAD = 128
LEVELS = 4
EPSILON = 1e-06
NEGATIVE = -1e30
BF = jnp.bfloat16
F32 = jnp.float32


def flip(shard, axis, bit):
    devices = lax.axis_size(axis)
    return lax.ppermute(shard, axis, [(i, i ^ bit) for i in range(devices)])


def turn(shard, axis, by):
    devices = lax.axis_size(axis)
    return lax.ppermute(shard, axis, [(i, (i + by) % devices) for i in range(devices)])


def put(buffer, part, index, dim):
    starts = [0] * buffer.ndim
    starts[dim] = index
    return lax.dynamic_update_slice(buffer, part, tuple(starts))


def take(buffer, index, dim):
    return lax.dynamic_index_in_dim(buffer, index, dim, keepdims=False)


def level_gather(part, mine):
    half = part.shape[0] // 2
    from_x = flip(part, "dp", 1)
    from_y = flip(part, "dp", 2)
    low_half = flip(from_x[:half], "dp", 2)
    high_half = flip(from_y[half:], "dp", 1)
    whole = jnp.zeros((LEVELS,) + part.shape, part.dtype)
    whole = put(whole, part[None], mine, 0)
    whole = put(whole, from_x[None], mine ^ 1, 0)
    whole = put(whole, from_y[None], mine ^ 2, 0)
    rest = jnp.concatenate([low_half, high_half], 0)
    return put(whole, rest[None], mine ^ 3, 0)


def level_scatter(parts, mine):
    half = parts.shape[1] // 2
    own, by_x, by_y, by_xy = (take(parts, mine ^ k, 0) for k in range(LEVELS))
    got_x = flip(jnp.stack([by_x[:half], by_xy[:half]]), "dp", 1)
    got_y = flip(jnp.stack([by_y[half:], by_xy[half:]]), "dp", 2)
    send_y = (by_y[:half].astype(F32) + got_x[1].astype(F32)).astype(parts.dtype)
    send_x = (by_x[half:].astype(F32) + got_y[1].astype(F32)).astype(parts.dtype)
    last_y = flip(send_y, "dp", 2)
    last_x = flip(send_x, "dp", 1)
    first = own[:half].astype(F32) + got_x[0].astype(F32) + last_y.astype(F32)
    second = own[half:].astype(F32) + got_y[0].astype(F32) + last_x.astype(F32)
    return jnp.concatenate([first, second], 0)


def level_swap(parts, mine):
    whole = jnp.zeros(parts.shape, parts.dtype)
    whole = put(whole, take(parts, mine, 0)[None], mine, 0)
    for k in range(1, LEVELS):
        whole = put(whole, flip(take(parts, mine ^ k, 0), "dp", k)[None], mine ^ k, 0)
    return whole


def rank_swap(parts, mine, axis):
    devices = lax.axis_size(axis)
    found = [(mine, take(parts, mine, 0))]
    for k in range(1, devices):
        sent = turn(take(parts, (mine + k) % devices, 0), axis, k)
        found.append(((mine + devices - k) % devices, sent))
    return found


def teams(devices):
    return [list(range(level, devices, LEVELS)) for level in range(LEVELS)]


def team_gather(part):
    devices = lax.axis_size("dp")
    if devices == LEVELS:
        return part[None]
    return lax.all_gather(part, "dp", axis=0, axis_index_groups=teams(devices))


def team_scatter(parts):
    devices = lax.axis_size("dp")
    if devices == LEVELS:
        return parts[0]
    return lax.psum_scatter(
        parts, "dp", scatter_dimension=0, axis_index_groups=teams(devices), tiled=False
    )


def pair_gather(part, mine, dim):
    other = flip(part, "ctx", 1)
    shape = part.shape[:dim] + (2,) + part.shape[dim:]
    whole = jnp.zeros(shape, part.dtype)
    whole = put(whole, jnp.expand_dims(part, dim), mine, dim)
    return put(whole, jnp.expand_dims(other, dim), 1 - mine, dim)


def pair_scatter(parts, mine, dim):
    other = flip(take(parts, 1 - mine, dim), "ctx", 1)
    return take(parts, mine, dim).astype(F32) + other.astype(F32)


def model_gather(part, level, ctx):
    rows, width = part.shape
    whole = team_gather(level_gather(part, level))
    whole = pair_gather(whole.reshape(-1, rows, width), ctx, 1)
    return whole.reshape(-1, width)


def model_scatter(grad, level, ctx, rows):
    width = grad.shape[1]
    parts = grad.reshape(-1, 2, rows, width)
    parts = pair_scatter(parts, ctx, 1).astype(grad.dtype)
    parts = parts.reshape(-1, LEVELS, rows, width)
    parts = team_scatter(parts)
    return level_scatter(parts, level)


def inverse_rms(values):
    return lax.rsqrt(jnp.mean(values * values, axis=-1, keepdims=True) + EPSILON)


def norm_back(values, inv_rms, weighted):
    return inv_rms * weighted - values * (inv_rms * inv_rms * inv_rms) * jnp.mean(
        weighted * values, axis=-1, keepdims=True
    )


def rotation(positions, head_size):
    half_size = head_size // 2
    frequency = 10000.0 ** (-jnp.arange(half_size, dtype=jnp.float32) / half_size)
    angles = positions.astype(jnp.float32)[:, None] * frequency[None, :]
    return (jnp.cos(angles)[:, None, :], jnp.sin(angles)[:, None, :])


def rotate(values, cosine, sine_part):
    half_size = values.shape[-1] // 2
    leading = values[..., :half_size]
    trailing = values[..., half_size:]
    return jnp.concatenate(
        [leading * cosine - trailing * sine_part, trailing * cosine + leading * sine_part], axis=-1
    )


def gelu_tanh(values):
    return jax.nn.gelu(values, approximate=True)


def product(equation, left, right):
    return jnp.einsum(equation, left, right, preferred_element_type=F32)


def local(inputs, w_query, w_key, w_value, w_out, w_up, w_down, gain_attn, gain_ffn, cotangent):
    count, shard_len, width = inputs.shape
    own_rows = count * shard_len
    ranks = lax.axis_size("mp")
    length_half = shard_len * ranks
    total_rows = count * length_half
    level = lax.axis_index("dp") % LEVELS
    ctx = lax.axis_index("ctx")
    rank = lax.axis_index("mp")
    part_rows, head_cols = w_query.shape
    head_count = head_cols // HEAD
    factor = HEAD ** (-0.5)
    gain_a = gain_attn.astype(F32)[:, None]
    gain_f = gain_ffn.astype(F32)[:, None]

    inputs_f = inputs.astype(F32)
    inv_first = inverse_rms(inputs_f)
    unit_first = (inputs_f * inv_first).astype(BF)
    rows_first = lax.all_gather(unit_first, "mp", axis=1, tiled=True).reshape(total_rows, width)

    scaled = jnp.concatenate(
        [(gain_a * w.astype(F32)).astype(BF) for w in (w_query, w_key, w_value)], axis=1
    )
    qkv_full = model_gather(scaled, level, ctx)
    out_cols = jnp.zeros((part_rows, ranks * head_cols), BF)
    out_turned = w_out.T
    out_cols = put(out_cols, out_turned, rank * head_cols, 1)
    for k in range(1, ranks):
        out_cols = put(
            out_cols, turn(out_turned, "mp", k), (rank + ranks - k) % ranks * head_cols, 1
        )
    out_full = model_gather(out_cols, level, ctx)

    cot_rows = level_gather(cotangent.reshape(own_rows, width), level)

    blocks = w_up.shape[1]
    unit_cols = w_up.shape[2]
    sub = unit_cols // LEVELS
    half_blocks = blocks // 2
    up_turned = (gain_f[:, :, None] * w_up.astype(F32)).astype(BF).transpose(1, 2, 0)
    both = jnp.stack([up_turned, w_down])
    both = both.reshape(2, 2, half_blocks, unit_cols, part_rows)
    sent_ctx = flip(take(both, 1 - ctx, 1), "ctx", 1)
    kept = take(both, ctx, 1)
    pair = jnp.zeros((2, half_blocks, unit_cols, 2, part_rows), BF)
    pair = put(pair, kept[:, :, :, None], ctx, 3)
    pair = put(pair, sent_ctx[:, :, :, None], 1 - ctx, 3)
    pair = pair.reshape(2, half_blocks, LEVELS, sub, 2 * part_rows).transpose(2, 0, 1, 3, 4)
    swapped = team_gather(level_swap(pair, level))
    swapped = swapped.transpose(2, 3, 4, 0, 1, 5).reshape(2, half_blocks, sub, width)
    ranked = lax.all_gather(swapped, "mp", axis=2)
    ranked = ranked.reshape(2, half_blocks, ranks * sub, width)
    whole = pair_gather(ranked, ctx, 1).reshape(2, blocks * unit_cols, width)
    up_mine, down_mine = whole[0], whole[1]

    positions = ctx * length_half + jnp.arange(length_half, dtype=jnp.int32)
    cosine, sine_part = rotation(positions, HEAD)
    projected = product("rd,dc->rc", rows_first, qkv_full).reshape(
        count, length_half, 3, head_count, HEAD
    )
    query_rows = rotate(projected[:, :, 0], cosine, sine_part).astype(BF)
    key_rows = rotate(projected[:, :, 1], cosine, sine_part).astype(BF)
    value_rows = projected[:, :, 2].astype(BF)
    early = [(0, 1)]
    early_keys, early_values = lax.ppermute((key_rows, value_rows), "ctx", early)
    row_ids = jnp.arange(length_half)[:, None]
    col_ids = jnp.arange(2 * length_half)[None, :]
    visible = jnp.where(col_ids < length_half, ctx >= 1, col_ids - length_half <= row_ids)

    def scores_of(query_one, keys_all):
        raw_scores = product("qhd,khd->hqk", query_one, keys_all) * factor
        return jnp.where(visible[None], raw_scores, NEGATIVE)

    def attend(package):
        query_one, key_one, value_one, key_early, value_early = package
        keys_all = jnp.concatenate([key_early, key_one], 0)
        values_all = jnp.concatenate([value_early, value_one], 0)
        scores = scores_of(query_one, keys_all)
        largest = jnp.max(scores, axis=-1, keepdims=True)
        exponent = jnp.exp(scores - largest)
        totals = jnp.sum(exponent, axis=-1, keepdims=True)
        softened = exponent / totals
        mixed_one = product("hqk,khd->qhd", softened.astype(BF), values_all)
        return (mixed_one.astype(BF), (largest + jnp.log(totals))[..., 0])

    mixed_rows, log_totals = lax.map(
        attend, (query_rows, key_rows, value_rows, early_keys, early_values)
    )
    mixed_parts = mixed_rows.reshape(count, ranks, shard_len, head_cols).transpose(1, 0, 2, 3)
    mixed_own = jnp.zeros((own_rows, ranks * head_cols), BF)
    for source, found in rank_swap(mixed_parts, rank, "mp"):
        mixed_own = put(mixed_own, found.reshape(own_rows, head_cols), source * head_cols, 1)
    attended = product("rc,dc->rd", mixed_own, out_full)
    hidden = inputs_f.reshape(own_rows, width) + attended
    inv_second = inverse_rms(hidden)
    unit_second = (hidden * inv_second).astype(BF)

    rows_second = level_gather(unit_second, level)
    results, grads_in, activated_all, grad_up_all = [], [], [], []
    for one in range(LEVELS):
        used = 2**one * unit_cols
        upped = product("rd,hd->rh", rows_second[one], up_mine[:used])
        activated, gelu_pull = jax.vjp(gelu_tanh, upped)
        activated = activated.astype(BF)
        grad_act = product("rd,hd->rh", cot_rows[one], down_mine[:used])
        grad_upped = gelu_pull(grad_act)[0].astype(BF)
        grads_in.append(product("rh,hd->rd", grad_upped, up_mine[:used]).astype(BF))
        results.append(product("rh,hd->rd", activated, down_mine[:used]).astype(BF))
        activated_all.append(activated)
        grad_up_all.append(grad_upped)

    grad_second = level_scatter(jnp.stack(grads_in), level)
    result = level_scatter(jnp.stack(results), level)
    outputs = (hidden + result).astype(BF).reshape(inputs.shape)
    grad_hidden = cotangent.astype(F32).reshape(own_rows, width) + norm_back(
        hidden, inv_second, grad_second
    )

    def block_grads(left_all, right):
        pieces = []
        for one in range(LEVELS):
            first = 0 if one == 0 else 2 ** (one - 1) * unit_cols
            last = 2**one * unit_cols
            left = jnp.concatenate([left_all[k][:, first:last] for k in range(one, LEVELS)], 0)
            pieces.append(product("rh,rd->hd", left, right[one:].reshape(-1, width)).astype(BF))
        return jnp.concatenate(pieces, 0)

    grad_ffn = jnp.stack(
        [block_grads(grad_up_all, rows_second), block_grads(activated_all, cot_rows)]
    )
    grad_ffn = pair_scatter(grad_ffn.reshape(2, 2, half_blocks * unit_cols, width), ctx, 1)
    grad_ffn = grad_ffn.astype(BF).reshape(2, half_blocks, ranks, sub, width)
    grad_ffn = lax.psum_scatter(grad_ffn, "mp", scatter_dimension=2, tiled=True)
    grad_ffn = grad_ffn.reshape(2, half_blocks, sub, -1, LEVELS, 2 * part_rows)
    grad_ffn = team_scatter(grad_ffn.transpose(3, 4, 0, 1, 2, 5))
    grad_ffn = level_swap(grad_ffn, level).transpose(1, 2, 0, 3, 4)
    grad_ffn = grad_ffn.reshape(2, half_blocks, unit_cols, 2, part_rows)
    sent_ctx = flip(take(grad_ffn, 1 - ctx, 3), "ctx", 1)
    own_ffn = jnp.zeros((2, 2, half_blocks, unit_cols, part_rows), BF)
    own_ffn = put(own_ffn, take(grad_ffn, ctx, 3)[:, None], ctx, 1)
    own_ffn = put(own_ffn, sent_ctx[:, None], 1 - ctx, 1)
    own_ffn = own_ffn.reshape(2, blocks, unit_cols, part_rows).astype(F32)
    grad_up_unit = own_ffn[0].transpose(2, 0, 1)
    grad_up_out = gain_f[:, :, None] * grad_up_unit
    grad_down_out = own_ffn[1]
    gain_ffn_part = jnp.sum(grad_up_unit * w_up.astype(F32), axis=(1, 2))

    grad_low = grad_hidden.astype(BF)
    grad_mixed_own = product("rd,dc->rc", grad_low, out_full).astype(BF)
    grad_parts = grad_mixed_own.reshape(count, shard_len, ranks, head_cols).transpose(2, 0, 1, 3)
    grad_mixed = jnp.zeros((count, ranks, shard_len, head_cols), BF)
    for source, found in rank_swap(grad_parts, rank, "mp"):
        grad_mixed = put(grad_mixed, found[:, None], source, 1)
    grad_mixed = grad_mixed.reshape(count, length_half, head_count, HEAD)
    grad_out_w = product("rd,rc->dc", grad_low, mixed_own).astype(BF)
    grad_out_w = model_scatter(grad_out_w, level, ctx, part_rows).astype(BF)
    grad_out_parts = grad_out_w.reshape(part_rows, ranks, head_cols).transpose(1, 0, 2)
    grad_out_out = 0.0
    for _, found in rank_swap(grad_out_parts, rank, "mp"):
        grad_out_out = grad_out_out + found.astype(F32)
    grad_out_out = grad_out_out.T

    def attend_back(package):
        query_one, key_one, value_one, key_early, value_early, log_one, grad_one = package
        keys_all = jnp.concatenate([key_early, key_one], 0)
        values_all = jnp.concatenate([value_early, value_one], 0)
        scores = scores_of(query_one, keys_all)
        softened = jnp.exp(scores - log_one[..., None])
        grad_soft = product("qhd,khd->hqk", grad_one, values_all)
        grad_values = product("hqk,qhd->khd", softened.astype(BF), grad_one)
        inner = jnp.sum(grad_soft * softened, axis=-1, keepdims=True)
        grad_scores = (softened * (grad_soft - inner)).astype(BF)
        grad_queries = product("hqk,khd->qhd", grad_scores, keys_all) * factor
        grad_keys = product("hqk,qhd->khd", grad_scores, query_one) * factor
        return (
            grad_queries,
            grad_keys[length_half:],
            grad_keys[:length_half].astype(BF),
            grad_values[length_half:],
            grad_values[:length_half].astype(BF),
        )

    grad_queries, grad_key_own, grad_key_early, grad_value_own, grad_value_early = lax.map(
        attend_back,
        (query_rows, key_rows, value_rows, early_keys, early_values, log_totals, grad_mixed),
    )
    key_back, value_back = lax.ppermute((grad_key_early, grad_value_early), "ctx", [(1, 0)])
    grad_query_low = rotate(grad_queries, cosine, -sine_part).astype(BF)
    grad_key_low = rotate(grad_key_own + key_back.astype(F32), cosine, -sine_part).astype(BF)
    grad_value_low = (grad_value_own + value_back.astype(F32)).astype(BF)
    grad_qkv = jnp.concatenate(
        [g.reshape(total_rows, head_cols) for g in (grad_query_low, grad_key_low, grad_value_low)],
        axis=1,
    )
    grad_first = product("rc,dc->rd", grad_qkv, qkv_full).astype(BF)
    grad_first = lax.psum_scatter(
        grad_first.reshape(count, length_half, width), "mp", scatter_dimension=1, tiled=True
    )
    input_grads = grad_hidden.reshape(inputs.shape) + norm_back(
        inputs_f, inv_first, grad_first.astype(F32)
    )
    grad_qkv_w = product("rd,rc->dc", rows_first, grad_qkv).astype(BF)
    grad_qkv_w = model_scatter(grad_qkv_w, level, ctx, part_rows)
    originals = jnp.concatenate([w.astype(F32) for w in (w_query, w_key, w_value)], axis=1)
    gain_attn_part = jnp.sum(grad_qkv_w * originals, axis=1)
    grad_qkv_out = gain_a * grad_qkv_w
    gains = lax.psum(jnp.stack([gain_attn_part, gain_ffn_part]), "mp")
    return (
        outputs,
        input_grads,
        grad_qkv_out[:, :head_cols],
        grad_qkv_out[:, head_cols : 2 * head_cols],
        grad_qkv_out[:, 2 * head_cols :],
        grad_out_out,
        grad_up_out,
        grad_down_out,
        gains[0],
        gains[1],
    )


def solution(mesh):
    in_specs = (
        P("dp", ("ctx", "mp"), None),
        P(("dp", "ctx"), "mp"),
        P(("dp", "ctx"), "mp"),
        P(("dp", "ctx"), "mp"),
        P("mp", ("dp", "ctx")),
        P(("dp", "ctx"), None, "mp"),
        P(None, "mp", ("dp", "ctx")),
        P(("dp", "ctx")),
        P(("dp", "ctx")),
        P("dp", ("ctx", "mp"), None),
    )
    out_specs = (
        P("dp", ("ctx", "mp"), None),
        P("dp", ("ctx", "mp"), None),
        P(("dp", "ctx"), "mp"),
        P(("dp", "ctx"), "mp"),
        P(("dp", "ctx"), "mp"),
        P("mp", ("dp", "ctx")),
        P(("dp", "ctx"), None, "mp"),
        P(None, "mp", ("dp", "ctx")),
        P(("dp", "ctx")),
        P(("dp", "ctx")),
    )
    return jax.shard_map(local, mesh=mesh, in_specs=in_specs, out_specs=out_specs, check_vma=False)
```

time: 1790 us -> 999 us (0.56)
  waiting for transfers between devices: 1300 us -> 288 us
  local copies, waits for them, and re-layouts: 144 us -> 363 us
  blocking collectives: 76.1 us -> 10.6 us
  starting transfers between devices: 9.75 us -> 71.2 us
  loops' own time: 21.7 us -> 0.49 us
  matrix products: 128 us -> 146 us
    reduce_scatter x8 -> x1, waiting for transfers between devices: 600 us -> 33.3 us  [local(): lax.psum_scatter(grad_first.reshape(count, length_half, width), 'mp', sca...]
    all_gather x9 -> x2, waiting for transfers between devices: 374 us -> 39.4 us  [the longest x1 39.4 us: local(): ranked = lax.all_gather(swapped, 'mp', axis=2)]
    psum x1 -> x0, waiting for transfers between devices: 320 us -> none  [local(): lax.psum(jnp.dot(mixed_flat, out_full, preferred_element_type=jnp.float32...]
    dynamic_update_slice x0 -> x43, local copies, waits for them, and re-layouts: none -> 199 us  [the longest x40 196 us: put(): return lax.dynamic_update_slice(buffer, part, tuple(starts))]
    ppermute x4 -> x62, waiting for transfers between devices: 1.94 us -> 139 us  [the longest x46 118 us: flip(): return lax.ppermute(shard, axis, [(i, i ^ bit) for i in range(devices)])]
    unnamed x4 -> x0, blocking collectives: 76.1 us -> none
    unnamed x20 -> x5, waiting for transfers between devices: 4.68 us -> 77 us
    ppermute x4 -> x62, starting transfers between devices: 8.11 us -> 70.8 us  [the longest x46 47.4 us: flip(): return lax.ppermute(shard, axis, [(i, i ^ bit) for i in range(devices)])]
  transfers between devices with their start and end apart: 23 -> 66, of which waited for: 17 -> 22; matrix products, arithmetic and copies ran while one was open for 15% -> 53% of each run, Pallas kernels for 0% -> 0%
where the time goes in v1:
time: 999 us; the launch traced here: 985 us
  local copies, waits for them, and re-layouts  363 us (36%)
  waiting for transfers between devices  288 us (29%)
  matrix products  146 us (15%)
  other arithmetic  89.1 us (9%)
  starting transfers between devices  71.2 us (7%)
  between operations  15.9 us (2%)
  blocking collectives  10.6 us (1%)
    dynamic_update_slice x40, local copies, waits for them, and re-layouts, put(): return lax.dynamic_update_slice(buffer, part, tuple(starts))  196 us
    dot_general x51, matrix products, product(): return jnp.einsum(equation, left, right, preferred_element_type=F32)  146 us
    ppermute x46, waiting for transfers between devices, flip(): return lax.ppermute(shard, axis, [(i, i ^ bit) for i in range(devices)])  118 us
    unnamed x5, waiting for transfers between devices  77 us
    ppermute x46, starting transfers between devices, flip(): return lax.ppermute(shard, axis, [(i, i ^ bit) for i in range(devices)])  47.4 us
    all_gather x1, waiting for transfers between devices, local(): ranked = lax.all_gather(swapped, 'mp', axis=2)  39.4 us
    reduce_scatter x1, waiting for transfers between devices, local(): lax.psum_scatter(grad_first.reshape(count, length_half, width), 'mp', sca...  33.3 us
    unnamed x163, local copies, waits for them, and re-layouts  27.7 us
  transfers between devices with their start and end apart: 66, of which 22 were waited for; matrix products, arithmetic and copies ran while one was open for 53% of the time, Pallas kernels for 0%

profile of v1, /device:TPU:0, one launch (start us, length us, event | category | flops | bytes accessed | tf_op | source)
XLA Modules:
  0.0 985.3 jit_solution(13637275437465337942)
XLA Ops:
  37.5 22.8 %dynamic_update_slice.190 = bf16[2,4,192,2,192]{4,3,2,1,0:T(2,128)(2,1)S(1)} dynamic-update-slice(bf16[2,4,192,2,192]{4,3,2,1,0:T(2,128)(2,1)S(1)} %broadcast_in_dim.235, bf16[2,4,192,1,192]{4,3,2,1,0:T(2,128)(2,1)S(1)} %copy.254, s32[]{:T(128)} %copy.457, s32[]{:T(128)} %copy.457, s32[]{:T(128)} %copy.457, s32[]{:T(128)S(6)} %select_n.196, s32[]{:T(128)} %copy.457) | dynamic-update-slice | bytes 1179652 | tf_op jit(solution)/shard_map/dynamic_update_slice | solution.py:27
  70.8 24.4 %collective-permute-done.3 = bf16[96,1152]{1,0:T(8,128)(2,1)S(1)} collective-permute-done((bf16[96,1152]{1,0:T(8,128)(2,1)S(1)}, bf16[96,1152]{1,0:T(8,128)(2,1)S(1)}, u32[]{:S(2)}, u32[]{:S(2)}) %collective-permute-start.3) | collective-permute-done | bytes 221216 | tf_op jit(solution)/shard_map/ppermute | solution.py:16
  103.5 22.6 %dynamic_update_slice.191 = bf16[2,4,192,2,192]{4,3,2,1,0:T(2,128)(2,1)S(1)} dynamic-update-slice(bf16[2,4,192,2,192]{4,3,2,1,0:T(2,128)(2,1)S(1)} %dynamic_update_slice.190, bf16[2,4,192,1,192]{4,3,2,1,0:T(2,128)(2,1)S(1)} %copy.255, s32[]{:T(128)} %copy.457, s32[]{:T(128)} %copy.457, s32[]{:T(128)} %copy.457, s32[]{:T(128)S(6)} %select_n.197, s32[]{:T(128)} %copy.457) | dynamic-update-slice | bytes 1179652 | tf_op jit(solution)/shard_map/dynamic_update_slice | solution.py:27
  131.2 15.5 %dynamic_update_slice.192 = bf16[1,4,2,4,48,384]{5,1,4,3,2,0:T(4,128)(2,1)} dynamic-update-slice(bf16[1,4,2,4,48,384]{5,1,4,3,2,0:T(4,128)(2,1)} %broadcast_in_dim.234, bf16[1,1,2,4,48,384]{5,1,4,3,2,0:T(2,128)(2,1)S(1)} %copy.256, s32[]{:T(128)} %copy.457, s32[]{:T(128)S(6)} %select_n.192, s32[]{:T(128)} %copy.457, s32[]{:T(128)} %copy.457, s32[]{:T(128)} %copy.457, s32[]{:T(128)} %copy.457) | dynamic-update-slice | bytes 589828 | tf_op jit(solution)/shard_map/dynamic_update_slice | solution.py:27
  163.5 9.2 fusion.72
  192.0 15.6 %dynamic_update_slice.193 = bf16[1,4,2,4,48,384]{5,1,4,3,2,0:T(4,128)(2,1)} dynamic-update-slice(bf16[1,4,2,4,48,384]{5,1,4,3,2,0:T(4,128)(2,1)} %dynamic_update_slice.192, bf16[1,1,2,4,48,384]{5,1,4,3,2,0:T(2,128)(2,1)} %copy.257, s32[]{:T(128)} %copy.457, s32[]{:T(128)S(6)} %select_n.193, s32[]{:T(128)} %copy.457, s32[]{:T(128)} %copy.457, s32[]{:T(128)} %copy.457, s32[]{:T(128)} %copy.457) | dynamic-update-slice | bytes 589828 | tf_op jit(solution)/shard_map/dynamic_update_slice | solution.py:27
  207.6 15.6 %dynamic_update_slice.194 = bf16[1,4,2,4,48,384]{5,1,4,3,2,0:T(4,128)(2,1)} dynamic-update-slice(bf16[1,4,2,4,48,384]{5,1,4,3,2,0:T(4,128)(2,1)} %dynamic_update_slice.193, bf16[1,1,2,4,48,384]{5,1,4,3,2,0:T(2,128)(2,1)} %copy.258, s32[]{:T(128)} %copy.457, s32[]{:T(128)S(6)} %select_n.194, s32[]{:T(128)} %copy.457, s32[]{:T(128)} %copy.457, s32[]{:T(128)} %copy.457, s32[]{:T(128)} %copy.457) | dynamic-update-slice | bytes 589828 | tf_op jit(solution)/shard_map/dynamic_update_slice | solution.py:27
  223.1 15.6 %dynamic_update_slice.195 = bf16[1,4,2,4,48,384]{5,1,4,3,2,0:T(4,128)(2,1)} dynamic-update-slice(bf16[1,4,2,4,48,384]{5,1,4,3,2,0:T(4,128)(2,1)} %dynamic_update_slice.194, bf16[1,1,2,4,48,384]{5,1,4,3,2,0:T(2,128)(2,1)} %copy.259, s32[]{:T(128)} %copy.457, s32[]{:T(128)S(6)} %select_n.195, s32[]{:T(128)} %copy.457, s32[]{:T(128)} %copy.457, s32[]{:T(128)} %copy.457, s32[]{:T(128)} %copy.457) | dynamic-update-slice | bytes 589828 | tf_op jit(solution)/shard_map/dynamic_update_slice | solution.py:27
  261.2 28.3 %while.32 = (s32[]{:T(128)}, bf16[3,512,3,128]{1,3,2,0:T(8,128)(2,1)}, f32[3,3,512]{2,1,0:T(4,128)}, bf16[3,512,3,128]{1,3,2,0:T(8,128)(2,1)}, bf16[3,512,3,128]...) while((s32[]{:T(128)}, ...), condition=%wide.region_4.5_spmd.clone, body=%wide.region_1.4_spmd.clone.sunk | while | flops 828570112 | bytes 26533008 | solution.py:247
  293.2 6.5 constant_dynamic-slice_fusion.31
  308.3 39.4 %all-gather.5.cloned.1.call-done = bf16[2,4,4,48,1536]{4,3,1,0,2:T(8,128)(2,1)} async-done(((bf16[2,4,1,48,1536]{4,3,1,0,2:T(8,128)(2,1)}), bf16[2,4,4,48,1536]{4,3,1,0,2:T(8,128)(2,1)}) %all-gather.5.cloned.1.call-update) | async-done | bytes 4718608 | tf_op jit(solution)/shard_map/all_gather | solution.py:212
  354.9 8.0 collective-permute-done.9
  389.6 9.3 collective-permute-done.19
  406.1 7.1 collective-permute-done.21
  483.2 9.3 collective-permute-done.35
  499.3 18.5 %collective-permute-done.27 = bf16[2,192,1536]{2,1,0:T(8,128)(2,1)S(1)} collective-permute-done((bf16[2,192,1536]{2,1,0:T(8,128)(2,1)S(1)}, bf16[2,192,1536]{2,1,0:T(8,128)(2,1)S(1)}, u32[]{:S(2)}, u32[]{:S(2)}) %collective-permute-start.27) | collective-permute-done | bytes 1179680 | tf_op jit(solution)/shard_map/ppermute | solution.py:16
  521.8 10.2 %collective-permute-done.36 = bf16[192,1536]{1,0:T(8,128)(2,1)S(1)} collective-permute-done((bf16[192,1536]{1,0:T(8,128)(2,1)S(1)}, bf16[192,1536]{1,0:T(8,128)(2,1)S(1)}, u32[]{:S(2)}, u32[]{:S(2)}) %collective-permute-start.36) | collective-permute-done | bytes 589856 | tf_op jit(solution)/shard_map/ppermute | solution.py:16
  532.8 7.2 collective-permute-done.28
  558.4 13.1 %dynamic_update_slice.202 = bf16[3,4,128,384]{2,1,3,0:T(4,128)(2,1)S(1)} dynamic-update-slice(bf16[3,4,128,384]{2,1,3,0:T(4,128)(2,1)S(1)} %broadcast_in_dim.246, bf16[3,1,128,384]{2,1,3,0:T(2,128)(2,1)S(1)} %copy.279, s32[]{:T(128)} %copy.457, s32[]{:T(128)S(6)} %select_n.199, s32[]{:T(128)} %copy.457, s32[]{:T(128)} %copy.457) | dynamic-update-slice | bytes 589828 | tf_op jit(solution)/shard_map/dynamic_update_slice | solution.py:27
  573.4 13.1 %dynamic_update_slice.203 = bf16[3,4,128,384]{2,1,3,0:T(4,128)(2,1)S(1)} dynamic-update-slice(bf16[3,4,128,384]{2,1,3,0:T(4,128)(2,1)S(1)} %dynamic_update_slice.202, bf16[3,1,128,384]{2,1,3,0:T(2,128)(2,1)S(1)} %copy.281, s32[]{:T(128)} %copy.457, s32[]{:T(128)S(6)} %select_n.208, s32[]{:T(128)} %copy.457, s32[]{:T(128)} %copy.457) | dynamic-update-slice | bytes 589828 | tf_op jit(solution)/shard_map/dynamic_update_slice | solution.py:27
  586.5 13.1 %dynamic_update_slice.204 = bf16[3,4,128,384]{2,1,3,0:T(4,128)(2,1)S(1)} dynamic-update-slice(bf16[3,4,128,384]{2,1,3,0:T(4,128)(2,1)S(1)} %dynamic_update_slice.203, bf16[3,1,128,384]{2,1,3,0:T(2,128)(2,1)S(1)} %copy.283, s32[]{:T(128)} %copy.457, s32[]{:T(128)S(6)} %select_n.206, s32[]{:T(128)} %copy.457, s32[]{:T(128)} %copy.457) | dynamic-update-slice | bytes 589828 | tf_op jit(solution)/shard_map/dynamic_update_slice | solution.py:27
  599.7 13.1 %dynamic_update_slice.205 = bf16[3,4,128,384]{2,1,3,0:T(4,128)(2,1)S(1)} dynamic-update-slice(bf16[3,4,128,384]{2,1,3,0:T(4,128)(2,1)S(1)} %dynamic_update_slice.204, bf16[3,1,128,384]{2,1,3,0:T(2,128)(2,1)S(1)} %copy.285, s32[]{:T(128)} %copy.457, s32[]{:T(128)S(6)} %select_n.202, s32[]{:T(128)} %copy.457, s32[]{:T(128)} %copy.457) | dynamic-update-slice | bytes 589828 | tf_op jit(solution)/shard_map/dynamic_update_slice | solution.py:27
  616.4 81.4 %while.33 = (s32[]{:T(128)}, f32[3,512,3,128]{1,3,2,0:T(8,128)}, f32[3,512,3,128]{1,3,2,0:T(8,128)}, bf16[3,512,3,128]{1,3,2,0:T(8,128)(2,1)}, f32[3,512,3,128]{...) while((s32[]{:T(128)}, f32[3,512,3,128]{1,3,2,0:T(8,128)}, ...), condition=%wide.region_9.10_spmd.clone, body=%wide.region_7.9_spmd.clone.sunk | while | flops 2043214336 | bytes 85507328 | solution.py:344
  699.2 7.2 fusion.66
  736.1 10.0 %convolution_convert_fusion.2 = bf16[1536,1536]{1,0:T(8,128)(2,1)} fusion(bf16[1536,1152]{1,0:T(8,128)(2,1)} %bitcast_dynamic-update-slice_fusion.6, bf16[1536,1152]{1,0:T(8,128)(2,1)S(1)} %bitcast.522), kind=kOutput, calls=%fused_computation.94 | convolution fusion | flops 5438177280 | bytes 11796480 | tf_op jit(solution)/shard_map/rc,dc->rd/dot_general | solution.py:159
  751.9 6.7 convolution_convert_fusion.1
  768.1 8.3 collective-permute-done.53
  793.4 11.1 %collective-permute-done.55 = bf16[192,384]{1,0:T(8,128)(2,1)} collective-permute-done((bf16[192,384]{1,0:T(8,128)(2,1)}, bf16[192,384]{1,0:T(8,128)(2,1)}, u32[]{:S(2)}, u32[]{:S(2)}) %collective-permute-start.55) | collective-permute-done | bytes 147488 | tf_op jit(solution)/shard_map/ppermute | solution.py:21
  811.1 76.9 %all-reduce.3.cloned.1.call-done = bf16[2,4,4,48,1536]{4,3,2,1,0:T(8,128)(2,1)} async-done(((bf16[2,4,4,48,1536]{4,3,2,1,0:T(8,128)(2,1)}), bf16[2,4,4,48,1536]{4,3,2,1,0:T(8,128)(2,1)}) %all-reduce.3.cloned.1.call-update) | async-done | bytes 4718608
  905.7 9.7 collective-permute-done.59
  930.2 10.6 %psum.7 = f32[2,192]{1,0:T(2,128)S(1)} all-reduce(f32[2,192]{1,0:T(2,128)S(1)} %pad_maximum_fusion.22), channel_id=1, replica_groups=mesh['dp'=4,'ctx'=2,'mp'=4] {'mp'}, use_global_device_ids=true, to_apply=%region_15.16 | all-reduce | flops 384 | bytes 3072 | tf_op jit(solution)/shard_map/psum | solution.py:368
  941.4 33.3 %reduce-scatter.5.cloned.1.call-done = bf16[3,128,1536]{2,1,0:T(8,128)(2,1)} async-done(((bf16[3,512,1536]{2,1,0:T(8,128)(2,1)}), bf16[3,128,1536]{2,1,0:T(8,128)(2,1)}) %reduce-scatter.5.cloned.1.call-update) | async-done | bytes 1179664 | tf_op jit(solution)/shard_map/reduce_scatter | solution.py:357
  (588 shorter events, 486.0 us)
Async XLA Ops:
  7.2 156.3 %all-gather.3.cloned.1.call-start = ((), (), s32[]{:S(2)}) async-start(), calls=%async_computation.1 | async-start | bytes 5898240 | tf_op jit(solution)/shard_map/all_gather | solution.py:180
  12.2 335.5 %all-gather.5.cloned.1.call-start = ((), (), s32[]{:S(2)}) async-start(), calls=%async_computation.2 | async-start | bytes 5898240 | tf_op jit(solution)/shard_map/all_gather | solution.py:212
  13.3 52.3 %collective-permute-start = (bf16[192,1152]{1,0:T(8,128)(2,1)}, bf16[192,1152]{1,0:T(8,128)(2,1)}, u32[]{:S(2)}, u32[]{:S(2)}) collective-permute-start(bf16[192,1152]{1,0:T(8,128)(2,1)} %pad_maximum_fusion.19), channel_id=1, source_target_pairs={{0,8},{8,0},{16,24},{24,16},{1,9},{9,1},{17,25},{25,17},{2,10},{10... | collective-permute-start | bytes 1327112 | tf_op jit(solution)/shard_map/ppermute | solution.py:16
  16.2 46.9 %collective-permute-start.1 = (bf16[192,1152]{1,0:T(8,128)(2,1)}, bf16[192,1152]{1,0:T(8,128)(2,1)}, u32[]{:S(2)}, u32[]{:S(2)}) collective-permute-start(bf16[192,1152]{1,0:T(8,128)(2,1)} %pad_maximum_fusion.19), channel_id=1, source_target_pairs={{0,16},{8,24},{16,0},{24,8},{1,17},{9,25},{17,1},{25,9},{2,18},{10... | collective-permute-start | bytes 1327112 | tf_op jit(solution)/shard_map/ppermute | solution.py:16
  17.8 42.5 %collective-permute-start.10 = (bf16[192,384]{1,0:T(8,128)(2,1)S(1)}, bf16[192,384]{1,0:T(8,128)(2,1)}, u32[]{:S(2)}, u32[]{:S(2)}) collective-permute-start(bf16[192,384]{1,0:T(8,128)(2,1)S(1)} %bitcast.590), channel_id=1, source_target_pairs={{0,1},{1,2},{2,3},{3,0},{4,5},{5,6},{6,7},{7,4},{8,9},{9,10},{10,1... | collective-permute-start | bytes 442376 | tf_op jit(solution)/shard_map/ppermute | solution.py:21
  19.3 42.6 %collective-permute-start.11 = (bf16[192,384]{1,0:T(8,128)(2,1)S(1)}, bf16[192,384]{1,0:T(8,128)(2,1)S(1)}, u32[]{:S(2)}, u32[]{:S(2)}) collective-permute-start(bf16[192,384]{1,0:T(8,128)(2,1)S(1)} %bitcast.591), channel_id=1, source_target_pairs={{0,2},{1,3},{2,0},{3,1},{4,6},{5,7},{6,4},{7,5},{8,10},{9,11},{10,... | collective-permute-start | bytes 442376 | tf_op jit(solution)/shard_map/ppermute | solution.py:21
  21.9 74.1 %collective-permute-start.12 = (bf16[192,384]{1,0:T(8,128)(2,1)S(1)}, bf16[192,384]{1,0:T(8,128)(2,1)}, u32[]{:S(2)}, u32[]{:S(2)}) collective-permute-start(bf16[192,384]{1,0:T(8,128)(2,1)S(1)} %bitcast.592), channel_id=1, source_target_pairs={{0,3},{1,0},{2,1},{3,2},{4,7},{5,4},{6,5},{7,6},{8,11},{9,8},{10,9... | collective-permute-start | bytes 442376 | tf_op jit(solution)/shard_map/ppermute | solution.py:21
  60.2 42.0 %collective-permute-start.22 = (bf16[2,4,192,192]{3,2,1,0:T(8,128)(2,1)}, bf16[2,4,192,192]{3,2,1,0:T(8,128)(2,1)S(1)}, u32[]{:S(2)}, u32[]{:S(2)}) collective-permute-start(bf16[2,4,192,192]{3,2,1,0:T(8,128)(2,1)} %get-tuple-element.462), channel_id=1, source_target_pairs={{0,4},{4,0},{1,5},{5,1},{2,6},{6,2},{3,7},{7,3},{8,12},{12,8},{9,1... | collective-permute-start | bytes 1769480 | tf_op jit(solution)/shard_map/ppermute | solution.py:16
  61.9 187.6 %collective-permute-start.31 = (bf16[384,1536]{1,0:T(8,128)(2,1)}, bf16[384,1536]{1,0:T(8,128)(2,1)}, u32[]{:S(2)}, u32[]{:S(2)}) collective-permute-start(bf16[384,1536]{1,0:T(8,128)(2,1)} %bitcast.548), channel_id=1, source_target_pairs={{0,8},{8,0},{16,24},{24,16},{1,9},{9,1},{17,25},{25,17},{2,10},{10... | collective-permute-start | bytes 3538952 | tf_op jit(solution)/shard_map/ppermute | solution.py:16
  96.0 60.3 %collective-permute-start.4 = (bf16[4,192,1152]{2,1,0:T(8,128)(2,1)}, bf16[4,192,1152]{2,1,0:T(8,128)(2,1)}, u32[]{:S(2)}, u32[]{:S(2)}) collective-permute-start(bf16[4,192,1152]{2,1,0:T(8,128)(2,1)} %fusion.169), channel_id=1, source_target_pairs={{0,4},{4,0},{1,5},{5,1},{2,6},{6,2},{3,7},{7,3},{8,12},{12,8},{9,1... | collective-permute-start | bytes 5308424 | tf_op jit(solution)/shard_map/ppermute | solution.py:16
  97.6 54.6 %collective-permute-start.13 = (bf16[192,1536]{1,0:T(8,128)(2,1)}, bf16[192,1536]{1,0:T(8,128)(2,1)}, u32[]{:S(2)}, u32[]{:S(2)}) collective-permute-start(bf16[192,1536]{1,0:T(8,128)(2,1)} %constant_dynamic-update-slice_fusion.1), channel_id=1, source_target_pairs={{0,8},{8,0},{16,24},{24,16},{1,9},{9,1},{17,25},{25,17},{2,10},{10... | collective-permute-start | bytes 1769480 | tf_op jit(solution)/shard_map/ppermute | solution.py:16
  98.2 50.8 %collective-permute-start.14 = (bf16[192,1536]{1,0:T(8,128)(2,1)}, bf16[192,1536]{1,0:T(8,128)(2,1)}, u32[]{:S(2)}, u32[]{:S(2)}) collective-permute-start(bf16[192,1536]{1,0:T(8,128)(2,1)} %constant_dynamic-update-slice_fusion.1), channel_id=1, source_target_pairs={{0,16},{8,24},{16,0},{24,8},{1,17},{9,25},{17,1},{25,9},{2,18},{10... | collective-permute-start | bytes 1769480 | tf_op jit(solution)/shard_map/ppermute | solution.py:16
  128.4 47.3 %collective-permute-start.23 = (bf16[2,4,48,384]{3,2,1,0:T(8,128)(2,1)}, bf16[2,4,48,384]{3,2,1,0:T(8,128)(2,1)}, u32[]{:S(2)}, u32[]{:S(2)}) collective-permute-start(bf16[2,4,48,384]{3,2,1,0:T(8,128)(2,1)} %get-tuple-element.478), channel_id=1, source_target_pairs={{0,8},{8,0},{16,24},{24,16},{1,9},{9,1},{17,25},{25,17},{2,10},{10... | collective-permute-start | bytes 884744 | tf_op jit(solution)/shard_map/ppermute | solution.py:16
  176.7 69.9 %collective-permute-start.32 = (bf16[384,1536]{1,0:T(8,128)(2,1)S(1)}, bf16[384,1536]{1,0:T(8,128)(2,1)}, u32[]{:S(2)}, u32[]{:S(2)}) collective-permute-start(bf16[384,1536]{1,0:T(8,128)(2,1)S(1)} %bitcast.550), channel_id=1, source_target_pairs={{0,16},{8,24},{16,0},{24,8},{1,17},{9,25},{17,1},{25,9},{2,18},{10... | collective-permute-start | bytes 3538952 | tf_op jit(solution)/shard_map/ppermute | solution.py:16
  178.3 63.9 %collective-permute-start.15 = (bf16[96,1536]{1,0:T(8,128)(2,1)}, bf16[96,1536]{1,0:T(8,128)(2,1)}, u32[]{:S(2)}, u32[]{:S(2)}) collective-permute-start(bf16[96,1536]{1,0:T(8,128)(2,1)} %slice.534), channel_id=1, source_target_pairs={{0,16},{8,24},{16,0},{24,8},{1,17},{9,25},{17,1},{25,9},{2,18},{10... | collective-permute-start | bytes 884744 | tf_op jit(solution)/shard_map/ppermute | solution.py:16
  178.7 81.4 %collective-permute-start.5 = (bf16[3,512,3,128]{1,3,2,0:T(8,128)(2,1)S(1)}, bf16[3,512,3,128]{1,3,2,0:T(8,128)(2,1)}, u32[]{:S(2)}, u32[]{:S(2)}) collective-permute-start(bf16[3,512,3,128]{1,3,2,0:T(8,128)(2,1)S(1)} %fusion.103), channel_id=1, source_target_pairs={{0,4},{1,5},{2,6},{3,7},{8,12},{9,13},{10,14},{11,15},{16,20},{17,... | collective-permute-start | bytes 3538952 | tf_op jit(solution)/shard_map/ppermute | solution.py:226
  181.1 77.4 %collective-permute-start.6 = (bf16[3,512,3,128]{1,3,2,0:T(8,128)(2,1)S(1)}, bf16[3,512,3,128]{1,3,2,0:T(8,128)(2,1)}, u32[]{:S(2)}, u32[]{:S(2)}) collective-permute-start(bf16[3,512,3,128]{1,3,2,0:T(8,128)(2,1)S(1)} %pad_maximum_fusion.9), channel_id=1, source_target_pairs={{0,4},{1,5},{2,6},{3,7},{8,12},{9,13},{10,14},{11,15},{16,20},{17,... | collective-permute-start | bytes 3538952 | tf_op jit(solution)/shard_map/ppermute | solution.py:226
  241.9 646.1 %all-reduce.3.cloned.1.call-start = ((), (), s32[]{:S(2)}) async-start(), calls=%async_computation.4 | async-start | bytes 9437184
  244.1 60.9 %collective-permute-start.17 = (bf16[4,192,1536]{2,1,0:T(8,128)(2,1)}, bf16[4,192,1536]{2,1,0:T(8,128)(2,1)}, u32[]{:S(2)}, u32[]{:S(2)}) collective-permute-start(bf16[4,192,1536]{2,1,0:T(8,128)(2,1)} %fusion.138), channel_id=1, source_target_pairs={{0,4},{4,0},{1,5},{5,1},{2,6},{6,2},{3,7},{7,3},{8,12},{12,8},{9,1... | collective-permute-start | bytes 7077896 | tf_op jit(solution)/shard_map/ppermute | solution.py:16
  249.0 129.2 %collective-permute-start.34 = (bf16[192,1536]{1,0:T(8,128)(2,1)}, bf16[192,1536]{1,0:T(8,128)(2,1)}, u32[]{:S(2)}, u32[]{:S(2)}) collective-permute-start(bf16[192,1536]{1,0:T(8,128)(2,1)} %slice.555), channel_id=1, source_target_pairs={{0,8},{8,0},{16,24},{24,16},{1,9},{9,1},{17,25},{25,17},{2,10},{10... | collective-permute-start | bytes 1769480 | tf_op jit(solution)/shard_map/ppermute | solution.py:16
  251.4 126.8 %collective-permute-start.33 = (bf16[192,1536]{1,0:T(8,128)(2,1)}, bf16[192,1536]{1,0:T(8,128)(2,1)}, u32[]{:S(2)}, u32[]{:S(2)}) collective-permute-start(bf16[192,1536]{1,0:T(8,128)(2,1)} %slice.554), channel_id=1, source_target_pairs={{0,16},{8,24},{16,0},{24,8},{1,17},{9,25},{17,1},{25,9},{2,18},{10... | collective-permute-start | bytes 1769480 | tf_op jit(solution)/shard_map/ppermute | solution.py:16
  301.9 52.8 %collective-permute-start.7 = (bf16[3,128,384]{2,1,0:T(8,128)(2,1)S(1)}, bf16[3,128,384]{2,1,0:T(8,128)(2,1)S(1)}, u32[]{:S(2)}, u32[]{:S(2)}) collective-permute-start(bf16[3,128,384]{2,1,0:T(8,128)(2,1)S(1)} %bitcast.576), channel_id=1, source_target_pairs={{0,1},{1,2},{2,3},{3,0},{4,5},{5,6},{6,7},{7,4},{8,9},{9,10},{10,1... | collective-permute-start | bytes 884744 | tf_op jit(solution)/shard_map/ppermute | solution.py:21
  304.7 50.1 %collective-permute-start.8 = (bf16[3,128,384]{2,1,0:T(8,128)(2,1)S(1)}, bf16[3,128,384]{2,1,0:T(8,128)(2,1)S(1)}, u32[]{:S(2)}, u32[]{:S(2)}) collective-permute-start(bf16[3,128,384]{2,1,0:T(8,128)(2,1)S(1)} %bitcast.574), channel_id=1, source_target_pairs={{0,2},{1,3},{2,0},{3,1},{4,6},{5,7},{6,4},{7,5},{8,10},{9,11},{10,... | collective-permute-start | bytes 884744 | tf_op jit(solution)/shard_map/ppermute | solution.py:21
  354.7 64.0 %collective-permute-start.26 = (bf16[2,4,192,1536]{3,2,1,0:T(8,128)(2,1)}, bf16[2,4,192,1536]{3,2,1,0:T(8,128)(2,1)}, u32[]{:S(2)}, u32[]{:S(2)}) collective-permute-start(bf16[2,4,192,1536]{3,2,1,0:T(8,128)(2,1)} %bitcast.515), channel_id=1, source_target_pairs={{0,4},{4,0},{1,5},{5,1},{2,6},{6,2},{3,7},{7,3},{8,12},{12,8},{9,1... | collective-permute-start | bytes 14155784 | tf_op jit(solution)/shard_map/ppermute | solution.py:16
  468.1 49.7 %collective-permute-start.27 = (bf16[2,192,1536]{2,1,0:T(8,128)(2,1)S(1)}, bf16[2,192,1536]{2,1,0:T(8,128)(2,1)S(1)}, u32[]{:S(2)}, u32[]{:S(2)}) collective-permute-start(bf16[2,192,1536]{2,1,0:T(8,128)(2,1)S(1)} %pad_maximum_fusion.10), channel_id=1, source_target_pairs={{0,8},{8,0},{16,24},{24,16},{1,9},{9,1},{17,25},{25,17},{2,10},{10... | collective-permute-start | bytes 3538952 | tf_op jit(solution)/shard_map/ppermute | solution.py:16
  468.9 50.5 %collective-permute-start.29 = (bf16[2,192,1536]{2,1,0:T(8,128)(2,1)S(1)}, bf16[2,192,1536]{2,1,0:T(8,128)(2,1)S(1)}, u32[]{:S(2)}, u32[]{:S(2)}) collective-permute-start(bf16[2,192,1536]{2,1,0:T(8,128)(2,1)S(1)} %pad_maximum_fusion.11), channel_id=1, source_target_pairs={{0,16},{8,24},{16,0},{24,8},{1,17},{9,25},{17,1},{25,9},{2,18},{10... | collective-permute-start | bytes 3538952 | tf_op jit(solution)/shard_map/ppermute | solution.py:16
  494.4 37.6 %collective-permute-start.36 = (bf16[192,1536]{1,0:T(8,128)(2,1)S(1)}, bf16[192,1536]{1,0:T(8,128)(2,1)S(1)}, u32[]{:S(2)}, u32[]{:S(2)}) collective-permute-start(bf16[192,1536]{1,0:T(8,128)(2,1)S(1)} %get-tuple-element.416), channel_id=1, source_target_pairs={{0,16},{8,24},{16,0},{24,8},{1,17},{9,25},{17,1},{25,9},{2,18},{10... | collective-permute-start | bytes 1769480 | tf_op jit(solution)/shard_map/ppermute | solution.py:16
  496.0 36.1 %collective-permute-start.38 = (bf16[192,1536]{1,0:T(8,128)(2,1)S(1)}, bf16[192,1536]{1,0:T(8,128)(2,1)S(1)}, u32[]{:S(2)}, u32[]{:S(2)}) collective-permute-start(bf16[192,1536]{1,0:T(8,128)(2,1)S(1)} %get-tuple-element.417), channel_id=1, source_target_pairs={{0,8},{8,0},{16,24},{24,16},{1,9},{9,1},{17,25},{25,17},{2,10},{10... | collective-permute-start | bytes 1769480 | tf_op jit(solution)/shard_map/ppermute | solution.py:16
  557.4 141.8 %collective-permute-start.57 = (bf16[2,768,1536]{2,1,0:T(8,128)(2,1)}, bf16[2,768,1536]{2,1,0:T(8,128)(2,1)}, u32[]{:S(2)}, u32[]{:S(2)}) collective-permute-start(bf16[2,768,1536]{2,1,0:T(8,128)(2,1)} %fusion.68), channel_id=1, source_target_pairs={{0,4},{4,0},{1,5},{5,1},{2,6},{6,2},{3,7},{7,3},{8,12},{12,8},{9,1... | collective-permute-start | bytes 14155784 | tf_op jit(solution)/shard_map/ppermute | solution.py:16
  706.4 268.4 %reduce-scatter.5.cloned.1.call-start = ((), (), s32[]{:S(2)}) async-start(), calls=%async_computation.3 | async-start | bytes 5898240 | tf_op jit(solution)/shard_map/reduce_scatter | solution.py:357
  808.2 89.4 %collective-permute-start.46 = (bf16[96,1152]{1,0:T(8,128)(2,1)}, bf16[96,1152]{1,0:T(8,128)(2,1)S(1)}, u32[]{:S(2)}, u32[]{:S(2)}) collective-permute-start(bf16[96,1152]{1,0:T(8,128)(2,1)} %get-tuple-element.450), channel_id=1, source_target_pairs={{0,16},{8,24},{16,0},{24,8},{1,17},{9,25},{17,1},{25,9},{2,18},{10... | collective-permute-start | bytes 663560 | tf_op jit(solution)/shard_map/ppermute | solution.py:16
  809.7 88.7 %collective-permute-start.48 = (bf16[96,1152]{1,0:T(8,128)(2,1)S(1)}, bf16[96,1152]{1,0:T(8,128)(2,1)}, u32[]{:S(2)}, u32[]{:S(2)}) collective-permute-start(bf16[96,1152]{1,0:T(8,128)(2,1)S(1)} %get-tuple-element.451), channel_id=1, source_target_pairs={{0,8},{8,0},{16,24},{24,16},{1,9},{9,1},{17,25},{25,17},{2,10},{10... | collective-permute-start | bytes 663560 | tf_op jit(solution)/shard_map/ppermute | solution.py:16
  (114 other events, 1302.9 us)
Sparse Core Ops, SparseCore 0:
  12.4 98.2 all-gather.2
  242.0 105.6 all-gather.4
  706.5 181.4 all-reduce.2
  890.2 84.5 reduce-scatter.4

commit v2 on v1

v2 whole, which is shorter than its diff:
```python
import functools

import jax
import jax.numpy as jnp
from jax import lax
from jax.experimental import pallas as pl
from jax.experimental.pallas import tpu as pltpu
from jax.sharding import PartitionSpec as P

HEAD = 128
LEVELS = 4
EPSILON = 1e-06
NEGATIVE = -1e30
BF = jnp.bfloat16
F32 = jnp.float32
MIB = 1 << 20


def flip(shard, axis, bit):
    devices = lax.axis_size(axis)
    return lax.ppermute(shard, axis, [(i, i ^ bit) for i in range(devices)])


def turn(shard, axis, by):
    devices = lax.axis_size(axis)
    return lax.ppermute(shard, axis, [(i, (i + by) % devices) for i in range(devices)])


def after(values, *others):
    return lax.optimization_barrier((values,) + others)[0]


def put(buffer, part, index, dim=0):
    starts = [0] * buffer.ndim
    starts[dim] = index
    return lax.dynamic_update_slice(buffer, jnp.expand_dims(part, dim), tuple(starts))


def take(buffer, index, dim=0):
    return lax.dynamic_index_in_dim(buffer, index, dim, keepdims=False)


def side_by_side(parts):
    return jnp.concatenate([parts[k] for k in range(parts.shape[0])], axis=-1)


def pack(part, width):
    rows, cols = part.shape
    return side_by_side(part.reshape(width // cols, -1, cols))


def unpack(packed, cols):
    strips = packed.shape[1] // cols
    return jnp.concatenate([packed[:, k * cols : (k + 1) * cols] for k in range(strips)], 0)


def line_gather(part):
    ranks, rank = lax.axis_size("mp"), lax.axis_index("mp")
    upward, downward = [], []
    up = down = part
    for k in range(1, ranks):
        up = lax.ppermute(up, "mp", [(i, i + 1) for i in range(k - 1, ranks - 1)])
        down = lax.ppermute(down, "mp", [(i, i - 1) for i in range(1, ranks - k + 1)])
        upward.append(up)
        downward.append(down)
    whole = jnp.zeros((ranks,) + part.shape, part.dtype)
    for k in range(ranks - 1, 0, -1):
        whole = put(whole, upward[k - 1], jnp.maximum(rank - k, 0))
        whole = put(whole, downward[k - 1], jnp.minimum(rank + k, ranks - 1))
    return put(whole, part, rank)


def line_scatter(parts):
    ranks, rank = lax.axis_size("mp"), lax.axis_index("mp")
    up = down = None
    for k in range(1, ranks):
        send_up = take(parts, jnp.minimum(rank + ranks - k, ranks - 1))
        send_down = take(parts, jnp.maximum(rank + k - ranks, 0))
        if up is not None:
            send_up = (send_up.astype(F32) + up.astype(F32)).astype(parts.dtype)
            send_down = (send_down.astype(F32) + down.astype(F32)).astype(parts.dtype)
        up = lax.ppermute(send_up, "mp", [(i, i + 1) for i in range(k)])
        down = lax.ppermute(send_down, "mp", [(i, i - 1) for i in range(ranks - k, ranks)])
    return take(parts, rank).astype(F32) + up.astype(F32) + down.astype(F32)


def rank_swap(parts):
    ranks, rank = lax.axis_size("mp"), lax.axis_index("mp")
    found = [turn(take(parts, (rank + k) % ranks), "mp", k) for k in range(1, ranks)]
    whole = put(jnp.zeros(parts.shape, parts.dtype), take(parts, rank), rank)
    for k in range(1, ranks):
        whole = put(whole, found[k - 1], (rank + ranks - k) % ranks)
    return whole


def level_gather(part, mine):
    half = part.shape[0] // 2
    from_x = flip(part, "dp", 1)
    from_y = flip(part, "dp", 2)
    low_half = flip(from_x[:half], "dp", 2)
    high_half = flip(from_y[half:], "dp", 1)
    whole = put(jnp.zeros((LEVELS,) + part.shape, part.dtype), part, mine)
    whole = put(whole, from_x, mine ^ 1)
    whole = put(whole, from_y, mine ^ 2)
    return put(whole, jnp.concatenate([low_half, high_half], 0), mine ^ 3)


def level_gather_small(part, mine):
    whole = put(jnp.zeros((LEVELS,) + part.shape, part.dtype), part, mine)
    for k in range(1, LEVELS):
        whole = put(whole, flip(part, "dp", k), mine ^ k)
    return whole


def level_scatter_open(parts, mine):
    half = parts.shape[1] // 2
    own, by_x, by_y, by_xy = (take(parts, mine ^ k) for k in range(LEVELS))
    got_x = flip(jnp.stack([by_x[:half], by_xy[:half]]), "dp", 1)
    got_y = flip(jnp.stack([by_y[half:], by_xy[half:]]), "dp", 2)
    return own, by_x[half:], by_y[:half], got_x, got_y


def level_scatter_close(own, by_x, by_y, got_x, got_y):
    half = by_y.shape[0]
    send_y = (by_y.astype(F32) + got_x[1].astype(F32)).astype(own.dtype)
    send_x = (by_x.astype(F32) + got_y[1].astype(F32)).astype(own.dtype)
    last_y = flip(send_y, "dp", 2)
    last_x = flip(send_x, "dp", 1)
    first = own[:half].astype(F32) + got_x[0].astype(F32) + last_y.astype(F32)
    second = own[half:].astype(F32) + got_y[0].astype(F32) + last_x.astype(F32)
    return jnp.concatenate([first, second], 0)


def level_scatter(parts, mine):
    return level_scatter_close(*level_scatter_open(parts, mine))


def level_swap(parts, mine):
    whole = put(jnp.zeros(parts.shape, parts.dtype), take(parts, mine), mine)
    for k in range(1, LEVELS):
        whole = put(whole, flip(take(parts, mine ^ k), "dp", k), mine ^ k)
    return whole


def teams(devices):
    return [list(range(level, devices, LEVELS)) for level in range(LEVELS)]


def team_gather(part):
    devices = lax.axis_size("dp")
    if devices == LEVELS:
        return part[None]
    return lax.all_gather(part, "dp", axis=0, axis_index_groups=teams(devices))


def team_scatter(parts):
    devices = lax.axis_size("dp")
    if devices == LEVELS:
        return parts[0]
    return lax.psum_scatter(
        parts, "dp", scatter_dimension=0, axis_index_groups=teams(devices), tiled=False
    )


def pair_gather(part, mine, dim=0):
    other = flip(part, "ctx", 1)
    shape = part.shape[:dim] + (2,) + part.shape[dim:]
    return put(put(jnp.zeros(shape, part.dtype), part, mine, dim), other, 1 - mine, dim)


def pair_split(first, second, mine):
    own = jnp.where(mine == 0, first, second)
    return own, flip(jnp.where(mine == 0, second, first), "ctx", 1)


def pair_scatter(parts, mine, dim):
    other = flip(take(parts, 1 - mine, dim), "ctx", 1)
    return take(parts, mine, dim).astype(F32) + other.astype(F32)


def model_gather(part, level, ctx):
    rows, width = part.shape
    whole = team_gather(level_gather(part, level))
    whole = pair_gather(whole.reshape(-1, rows, width), ctx, 1)
    return whole.reshape(-1, width)


def model_scatter(grad, level, ctx, rows):
    width = grad.shape[1]
    parts = grad.reshape(-1, 2, rows, width)
    parts = pair_scatter(parts, ctx, 1).astype(grad.dtype)
    parts = team_scatter(parts.reshape(-1, LEVELS, rows, width))
    return level_scatter(parts, level)


def contract(left, right, left_dim, right_dim):
    return lax.dot_general(
        left, right, (((left_dim,), (right_dim,)), ((), ())), preferred_element_type=F32
    )


def turned(values, cosine, sine):
    return values * cosine + pltpu.roll(values, HEAD // 2, 1) * sine


def project_kernel(rows_ref, gain_ref, weight_ref, cos_ref, sin_ref, out_ref, normed_ref):
    @pl.when(pl.program_id(0) == 0)
    def _():
        values = rows_ref[...].reshape(normed_ref.shape).astype(F32)
        inv = lax.rsqrt(jnp.mean(values * values, axis=-1, keepdims=True) + EPSILON)
        normed_ref[...] = (values * inv * gain_ref[...]).astype(BF)

    values = contract(normed_ref[...], weight_ref[...], 1, 0)
    cosine, sine = cos_ref[0], sin_ref[0]
    for head in range(values.shape[1] // HEAD):
        cols = slice(head * HEAD, (head + 1) * HEAD)
        out_ref[0, :, cols] = turned(values[:, cols], cosine, sine).astype(BF)


def project(which, shard_len, rows, gain, weight, cosine, sine):
    ranks, _, width = rows.shape
    length = ranks * shard_len
    cols = weight.shape[1] // 3
    table = pl.BlockSpec((1, length, HEAD), lambda j: (j // 2, 0, 0))
    return pl.pallas_call(
        project_kernel,
        grid=(3,),
        in_specs=[
            pl.BlockSpec((ranks, shard_len, width), lambda j: (0, which, 0)),
            pl.BlockSpec((1, width), lambda j: (0, 0)),
            pl.BlockSpec((width, cols), lambda j: (0, j)),
            table,
            table,
        ],
        out_specs=[
            pl.BlockSpec((1, length, cols), lambda j: (j, 0, 0)),
            pl.BlockSpec((length, width), lambda j: (0, 0)),
        ],
        out_shape=[
            jax.ShapeDtypeStruct((3, length, cols), BF),
            jax.ShapeDtypeStruct((length, width), BF),
        ],
        compiler_params=pltpu.CompilerParams(vmem_limit_bytes=24 * MIB),
        cost_estimate=pl.CostEstimate(
            flops=6 * length * width * cols,
            bytes_accessed=4 * length * width + 6 * width * cols + 6 * length * cols,
            transcendentals=0,
        ),
        name="project",
    )(rows, gain, weight, cosine, sine)


def softmax_parts(query, key_own, key_early, first, late):
    factor = HEAD ** (-0.5)
    own = contract(query, key_own, 1, 1) * factor
    row_ids = first + lax.broadcasted_iota(jnp.int32, own.shape, 0)
    col_ids = lax.broadcasted_iota(jnp.int32, own.shape, 1)
    own = jnp.where(col_ids <= row_ids, own, NEGATIVE)
    early = contract(query, key_early, 1, 1) * factor if late else None
    return own, early


def attend_kernel(strip, ctx_ref, query_ref, key_ref, value_ref, early_ref, mixed_ref, log_ref):
    length = query_ref.shape[1]

    def run(late):
        for first in range(0, length, strip):
            end = first + strip
            own, early = softmax_parts(
                query_ref[0, first:end], key_ref[0, :end], early_ref[0], first, late
            )
            largest = jnp.max(own, axis=-1, keepdims=True)
            if late:
                largest = jnp.maximum(largest, jnp.max(early, axis=-1, keepdims=True))
            own = jnp.exp(own - largest)
            total = jnp.sum(own, axis=-1, keepdims=True)
            if late:
                early = jnp.exp(early - largest)
                total = total + jnp.sum(early, axis=-1, keepdims=True)
            inverse = 1.0 / total
            mixed = contract((own * inverse).astype(BF), value_ref[0, :end], 1, 0)
            if late:
                mixed = mixed + contract((early * inverse).astype(BF), early_ref[1], 1, 0)
            mixed_ref[first:end] = mixed.astype(BF)
            log_ref[0, first:end] = largest + jnp.log(total)

    @pl.when(ctx_ref[0] == 0)
    def _():
        run(False)

    @pl.when(ctx_ref[0] != 0)
    def _():
        run(True)


def attend(ctx_flag, qkv, early):
    _, length, cols = qkv.shape
    heads = cols // HEAD
    one = lambda which: pl.BlockSpec((1, length, HEAD), lambda h, c: (which, 0, h))
    return pl.pallas_call(
        functools.partial(attend_kernel, length // 2),
        grid_spec=pltpu.PrefetchScalarGridSpec(
            num_scalar_prefetch=1,
            grid=(heads,),
            in_specs=[
                one(0),
                one(1),
                one(2),
                pl.BlockSpec((2, length, HEAD), lambda h, c: (0, 0, h)),
            ],
            out_specs=[
                pl.BlockSpec((length, HEAD), lambda h, c: (0, h)),
                pl.BlockSpec((1, length, 1), lambda h, c: (h, 0, 0)),
            ],
        ),
        out_shape=[
            jax.ShapeDtypeStruct((length, cols), BF),
            jax.ShapeDtypeStruct((heads, length, 1), F32),
        ],
        compiler_params=pltpu.CompilerParams(vmem_limit_bytes=24 * MIB),
        cost_estimate=pl.CostEstimate(
            flops=8 * length * length * cols,
            bytes_accessed=14 * length * cols,
            transcendentals=2 * length * length * heads,
        ),
        name="attend",
    )(ctx_flag, qkv, qkv, qkv, early)


def attend_back_kernel(
    strip,
    ctx_ref,
    query_ref,
    key_ref,
    value_ref,
    early_ref,
    log_ref,
    grad_ref,
    cos_ref,
    sin_ref,
    query_out,
    own_out,
    early_out,
):
    length = query_ref.shape[1]
    factor = HEAD ** (-0.5)

    def run(late):
        early_key_sum = early_value_sum = 0.0
        for first in range(length - strip, -1, -strip):
            end = first + strip
            query = query_ref[0, first:end]
            grad = grad_ref[first:end]
            log = log_ref[0, first:end]
            own, early = softmax_parts(query, key_ref[0, :end], early_ref[0], first, late)
            own = jnp.exp(own - log)
            own_grad = contract(grad, value_ref[0, :end], 1, 1)
            inner = jnp.sum(own_grad * own, axis=-1, keepdims=True)
            if late:
                early = jnp.exp(early - log)
                early_grad = contract(grad, early_ref[1], 1, 1)
                inner = inner + jnp.sum(early_grad * early, axis=-1, keepdims=True)
            own_low = (own * (own_grad - inner)).astype(BF)
            grad_query = contract(own_low, key_ref[0, :end], 1, 0)
            grad_key = contract(own_low, query, 0, 0) * factor
            grad_value = contract(own.astype(BF), grad, 0, 0)
            if first == length - strip:
                own_out[0] = grad_key
                own_out[1] = grad_value
            else:
                own_out[0, :end] += grad_key
                own_out[1, :end] += grad_value
            if late:
                early_low = (early * (early_grad - inner)).astype(BF)
                grad_query = grad_query + contract(early_low, early_ref[0], 1, 0)
                early_key_sum = early_key_sum + contract(early_low, query, 0, 0)
                early_value_sum = early_value_sum + contract(early.astype(BF), grad, 0, 0)
            grad_query = grad_query * factor
            query_out[first:end] = turned(
                grad_query, cos_ref[0, first:end], -sin_ref[0, first:end]
            ).astype(BF)
        if late:
            early_out[0] = (early_key_sum * factor).astype(BF)
            early_out[1] = early_value_sum.astype(BF)
        else:
            early_out[...] = jnp.zeros(early_out.shape, BF)

    @pl.when(ctx_ref[0] == 0)
    def _():
        run(False)

    @pl.when(ctx_ref[0] != 0)
    def _():
        run(True)


def attend_back(ctx_flag, qkv, early, logs, grad, cosine, sine):
    _, length, cols = qkv.shape
    heads = cols // HEAD
    one = lambda which: pl.BlockSpec((1, length, HEAD), lambda h, c: (which, 0, h))
    pair = pl.BlockSpec((2, length, HEAD), lambda h, c: (0, 0, h))
    flat = pl.BlockSpec((length, HEAD), lambda h, c: (0, h))
    table = pl.BlockSpec((1, length, HEAD), lambda h, c: (0, 0, 0))
    return pl.pallas_call(
        functools.partial(attend_back_kernel, length // 2),
        grid_spec=pltpu.PrefetchScalarGridSpec(
            num_scalar_prefetch=1,
            grid=(heads,),
            in_specs=[
                one(0),
                one(1),
                one(2),
                pair,
                pl.BlockSpec((1, length, 1), lambda h, c: (h, 0, 0)),
                flat,
                table,
                table,
            ],
            out_specs=[flat, pair, pair],
        ),
        out_shape=[
            jax.ShapeDtypeStruct((length, cols), BF),
            jax.ShapeDtypeStruct((2, length, cols), F32),
            jax.ShapeDtypeStruct((2, length, cols), BF),
        ],
        compiler_params=pltpu.CompilerParams(vmem_limit_bytes=32 * MIB),
        cost_estimate=pl.CostEstimate(
            flops=20 * length * length * cols,
            bytes_accessed=28 * length * cols,
            transcendentals=2 * length * length * heads,
        ),
        name="attend_back",
    )(ctx_flag, qkv, qkv, qkv, early, logs, grad, cosine, sine)


def project_back_kernel(
    query_ref, own_ref, back_ref, cos_ref, sin_ref, weight_ref, low_ref, out_ref
):
    cols = query_ref.shape[1]

    @pl.when(pl.program_id(0) == 0)
    def _():
        low_ref[:, :cols] = query_ref[...]
        keys = own_ref[0] + back_ref[0].astype(F32)
        cosine, sine = cos_ref[0], -sin_ref[0]
        for head in range(cols // HEAD):
            part = slice(head * HEAD, (head + 1) * HEAD)
            into = slice(cols + head * HEAD, cols + (head + 1) * HEAD)
            low_ref[:, into] = turned(keys[:, part], cosine, sine).astype(BF)
        low_ref[:, 2 * cols :] = (own_ref[1] + back_ref[1].astype(F32)).astype(BF)

    out_ref[...] = contract(low_ref[...], weight_ref[...], 1, 1).astype(BF)


def project_back(grad_query, grad_own, back, cosine, sine, weight):
    length, cols = grad_query.shape
    width = weight.shape[0]
    step = width // 3
    whole = lambda shape: pl.BlockSpec(shape, lambda j: (0,) * len(shape))
    return pl.pallas_call(
        project_back_kernel,
        grid=(3,),
        in_specs=[
            whole((length, cols)),
            whole((2, length, cols)),
            whole((2, length, cols)),
            whole((1, length, HEAD)),
            whole((1, length, HEAD)),
            pl.BlockSpec((step, 3 * cols), lambda j: (j, 0)),
        ],
        out_specs=[
            whole((length, 3 * cols)),
            pl.BlockSpec((length, step), lambda j: (0, j)),
        ],
        out_shape=[
            jax.ShapeDtypeStruct((length, 3 * cols), BF),
            jax.ShapeDtypeStruct((length, width), BF),
        ],
        compiler_params=pltpu.CompilerParams(vmem_limit_bytes=24 * MIB),
        cost_estimate=pl.CostEstimate(
            flops=6 * length * width * cols,
            bytes_accessed=6 * width * cols + 18 * length * cols + 2 * length * width,
            transcendentals=0,
        ),
        name="project_back",
    )(grad_query, grad_own, back, cosine, sine, weight)


def gelu_both(values):
    scale = (2.0 / jnp.pi) ** 0.5
    square = values * values
    tanh = jnp.tanh(scale * values * (1.0 + 0.044715 * square))
    half = 0.5 * (1.0 + tanh)
    slope = half + 0.5 * values * (1.0 - tanh * tanh) * scale * (1.0 + 3 * 0.044715 * square)
    return values * half, slope


def feed_kernel(rows_ref, cot_ref, up_ref, down_ref, grad_ref, act_ref, pre_ref, sum_ref):
    step = pl.program_id(0)
    half = up_ref.shape[0]

    def run(used):
        upped = contract(rows_ref[0], up_ref[:used], 1, 1)
        activated, slope = gelu_both(upped)
        grad_act = contract(cot_ref[0], down_ref[:used], 1, 1)
        grad_upped = (grad_act * slope).astype(BF)
        act_ref[0, :, :used] = activated.astype(BF)
        pre_ref[0, :, :used] = grad_upped
        return contract(grad_upped, up_ref[:used], 1, 0)

    for one in range(LEVELS - 1):

        @pl.when(step == one)
        def _(one=one):
            grad_ref[0] = run(half // 2 ** (LEVELS - 2 - one)).astype(BF)

    @pl.when(step == LEVELS - 1)
    def _():
        sum_ref[...] = run(half)

    @pl.when(step == LEVELS)
    def _():
        grad_ref[0] = (sum_ref[...] + run(half)).astype(BF)


def feed(rows, cot, up, down):
    _, length, width = rows.shape
    half = up.shape[0] // 2
    by_level = pl.BlockSpec((1, length, width), lambda s: (jnp.minimum(s, LEVELS - 1), 0, 0))
    by_half = pl.BlockSpec((half, width), lambda s: (s // LEVELS, 0))
    by_step = pl.BlockSpec((1, length, half), lambda s: (s, 0, 0))
    return pl.pallas_call(
        feed_kernel,
        grid=(LEVELS + 1,),
        in_specs=[by_level, by_level, by_half, by_half],
        out_specs=[by_level, by_step, by_step],
        out_shape=[
            jax.ShapeDtypeStruct(rows.shape, BF),
            jax.ShapeDtypeStruct((LEVELS + 1, length, half), BF),
            jax.ShapeDtypeStruct((LEVELS + 1, length, half), BF),
        ],
        scratch_shapes=[pltpu.VMEM((length, width), F32)],
        compiler_params=pltpu.CompilerParams(vmem_limit_bytes=44 * MIB),
        cost_estimate=pl.CostEstimate(
            flops=24 * length * width * half,
            bytes_accessed=24 * length * width + 8 * half * width + 20 * length * half,
            transcendentals=5 * length * half,
        ),
        name="feed",
    )(rows, cot, up, down)


def feed_weights_kernel(
    rows_ref, cot_ref, act_ref, pre_ref, down_ref, grad_ref, out_ref, up_sum, down_sum, out_sum
):
    step = pl.program_id(0)
    half = down_ref.shape[0]
    _, ranks, _, blocks, sub, _ = grad_ref.shape

    def add(used, fresh):
        up_part = contract(pre_ref[0, :, :used], rows_ref[0], 0, 0)
        down_part = contract(act_ref[0, :, :used], cot_ref[0], 0, 0)
        if fresh == used:
            up_sum[:used] = up_part
            down_sum[:used] = down_part
        else:
            up_sum[:fresh] += up_part[:fresh]
            down_sum[:fresh] += down_part[:fresh]
            if fresh < used:
                up_sum[fresh:used] = up_part[fresh:]
                down_sum[fresh:used] = down_part[fresh:]
        return contract(act_ref[0, :, :used], down_ref[:used], 1, 0)

    def store():
        for block in range(blocks):
            for rank in range(ranks):
                first = (block * ranks + rank) * sub
                grad_ref[0, rank, 0, block] = up_sum[first : first + sub].astype(BF)
                grad_ref[0, rank, 1, block] = down_sum[first : first + sub].astype(BF)

    for one in range(LEVELS - 1):

        @pl.when(step == one)
        def _(one=one):
            used = half // 2 ** (LEVELS - 2 - one)
            out_ref[0] = add(used, used if one == 0 else used // 2).astype(BF)

    @pl.when(step == LEVELS - 1)
    def _():
        up_sum[...] += contract(pre_ref[0], rows_ref[0], 0, 0)
        down_sum[...] += contract(act_ref[0], cot_ref[0], 0, 0)
        out_sum[...] = contract(act_ref[0], down_ref[...], 1, 0)
        store()

    @pl.when(step == LEVELS)
    def _():
        out_ref[0] = (out_sum[...] + add(half, half)).astype(BF)
        store()


def feed_weights(rows, cot, activated, before, down, ranks, blocks):
    _, length, width = rows.shape
    half = down.shape[0] // 2
    sub = half // (ranks * blocks)
    by_level = pl.BlockSpec((1, length, width), lambda s: (jnp.minimum(s, LEVELS - 1), 0, 0))
    by_half = pl.BlockSpec((half, width), lambda s: (s // LEVELS, 0))
    by_step = pl.BlockSpec((1, length, half), lambda s: (s, 0, 0))
    shape = (2, ranks, 2, blocks, sub, width)
    return pl.pallas_call(
        feed_weights_kernel,
        grid=(LEVELS + 1,),
        in_specs=[by_level, by_level, by_step, by_step, by_half],
        out_specs=[
            pl.BlockSpec((1,) + shape[1:], lambda s: (s // LEVELS, 0, 0, 0, 0, 0)),
            by_level,
        ],
        out_shape=[jax.ShapeDtypeStruct(shape, BF), jax.ShapeDtypeStruct(rows.shape, BF)],
        scratch_shapes=[
            pltpu.VMEM((half, width), F32),
            pltpu.VMEM((half, width), F32),
            pltpu.VMEM((length, width), F32),
        ],
        compiler_params=pltpu.CompilerParams(vmem_limit_bytes=56 * MIB),
        cost_estimate=pl.CostEstimate(
            flops=24 * length * width * half,
            bytes_accessed=24 * length * width + 12 * half * width + 20 * length * half,
            transcendentals=0,
        ),
        name="feed_weights",
    )(rows, cot, activated, before, down)


def outer_kernel(count, *refs):
    lefts, rights, out_ref = refs[:count], refs[count : 2 * count], refs[-1]
    total = contract(lefts[0][...], rights[0][...], 0, 0)
    for left, right in zip(lefts[1:], rights[1:]):
        total = total + contract(left[...], right[...], 0, 0)
    out_ref[...] = total.astype(BF)


def outer(lefts, rights):
    rows, m = lefts[0].shape
    n = rights[0].shape[1]
    count = len(lefts)
    step = m // 4
    return pl.pallas_call(
        functools.partial(outer_kernel, count),
        grid=(4,),
        in_specs=[pl.BlockSpec((rows, step), lambda j: (0, j))] * count
        + [pl.BlockSpec((rows, n), lambda j: (0, 0))] * count,
        out_specs=pl.BlockSpec((step, n), lambda j: (j, 0)),
        out_shape=jax.ShapeDtypeStruct((m, n), BF),
        compiler_params=pltpu.CompilerParams(vmem_limit_bytes=32 * MIB),
        cost_estimate=pl.CostEstimate(
            flops=2 * count * rows * m * n,
            bytes_accessed=2 * (count * rows * (m + n) + m * n),
            transcendentals=0,
        ),
        name="outer",
    )(*lefts, *rights)


def inverse_rms(values):
    return lax.rsqrt(jnp.mean(values * values, axis=-1, keepdims=True) + EPSILON)


def norm_back(values, inv_rms, weighted):
    return inv_rms * weighted - values * (inv_rms * inv_rms * inv_rms) * jnp.mean(
        weighted * values, axis=-1, keepdims=True
    )


def rotation(positions, head_size):
    half_size = head_size // 2
    frequency = 10000.0 ** (-jnp.arange(half_size, dtype=jnp.float32) / half_size)
    angles = positions.astype(jnp.float32)[:, None] * frequency[None, :]
    cosine, sine = jnp.cos(angles), jnp.sin(angles)
    cosine = jnp.concatenate([cosine, cosine], -1)
    sine = jnp.concatenate([-sine, sine], -1)
    return (
        jnp.stack([cosine, jnp.ones_like(cosine)]),
        jnp.stack([sine, jnp.zeros_like(sine)]),
    )


def product(equation, left, right):
    return jnp.einsum(equation, left, right, preferred_element_type=F32)


def local(inputs, w_query, w_key, w_value, w_out, w_up, w_down, gain_attn, gain_ffn, cotangent):
    count, shard_len, width = inputs.shape
    own_rows = count * shard_len
    ranks = lax.axis_size("mp")
    length_half = shard_len * ranks
    level = lax.axis_index("dp") % LEVELS
    ctx = lax.axis_index("ctx")
    rank = lax.axis_index("mp")
    part_rows, head_cols = w_query.shape
    each = range(count)
    ctx_flag = ctx.astype(jnp.int32)[None]

    out_rows = w_out.size // width
    rows_all = jnp.concatenate([inputs.reshape(own_rows, width), pack(w_out.T, width)], 0)
    rows_all = lax.all_gather(rows_all, "mp", axis=0)

    gains = team_gather(level_gather_small(jnp.stack([gain_attn, gain_ffn]), level))
    gains = pair_gather(gains.reshape(-1, 2, part_rows), ctx, 1)
    gains = gains.transpose(2, 0, 1, 3).reshape(2, 1, width).astype(F32)
    gain_first, gain_second = gains[0], gains[1]

    qkv_full = model_gather(jnp.concatenate([w_query, w_key, w_value], axis=1), level, ctx)
    out_parts = [unpack(rows_all[k, own_rows:], head_cols) for k in range(ranks)]
    out_full = model_gather(jnp.concatenate(out_parts, 1), level, ctx)

    blocks, unit_cols = w_up.shape[1:]
    sub = unit_cols // LEVELS
    half_blocks = blocks // 2
    up_turned = w_up.transpose(1, 2, 0)
    halves = [
        jnp.stack([up_turned[b : b + half_blocks], w_down[b : b + half_blocks]])
        for b in (0, half_blocks)
    ]
    own_part, sent_part = pair_split(halves[0], halves[1], ctx)
    pair = jnp.concatenate(
        [jnp.where(ctx == 0, own_part, sent_part), jnp.where(ctx == 0, sent_part, own_part)], -1
    )
    pair = pair.reshape(2, half_blocks, LEVELS, sub, 2 * part_rows).transpose(2, 0, 1, 3, 4)
    swapped = team_gather(level_swap(pair, level))
    swapped = side_by_side(swapped.reshape(-1, 2, half_blocks, sub, 2 * part_rows))
    cot_rows = level_gather(
        after(cotangent, swapped, qkv_full).reshape(own_rows, width), level
    )
    ranked = lax.all_gather(swapped, "mp", axis=0)
    positions = ctx * length_half + jnp.arange(length_half, dtype=jnp.int32)
    cosine, sine = rotation(positions, HEAD)
    qkv, early, logs, normed_all, mixed_own, hidden, inv_second, rows_second = (
        [] for _ in range(8)
    )
    for i in each:
        qkv_one, normed_one = project(i, shard_len, rows_all, gain_first, qkv_full, cosine, sine)
        early_one = lax.ppermute(qkv_one[1:], "ctx", [(0, 1)])
        mixed_one, log_one = attend(ctx_flag, qkv_one, early_one)
        mixed_one = side_by_side(rank_swap(mixed_one.reshape(ranks, shard_len, head_cols)))
        attended = product("rc,dc->rd", mixed_one, out_full)
        hidden_one = inputs[i].astype(F32) + attended
        inv_one = inverse_rms(hidden_one)
        normed_two = (hidden_one * inv_one * gain_second).astype(BF)
        rows_second.append(level_gather(normed_two, level))
        qkv.append(qkv_one)
        early.append(early_one)
        logs.append(log_one)
        normed_all.append(normed_one)
        mixed_own.append(mixed_one)
        hidden.append(hidden_one)
        inv_second.append(inv_one)

    ranked = after(ranked, hidden[-1])
    ranked = ranked.transpose(1, 2, 0, 3, 4).reshape(2, half_blocks, unit_cols, width)
    up_mine = pair_gather(ranked[0], ctx).reshape(blocks * unit_cols, width)
    down_mine = pair_gather(ranked[1], ctx).reshape(blocks * unit_cols, width)
    rows_second = jnp.concatenate(rows_second, 1)
    grads_in, activated, before = feed(rows_second, cot_rows, up_mine, down_mine)
    grads_in = grads_in.reshape(LEVELS, count, shard_len, width)
    opened = [list(level_scatter_open(grads_in[:, i], level)) for i in each]

    activated = after(activated, *opened[0][3:])
    grad_ffn, results = feed_weights(
        rows_second, cot_rows, activated, before, down_mine, ranks, half_blocks
    )
    grad_ffn = pair_scatter(grad_ffn.reshape(2, -1, width), ctx, 0).astype(BF)

    grad_first_all, grad_hidden_all, grad_low_all, grad_qkv_all = [], [], [], []
    for i in each:
        if i == 0:
            opened[i] = lax.optimization_barrier((opened[i], grad_ffn))[0]
        grad_second = gain_second * level_scatter_close(*opened[i])
        grad_hidden = cotangent[i].astype(F32) + norm_back(hidden[i], inv_second[i], grad_second)
        grad_low = grad_hidden.astype(BF)
        grad_mixed = product("rd,dc->rc", grad_low, out_full).astype(BF)
        grad_mixed = jnp.stack(jnp.split(grad_mixed, ranks, axis=1))
        grad_mixed = rank_swap(grad_mixed).reshape(length_half, head_cols)
        grad_query, grad_own, grad_early = attend_back(
            ctx_flag, qkv[i], early[i], logs[i], grad_mixed, cosine, sine
        )
        back = lax.ppermute(grad_early, "ctx", [(1, 0)])
        grad_qkv, grad_first = project_back(grad_query, grad_own, back, cosine, sine, qkv_full)
        grad_first_all.append(grad_first.reshape(ranks, shard_len, width))
        grad_hidden_all.append(grad_hidden)
        grad_low_all.append(grad_low)
        grad_qkv_all.append(grad_qkv)

    grad_out_w = outer(grad_low_all, mixed_own)
    grad_out_w = model_scatter(grad_out_w, level, ctx, part_rows).astype(BF)
    pieces = []
    for k in range(ranks):
        pieces += [one[k] for one in grad_first_all]
        pieces.append(pack(grad_out_w[:, k * head_cols : (k + 1) * head_cols], width))
    grad_first = jnp.concatenate(pieces, 0)
    grad_first = lax.psum_scatter(grad_first, "mp", scatter_dimension=0, tiled=True)

    result = level_scatter(after(results, grad_hidden_all[-1]), level)
    outputs = (jnp.concatenate(hidden, 0) + result).astype(BF).reshape(inputs.shape)

    grad_ffn = lax.psum_scatter(grad_ffn, "mp", scatter_dimension=0, tiled=True)
    grad_ffn = grad_ffn.reshape(2, half_blocks, sub, width)
    grad_ffn = jnp.stack(jnp.split(grad_ffn, width // (2 * part_rows), axis=-1))
    grad_ffn = team_scatter(grad_ffn.reshape((-1, LEVELS) + grad_ffn.shape[1:]))
    grad_ffn = level_swap(grad_ffn, level).transpose(1, 2, 0, 3, 4)
    grad_ffn = grad_ffn.reshape(2, half_blocks, unit_cols, 2 * part_rows)
    own_part, sent_part = pair_split(grad_ffn[..., :part_rows], grad_ffn[..., part_rows:], ctx)
    grad_ffn = jnp.concatenate(
        [jnp.where(ctx == 0, own_part, sent_part), jnp.where(ctx == 0, sent_part, own_part)], 1
    ).astype(F32)
    grad_up_out = grad_ffn[0].transpose(2, 0, 1)
    grad_down_out = grad_ffn[1]
    gain_ffn_part = jnp.sum(grad_up_out * w_up.astype(F32), axis=(1, 2)) / gain_ffn.astype(F32)

    grad_qkv_w = outer(normed_all, grad_qkv_all)
    grad_qkv_w = model_scatter(grad_qkv_w, level, ctx, part_rows)
    originals = jnp.concatenate([w_query, w_key, w_value], axis=1).astype(F32)
    gain_attn_part = jnp.sum(grad_qkv_w * originals, axis=1) / gain_attn.astype(F32)
    gain_grads = jnp.stack([gain_attn_part, gain_ffn_part])
    gain_grads = gain_grads + sum([turn(gain_grads, "mp", k) for k in range(1, ranks)])

    grad_first = after(grad_first, gain_grads, outputs, grad_qkv_w, grad_up_out, grad_down_out)
    grad_out_out = unpack(grad_first[own_rows:], head_cols).astype(F32).T
    inputs_f = inputs.astype(F32)
    input_grads = jnp.stack(grad_hidden_all) + norm_back(
        inputs_f,
        inverse_rms(inputs_f),
        gain_first * grad_first[:own_rows].reshape(inputs.shape).astype(F32),
    )
    return (
        outputs,
        input_grads,
        grad_qkv_w[:, :head_cols],
        grad_qkv_w[:, head_cols : 2 * head_cols],
        grad_qkv_w[:, 2 * head_cols :],
        grad_out_out,
        grad_up_out,
        grad_down_out,
        gain_grads[0],
        gain_grads[1],
    )


def solution(mesh):
    in_specs = (
        P("dp", ("ctx", "mp"), None),
        P(("dp", "ctx"), "mp"),
        P(("dp", "ctx"), "mp"),
        P(("dp", "ctx"), "mp"),
        P("mp", ("dp", "ctx")),
        P(("dp", "ctx"), None, "mp"),
        P(None, "mp", ("dp", "ctx")),
        P(("dp", "ctx")),
        P(("dp", "ctx")),
        P("dp", ("ctx", "mp"), None),
    )
    out_specs = (
        P("dp", ("ctx", "mp"), None),
        P("dp", ("ctx", "mp"), None),
        P(("dp", "ctx"), "mp"),
        P(("dp", "ctx"), "mp"),
        P(("dp", "ctx"), "mp"),
        P("mp", ("dp", "ctx")),
        P(("dp", "ctx"), None, "mp"),
        P(None, "mp", ("dp", "ctx")),
        P(("dp", "ctx")),
        P(("dp", "ctx")),
    )
    return jax.shard_map(local, mesh=mesh, in_specs=in_specs, out_specs=out_specs, check_vma=False)
```

time: 999 us -> 626 us (0.63)
  local copies, waits for them, and re-layouts: 363 us -> 99.7 us
  matrix products: 146 us -> 11.3 us
  Pallas kernels: 0 us -> 96.8 us
  waiting for transfers between devices: 288 us -> 202 us
  starting transfers between devices: 71.2 us -> 125 us
  other arithmetic: 89.1 us -> 65.4 us
  blocking collectives: 10.6 us -> 0 us
    dynamic_update_slice x46 -> x52, local copies, waits for them, and re-layouts: 203 us -> 22.4 us  [put(): lax.dynamic_update_slice(buffer, jnp.expand_dims(part, dim), tuple(starts))]
    dot_general x51 -> x6, matrix products: 146 us -> 11.3 us  [product(): return jnp.einsum(equation, left, right, preferred_element_type=F32)]
    pallas_call x0 -> x16, Pallas kernels: none -> 96.8 us  [the longest x1 20.5 us: feed_weights(): pl.pallas_call(feed_weights_kernel, grid=(LEVELS + 1,), in_specs=[by_leve...]
    unnamed x5 -> x4, waiting for transfers between devices: 77 us -> 0.07 us
    reduce_scatter x1 -> x2, waiting for transfers between devices: 33.3 us -> 0.01 us  [the longest x1 0.01 us: local(): lax.psum_scatter(grad_first, 'mp', scatter_dimension=0, tiled=True)]
    ppermute x12 -> x21, starting transfers between devices: 15.8 us -> 48.4 us  [turn(): lax.ppermute(shard, axis, [(i, (i + by) % devices) for i in range(devices)])]
    ppermute x12 -> x21, waiting for transfers between devices: 20.3 us -> 46 us  [turn(): lax.ppermute(shard, axis, [(i, (i + by) % devices) for i in range(devices)])]
    ppermute x46 -> x67, starting transfers between devices: 47.4 us -> 68 us  [flip(): return lax.ppermute(shard, axis, [(i, i ^ bit) for i in range(devices)])]
  transfers between devices with their start and end apart: 66 -> 98, of which waited for: 22 -> 43; matrix products, arithmetic and copies ran while one was open for 53% -> 23% of each run, Pallas kernels for 0% -> 10%
where the time goes in v2:
time: 626 us; the launch traced here: 617 us
  waiting for transfers between devices  202 us (32%)
  starting transfers between devices  125 us (20%)
  local copies, waits for them, and re-layouts  99.7 us (16%)
  Pallas kernels  96.8 us (15%)
  other arithmetic  65.4 us (10%)
  between operations  16.9 us (3%)
  matrix products  11.3 us (2%)
    ppermute x67, waiting for transfers between devices, flip(): return lax.ppermute(shard, axis, [(i, i ^ bit) for i in range(devices)])  120 us
    ppermute x67, starting transfers between devices, flip(): return lax.ppermute(shard, axis, [(i, i ^ bit) for i in range(devices)])  68 us
    ppermute x21, starting transfers between devices, turn(): lax.ppermute(shard, axis, [(i, (i + by) % devices) for i in range(devices)])  48.4 us
    ppermute x21, waiting for transfers between devices, turn(): lax.ppermute(shard, axis, [(i, (i + by) % devices) for i in range(devices)])  46 us
    unnamed x260, local copies, waits for them, and re-layouts  25.5 us
    dynamic_update_slice x52, local copies, waits for them, and re-layouts, put(): lax.dynamic_update_slice(buffer, jnp.expand_dims(part, dim), tuple(starts))  22.4 us
    all_gather x1, waiting for transfers between devices, local(): rows_all = lax.all_gather(rows_all, 'mp', axis=0)  21.7 us
    pallas_call x1, Pallas kernels, feed_weights(): pl.pallas_call(feed_weights_kernel, grid=(LEVELS + 1,), in_specs=[by_leve...  20.5 us
  transfers between devices with their start and end apart: 98, of which 43 were waited for; matrix products, arithmetic and copies ran while one was open for 23% of the time, Pallas kernels for 10%

profile of v2, /device:TPU:0, one launch (start us, length us, event | category | flops | bytes accessed | tf_op | source)
XLA Modules:
  0.0 617.0 jit_solution(7277260138779634275)
XLA Ops:
  38.2 4.5 collective-permute-done.39
  45.9 5.9 collective-permute-done.41
  69.6 11.9 %collective-permute-done.42 = bf16[384,1536]{1,0:T(8,128)(2,1)} collective-permute-done((bf16[384,1536]{1,0:T(8,128)(2,1)}, bf16[384,1536]{1,0:T(8,128)(2,1)}, u32[]{:S(2)}, u32[]{:S(2)}) %collective-permute-start.42) | collective-permute-done | bytes 1179680 | tf_op jit(solution)/shard_map/ppermute | solution.py:21
  90.9 21.7 %all-gather.5.cloned.1.call-done = bf16[1728,1536]{1,0:T(8,128)(2,1)} async-done(((bf16[432,1536]{1,0:T(8,128)(2,1)}), bf16[1728,1536]{1,0:T(8,128)(2,1)}) %all-gather.5.cloned.1.call-update) | async-done | bytes 5308432 | tf_op jit(solution)/shard_map/all_gather | solution.py:704
  119.6 4.5 project.5
  125.8 4.5 project.3
  132.9 4.5 project.4
  166.4 8.2 %collective-permute-start.21 = (bf16[128,384]{1,0:T(8,128)(2,1)S(1)}, bf16[128,384]{1,0:T(8,128)(2,1)S(1)}, u32[]{:S(2)}, u32[]{:S(2)}) collective-permute-start(bf16[128,384]{1,0:T(8,128)(2,1)S(1)} %get-tuple-element.278), channel_id=1, source_target_pairs={{0,3},{1,0},{2,1},{3,2},{4,7},{5,4},{6,5},{7,6},{8,11},{9,8},{10,9... | collective-permute-start | bytes 294920 | tf_op jit(solution)/shard_map/ppermute | solution.py:26
  179.1 16.2 %collective-permute-done.20 = bf16[128,384]{1,0:T(8,128)(2,1)S(1)} collective-permute-done((bf16[128,384]{1,0:T(8,128)(2,1)S(1)}, bf16[128,384]{1,0:T(8,128)(2,1)S(1)}, u32[]{:S(2)}, u32[]{:S(2)}) %collective-permute-start.20) | collective-permute-done | bytes 98336 | tf_op jit(solution)/shard_map/ppermute | solution.py:26
  212.9 14.7 %all-gather.7.cloned.1.call-done = bf16[8,4,48,1536]{3,2,1,0:T(8,128)(2,1)} async-done(((bf16[2,4,48,1536]{3,2,1,0:T(8,128)(2,1)}), bf16[8,4,48,1536]{3,2,1,0:T(8,128)(2,1)}) %all-gather.7.cloned.1.call-update) | async-done | bytes 4718608 | tf_op jit(solution)/shard_map/all_gather | solution.py:733
  267.9 16.7 %feed.1 = (bf16[4,384,1536]{2,1,0:T(8,128)(2,1)}, bf16[5,384,768]{2,1,0:T(8,128)(2,1)S(1)}, bf16[5,384,768]{2,1,0:T(8,128)(2,1)S(1)}) custom-call(bf16[4,384,1536]{2,1,0:T(8,128)(2,1)} %pad_maximum_fusion.rows_ref, bf16[4,384,1536]{2,1,0:T(8,128)(2,1)} %fusion.10.cot_ref, bf16[1536,1536]{1,0:T(8,128)(2,1)} %bitcast.579, bf16[1536,1536]{1,0:T(8,128)(2,1)} %bitcast.577), custom_call_target="tpu_custom_call" | custom-call | flops 10871635968 | bytes 29491200 | tf_op jit(solution)/shard_map/feed/pallas_call | solution.py:532
  284.6 6.4 %fusion.43 = (bf16[4,1,128,1536]{3,2,1,0:T(8,128)(2,1)}, bf16[4,1,128,1536]{3,2,1,0:T(8,128)(2,1)}, bf16[4,1,128,1536]{3,2,1,0:T(8,128)(2,1)S(1)}) fusion(bf16[4,3,128,1536]{3,2,1,0:T(8,128)(2,1)} %bitcast.576), kind=kLoop, calls=%fused_computation.364 | loop fusion | bytes 9437184 | tf_op jit(solution)/shard_map/slice | solution.py:764
  296.3 6.1 collective-permute-done.49
  304.6 20.5 %feed_weights.1 = (bf16[2,4,2,4,48,1536]{5,4,3,2,1,0:T(8,128)(2,1)}, bf16[4,384,1536]{2,1,0:T(8,128)(2,1)}) custom-call(bf16[4,384,1536]{2,1,0:T(8,128)(2,1)} %pad_maximum_fusion.rows_ref, bf16[4,384,1536]{2,1,0:T(8,128)(2,1)} %fusion.10.cot_ref, bf16[5,384,768]{2,1,0:T(8,128)(2,1)} %copy-done.38, bf16[5,384,768]{2,1,0:T(8,128)(2,1)} %copy-done.39, ...), custom_call_target="tpu_custom_call" | custom-call | flops 10871635968 | bytes 34209792 | tf_op jit(solution)/shard_map/feed_weights/pallas_call | solution.py:609
  337.0 6.1 collective-permute-done.50
  345.0 5.8 collective-permute-done.61
  363.2 5.8 fusion
  399.9 4.6 outer.2
  408.3 6.9 %collective-permute-start.66 = (bf16[128,384]{1,0:T(8,128)(2,1)S(1)}, bf16[128,384]{1,0:T(8,128)(2,1)S(1)}, u32[]{:S(2)}, u32[]{:S(2)}) collective-permute-start(bf16[128,384]{1,0:T(8,128)(2,1)S(1)} %get-tuple-element.257), channel_id=1, source_target_pairs={{0,2},{1,3},{2,0},{3,1},{4,6},{5,7},{6,4},{7,5},{8,10},{9,11},{10,... | collective-permute-start | bytes 294920 | tf_op jit(solution)/shard_map/ppermute | solution.py:26
  415.2 8.9 %collective-permute-done.65 = bf16[128,384]{1,0:T(8,128)(2,1)S(1)} collective-permute-done((bf16[128,384]{1,0:T(8,128)(2,1)S(1)}, bf16[128,384]{1,0:T(8,128)(2,1)S(1)}, u32[]{:S(2)}, u32[]{:S(2)}) %collective-permute-start.65) | collective-permute-done | bytes 98336 | tf_op jit(solution)/shard_map/ppermute | solution.py:26
  425.9 14.7 %collective-permute-done.66 = bf16[128,384]{1,0:T(8,128)(2,1)S(1)} collective-permute-done((bf16[128,384]{1,0:T(8,128)(2,1)S(1)}, bf16[128,384]{1,0:T(8,128)(2,1)S(1)}, u32[]{:S(2)}, u32[]{:S(2)}) %collective-permute-start.66) | collective-permute-done | bytes 98336 | tf_op jit(solution)/shard_map/ppermute | solution.py:26
  440.7 4.7 attend_back.5
  448.2 4.6 attend_back.3
  454.2 4.5 attend_back.4
  476.6 4.0 collective-permute-done.80
  505.0 7.7 %outer.3 = bf16[1536,1152]{1,0:T(8,128)(2,1)S(1)} custom-call(bf16[512,1536]{1,0:T(8,128)(2,1)S(1)} %copy-done.23, bf16[512,1536]{1,0:T(8,128)(2,1)S(1)} %copy-done.25, bf16[512,1536]{1,0:T(8,128)(2,1)S(1)} %copy-done.21, bf16[512,1152]{1,0:T(8,128)(2,1)S(1)} %copy-done.27, bf16[512,1152]{1,0:T(8,128)(2,1)S(1)} %copy-done.31, bf16[512,1152]{1,0:T(8,128)(2,1)S(1)} %copy-done.29), custom_call_target="tpu_custom_call" | custom-call | flops 5435817984 | bytes 11796480 | tf_op jit(solution)/shard_map/outer/pallas_call | solution.py:646
  514.1 4.3 collective-permute-start.82
  518.4 10.6 %collective-permute-done.56 = bf16[2,192,1536]{2,1,0:T(8,128)(2,1)S(1)} collective-permute-done((bf16[2,192,1536]{2,1,0:T(8,128)(2,1)S(1)}, bf16[2,192,1536]{2,1,0:T(8,128)(2,1)S(1)}, u32[]{:S(2)}, u32[]{:S(2)}) %collective-permute-start.56) | collective-permute-done | bytes 1179680 | tf_op jit(solution)/shard_map/ppermute | solution.py:21
  535.9 11.0 %collective-permute-done.55 = bf16[192,1536]{1,0:T(8,128)(2,1)} collective-permute-done((bf16[192,1536]{1,0:T(8,128)(2,1)}, bf16[192,1536]{1,0:T(8,128)(2,1)}, u32[]{:S(2)}, u32[]{:S(2)}) %collective-permute-start.55) | collective-permute-done | bytes 589856 | tf_op jit(solution)/shard_map/ppermute | solution.py:21
  561.6 6.5 %collective-permute-done.85 = bf16[2,96,1152]{2,1,0:T(8,128)(2,1)S(1)} collective-permute-done((bf16[2,96,1152]{2,1,0:T(8,128)(2,1)S(1)}, bf16[2,96,1152]{2,1,0:T(8,128)(2,1)S(1)}, u32[]{:S(2)}, u32[]{:S(2)}) %collective-permute-start.85) | collective-permute-done | bytes 442400 | tf_op jit(solution)/shard_map/ppermute | solution.py:21
  575.6 11.7 %collective-permute-done.89 = bf16[2,4,48,384]{3,2,1,0:T(8,128)(2,1)S(1)} collective-permute-done((bf16[2,4,48,384]{3,2,1,0:T(8,128)(2,1)S(1)}, bf16[2,4,48,384]{3,2,1,0:T(8,128)(2,1)S(1)}, u32[]{:S(2)}, u32[]{:S(2)}) %collective-permute-start.89) | collective-permute-done | bytes 294944 | tf_op jit(solution)/shard_map/ppermute | solution.py:21
  595.8 4.2 collective-permute-start.92
  (679 shorter events, 326.8 us)
Async XLA Ops:
  7.2 105.4 %all-gather.5.cloned.1.call-start = ((), (), s32[]{:S(2)}) async-start(), calls=%async_computation.4 | async-start | bytes 6635520 | tf_op jit(solution)/shard_map/all_gather | solution.py:704
  10.6 217.0 %all-gather.7.cloned.1.call-start = ((), (), s32[]{:S(2)}) async-start(), calls=%async_computation.5 | async-start | bytes 5898240 | tf_op jit(solution)/shard_map/all_gather | solution.py:733
  16.5 39.3 %collective-permute-start = (bf16[2,192]{1,0:T(2,128)(2,1)S(1)}, bf16[2,192]{1,0:T(2,128)(2,1)S(1)}, u32[]{:S(2)}, u32[]{:S(2)}) collective-permute-start(bf16[2,192]{1,0:T(2,128)(2,1)S(1)} %get-tuple-element.152), channel_id=1, source_target_pairs={{0,8},{8,0},{16,24},{24,16},{1,9},{9,1},{17,25},{25,17},{2,10},{10... | collective-permute-start | bytes 2312 | tf_op jit(solution)/shard_map/ppermute | solution.py:21
  17.1 39.3 %collective-permute-start.1 = (bf16[2,192]{1,0:T(2,128)(2,1)S(1)}, bf16[2,192]{1,0:T(2,128)(2,1)S(1)}, u32[]{:S(2)}, u32[]{:S(2)}) collective-permute-start(bf16[2,192]{1,0:T(2,128)(2,1)S(1)} %get-tuple-element.152), channel_id=1, source_target_pairs={{0,16},{8,24},{16,0},{24,8},{1,17},{9,25},{17,1},{25,9},{2,18},{10... | collective-permute-start | bytes 2312 | tf_op jit(solution)/shard_map/ppermute | solution.py:21
  54.8 26.6 %collective-permute-start.42 = (bf16[384,1536]{1,0:T(8,128)(2,1)}, bf16[384,1536]{1,0:T(8,128)(2,1)}, u32[]{:S(2)}, u32[]{:S(2)}) collective-permute-start(bf16[384,1536]{1,0:T(8,128)(2,1)} %bitcast.99), channel_id=1, source_target_pairs={{0,8},{8,0},{16,24},{24,16},{1,9},{9,1},{17,25},{25,17},{2,10},{10... | collective-permute-start | bytes 3538952 | tf_op jit(solution)/shard_map/ppermute | solution.py:21
  55.5 28.5 %collective-permute-start.43 = (bf16[384,1536]{1,0:T(8,128)(2,1)}, bf16[384,1536]{1,0:T(8,128)(2,1)}, u32[]{:S(2)}, u32[]{:S(2)}) collective-permute-start(bf16[384,1536]{1,0:T(8,128)(2,1)} %bitcast.99), channel_id=1, source_target_pairs={{0,16},{8,24},{16,0},{24,8},{1,17},{9,25},{17,1},{25,9},{2,18},{10... | collective-permute-start | bytes 3538952 | tf_op jit(solution)/shard_map/ppermute | solution.py:21
  64.6 493.0 %reduce-scatter.5.cloned.1.call-start = ((), (), s32[]{:S(2)}) async-start(), calls=%async_computation.3 | async-start | bytes 5898240 | tf_op jit(solution)/shard_map/reduce_scatter | solution.py:804
  83.4 33.8 %collective-permute-start.44 = (bf16[192,1536]{1,0:T(8,128)(2,1)}, bf16[192,1536]{1,0:T(8,128)(2,1)}, u32[]{:S(2)}, u32[]{:S(2)}) collective-permute-start(bf16[192,1536]{1,0:T(8,128)(2,1)} %slice.933), channel_id=1, source_target_pairs={{0,16},{8,24},{16,0},{24,8},{1,17},{9,25},{17,1},{25,9},{2,18},{10... | collective-permute-start | bytes 1769480 | tf_op jit(solution)/shard_map/ppermute | solution.py:21
  85.8 31.4 %collective-permute-start.45 = (bf16[192,1536]{1,0:T(8,128)(2,1)}, bf16[192,1536]{1,0:T(8,128)(2,1)}, u32[]{:S(2)}, u32[]{:S(2)}) collective-permute-start(bf16[192,1536]{1,0:T(8,128)(2,1)} %slice.934), channel_id=1, source_target_pairs={{0,8},{8,0},{16,24},{24,16},{1,9},{9,1},{17,25},{25,17},{2,10},{10... | collective-permute-start | bytes 1769480 | tf_op jit(solution)/shard_map/ppermute | solution.py:21
  114.2 24.7 %collective-permute-start.13 = (bf16[192,1536]{1,0:T(8,128)(2,1)S(1)}, bf16[192,1536]{1,0:T(8,128)(2,1)S(1)}, u32[]{:S(2)}, u32[]{:S(2)}) collective-permute-start(bf16[192,1536]{1,0:T(8,128)(2,1)S(1)} %get-tuple-element.154), channel_id=1, source_target_pairs={{0,8},{8,0},{16,24},{24,16},{1,9},{9,1},{17,25},{25,17},{2,10},{10... | collective-permute-start | bytes 1769480 | tf_op jit(solution)/shard_map/ppermute | solution.py:21
  115.7 23.9 %collective-permute-start.14 = (bf16[192,1536]{1,0:T(8,128)(2,1)S(1)}, bf16[192,1536]{1,0:T(8,128)(2,1)S(1)}, u32[]{:S(2)}, u32[]{:S(2)}) collective-permute-start(bf16[192,1536]{1,0:T(8,128)(2,1)S(1)} %get-tuple-element.154), channel_id=1, source_target_pairs={{0,16},{8,24},{16,0},{24,8},{1,17},{9,25},{17,1},{25,9},{2,18},{10... | collective-permute-start | bytes 1769480 | tf_op jit(solution)/shard_map/ppermute | solution.py:21
  162.5 32.8 %collective-permute-start.20 = (bf16[128,384]{1,0:T(8,128)(2,1)S(1)}, bf16[128,384]{1,0:T(8,128)(2,1)S(1)}, u32[]{:S(2)}, u32[]{:S(2)}) collective-permute-start(bf16[128,384]{1,0:T(8,128)(2,1)S(1)} %get-tuple-element.279), channel_id=1, source_target_pairs={{0,2},{1,3},{2,0},{3,1},{4,6},{5,7},{6,4},{7,5},{8,10},{9,11},{10,... | collective-permute-start | bytes 294920 | tf_op jit(solution)/shard_map/ppermute | solution.py:26
  166.4 28.9 %collective-permute-start.21 = (bf16[128,384]{1,0:T(8,128)(2,1)S(1)}, bf16[128,384]{1,0:T(8,128)(2,1)S(1)}, u32[]{:S(2)}, u32[]{:S(2)}) collective-permute-start(bf16[128,384]{1,0:T(8,128)(2,1)S(1)} %get-tuple-element.278), channel_id=1, source_target_pairs={{0,3},{1,0},{2,1},{3,2},{4,7},{5,4},{6,5},{7,6},{8,11},{9,8},{10,9... | collective-permute-start | bytes 294920 | tf_op jit(solution)/shard_map/ppermute | solution.py:26
  201.1 34.0 %collective-permute-start.26 = (bf16[128,1536]{1,0:T(8,128)(2,1)}, bf16[128,1536]{1,0:T(8,128)(2,1)}, u32[]{:S(2)}, u32[]{:S(2)}) collective-permute-start(bf16[128,1536]{1,0:T(8,128)(2,1)} %get-tuple-element.146), channel_id=1, source_target_pairs={{0,8},{8,0},{16,24},{24,16},{1,9},{9,1},{17,25},{25,17},{2,10},{10... | collective-permute-start | bytes 1179656 | tf_op jit(solution)/shard_map/ppermute | solution.py:21
  202.2 36.4 %collective-permute-start.27 = (bf16[128,1536]{1,0:T(8,128)(2,1)}, bf16[128,1536]{1,0:T(8,128)(2,1)}, u32[]{:S(2)}, u32[]{:S(2)}) collective-permute-start(bf16[128,1536]{1,0:T(8,128)(2,1)} %get-tuple-element.146), channel_id=1, source_target_pairs={{0,16},{8,24},{16,0},{24,8},{1,17},{9,25},{17,1},{25,9},{2,18},{10... | collective-permute-start | bytes 1179656 | tf_op jit(solution)/shard_map/ppermute | solution.py:21
  208.3 32.4 %collective-permute-start.30 = (bf16[128,1536]{1,0:T(8,128)(2,1)}, bf16[128,1536]{1,0:T(8,128)(2,1)}, u32[]{:S(2)}, u32[]{:S(2)}) collective-permute-start(bf16[128,1536]{1,0:T(8,128)(2,1)} %get-tuple-element.148), channel_id=1, source_target_pairs={{0,8},{8,0},{16,24},{24,16},{1,9},{9,1},{17,25},{25,17},{2,10},{10... | collective-permute-start | bytes 1179656 | tf_op jit(solution)/shard_map/ppermute | solution.py:21
  208.9 33.4 %collective-permute-start.31 = (bf16[128,1536]{1,0:T(8,128)(2,1)}, bf16[128,1536]{1,0:T(8,128)(2,1)}, u32[]{:S(2)}, u32[]{:S(2)}) collective-permute-start(bf16[128,1536]{1,0:T(8,128)(2,1)} %get-tuple-element.148), channel_id=1, source_target_pairs={{0,16},{8,24},{16,0},{24,8},{1,17},{9,25},{17,1},{25,9},{2,18},{10... | collective-permute-start | bytes 1179656 | tf_op jit(solution)/shard_map/ppermute | solution.py:21
  238.6 24.6 %collective-permute-start.47 = (bf16[4,192,1536]{2,1,0:T(8,128)(2,1)S(1)}, bf16[4,192,1536]{2,1,0:T(8,128)(2,1)S(1)}, u32[]{:S(2)}, u32[]{:S(2)}) collective-permute-start(bf16[4,192,1536]{2,1,0:T(8,128)(2,1)S(1)} %bitcast.567), channel_id=1, source_target_pairs={{0,4},{4,0},{1,5},{5,1},{2,6},{6,2},{3,7},{7,3},{8,12},{12,8},{9,1... | collective-permute-start | bytes 7077896 | tf_op jit(solution)/shard_map/ppermute | solution.py:21
  240.7 22.8 %collective-permute-start.46 = (bf16[4,192,1536]{2,1,0:T(8,128)(2,1)S(1)}, bf16[4,192,1536]{2,1,0:T(8,128)(2,1)S(1)}, u32[]{:S(2)}, u32[]{:S(2)}) collective-permute-start(bf16[4,192,1536]{2,1,0:T(8,128)(2,1)S(1)} %bitcast.569), channel_id=1, source_target_pairs={{0,4},{4,0},{1,5},{5,1},{2,6},{6,2},{3,7},{7,3},{8,12},{12,8},{9,1... | collective-permute-start | bytes 7077896 | tf_op jit(solution)/shard_map/ppermute | solution.py:21
  328.1 35.1 %collective-permute-start.58 = (bf16[1536,1536]{1,0:T(8,128)(2,1)S(1)}, bf16[1536,1536]{1,0:T(8,128)(2,1)}, u32[]{:S(2)}, u32[]{:S(2)}) collective-permute-start(bf16[1536,1536]{1,0:T(8,128)(2,1)S(1)} %dynamic-slice_bitcast_fusion), channel_id=1, source_target_pairs={{0,4},{4,0},{1,5},{5,1},{2,6},{6,2},{3,7},{7,3},{8,12},{12,8},{9,1... | collective-permute-start | bytes 14155784 | tf_op jit(solution)/shard_map/ppermute | solution.py:21
  330.8 22.0 %collective-permute-start.52 = (bf16[2,64,1536]{2,1,0:T(8,128)(2,1)S(1)}, bf16[2,64,1536]{2,1,0:T(8,128)(2,1)S(1)}, u32[]{:S(2)}, u32[]{:S(2)}) collective-permute-start(bf16[2,64,1536]{2,1,0:T(8,128)(2,1)S(1)} %pad_maximum_fusion.19), channel_id=1, source_target_pairs={{0,16},{8,24},{16,0},{24,8},{1,17},{9,25},{17,1},{25,9},{2,18},{10... | collective-permute-start | bytes 1179656 | tf_op jit(solution)/shard_map/ppermute | solution.py:21
  332.2 24.5 %collective-permute-start.63 = (bf16[2,64,1536]{2,1,0:T(8,128)(2,1)S(1)}, bf16[2,64,1536]{2,1,0:T(8,128)(2,1)S(1)}, u32[]{:S(2)}, u32[]{:S(2)}) collective-permute-start(bf16[2,64,1536]{2,1,0:T(8,128)(2,1)S(1)} %pad_maximum_fusion.21), channel_id=1, source_target_pairs={{0,16},{8,24},{16,0},{24,8},{1,17},{9,25},{17,1},{25,9},{2,18},{10... | collective-permute-start | bytes 1179656 | tf_op jit(solution)/shard_map/ppermute | solution.py:21
  375.6 228.5 %reduce-scatter.3.cloned.1.call-start = ((), (), s32[]{:S(2)}) async-start(), calls=%async_computation.2 | async-start | bytes 6635520 | tf_op jit(solution)/shard_map/reduce_scatter | solution.py:799
  396.5 56.2 %collective-permute-start.69 = (bf16[128,384]{1,0:T(8,128)(2,1)S(1)}, bf16[128,384]{1,0:T(8,128)(2,1)S(1)}, u32[]{:S(2)}, u32[]{:S(2)}) collective-permute-start(bf16[128,384]{1,0:T(8,128)(2,1)S(1)} %get-tuple-element.250), channel_id=1, source_target_pairs={{0,1},{1,2},{2,3},{3,0},{4,5},{5,6},{6,7},{7,4},{8,9},{9,10},{10,1... | collective-permute-start | bytes 294920 | tf_op jit(solution)/shard_map/ppermute | solution.py:26
  397.1 57.0 %collective-permute-start.70 = (bf16[128,384]{1,0:T(8,128)(2,1)S(1)}, bf16[128,384]{1,0:T(8,128)(2,1)S(1)}, u32[]{:S(2)}, u32[]{:S(2)}) collective-permute-start(bf16[128,384]{1,0:T(8,128)(2,1)S(1)} %get-tuple-element.249), channel_id=1, source_target_pairs={{0,2},{1,3},{2,0},{3,1},{4,6},{5,7},{6,4},{7,5},{8,10},{9,11},{10,... | collective-permute-start | bytes 294920 | tf_op jit(solution)/shard_map/ppermute | solution.py:26
  404.9 49.2 %collective-permute-start.71 = (bf16[128,384]{1,0:T(8,128)(2,1)S(1)}, bf16[128,384]{1,0:T(8,128)(2,1)S(1)}, u32[]{:S(2)}, u32[]{:S(2)}) collective-permute-start(bf16[128,384]{1,0:T(8,128)(2,1)S(1)} %get-tuple-element.248), channel_id=1, source_target_pairs={{0,3},{1,0},{2,1},{3,2},{4,7},{5,4},{6,5},{7,6},{8,11},{9,8},{10,9... | collective-permute-start | bytes 294920 | tf_op jit(solution)/shard_map/ppermute | solution.py:26
  408.3 32.3 %collective-permute-start.66 = (bf16[128,384]{1,0:T(8,128)(2,1)S(1)}, bf16[128,384]{1,0:T(8,128)(2,1)S(1)}, u32[]{:S(2)}, u32[]{:S(2)}) collective-permute-start(bf16[128,384]{1,0:T(8,128)(2,1)S(1)} %get-tuple-element.257), channel_id=1, source_target_pairs={{0,2},{1,3},{2,0},{3,1},{4,6},{5,7},{6,4},{7,5},{8,10},{9,11},{10,... | collective-permute-start | bytes 294920 | tf_op jit(solution)/shard_map/ppermute | solution.py:26
  424.2 22.6 %collective-permute-start.67 = (bf16[128,384]{1,0:T(8,128)(2,1)S(1)}, bf16[128,384]{1,0:T(8,128)(2,1)S(1)}, u32[]{:S(2)}, u32[]{:S(2)}) collective-permute-start(bf16[128,384]{1,0:T(8,128)(2,1)S(1)} %get-tuple-element.256), channel_id=1, source_target_pairs={{0,3},{1,0},{2,1},{3,2},{4,7},{5,4},{6,5},{7,6},{8,11},{9,8},{10,9... | collective-permute-start | bytes 294920 | tf_op jit(solution)/shard_map/ppermute | solution.py:26
  440.6 27.8 %collective-permute-start.77 = (bf16[4,192,1536]{2,1,0:T(8,128)(2,1)S(1)}, bf16[4,192,1536]{2,1,0:T(8,128)(2,1)S(1)}, u32[]{:S(2)}, u32[]{:S(2)}) collective-permute-start(bf16[4,192,1536]{2,1,0:T(8,128)(2,1)S(1)} %dynamic-slice_bitcast_fusion.1), channel_id=1, source_target_pairs={{0,4},{4,0},{1,5},{5,1},{2,6},{6,2},{3,7},{7,3},{8,12},{12,8},{9,1... | collective-permute-start | bytes 7077896 | tf_op jit(solution)/shard_map/ppermute | solution.py:21
  502.7 26.3 %collective-permute-start.56 = (bf16[2,192,1536]{2,1,0:T(8,128)(2,1)S(1)}, bf16[2,192,1536]{2,1,0:T(8,128)(2,1)S(1)}, u32[]{:S(2)}, u32[]{:S(2)}) collective-permute-start(bf16[2,192,1536]{2,1,0:T(8,128)(2,1)S(1)} %pad_maximum_fusion.5), channel_id=1, source_target_pairs={{0,16},{8,24},{16,0},{24,8},{1,17},{9,25},{17,1},{25,9},{2,18},{10... | collective-permute-start | bytes 3538952 | tf_op jit(solution)/shard_map/ppermute | solution.py:21
  503.6 25.7 %collective-permute-start.54 = (bf16[2,192,1536]{2,1,0:T(8,128)(2,1)S(1)}, bf16[2,192,1536]{2,1,0:T(8,128)(2,1)S(1)}, u32[]{:S(2)}, u32[]{:S(2)}) collective-permute-start(bf16[2,192,1536]{2,1,0:T(8,128)(2,1)S(1)} %pad_maximum_fusion.4), channel_id=1, source_target_pairs={{0,8},{8,0},{16,24},{24,16},{1,9},{9,1},{17,25},{25,17},{2,10},{10... | collective-permute-start | bytes 3538952 | tf_op jit(solution)/shard_map/ppermute | solution.py:21
  514.1 39.3 %collective-permute-start.82 = (bf16[4,192,1152]{2,1,0:T(8,128)(2,1)}, bf16[4,192,1152]{2,1,0:T(8,128)(2,1)}, u32[]{:S(2)}, u32[]{:S(2)}) collective-permute-start(bf16[4,192,1152]{2,1,0:T(8,128)(2,1)} %dynamic-slice_bitcast_fusion.2), channel_id=1, source_target_pairs={{0,4},{4,0},{1,5},{5,1},{2,6},{6,2},{3,7},{7,3},{8,12},{12,8},{9,1... | collective-permute-start | bytes 5308424 | tf_op jit(solution)/shard_map/ppermute | solution.py:21
  (188 other events, 1696.0 us)
Sparse Core Ops, SparseCore 0:
  10.7 101.8 all-gather.4
  114.7 112.7 all-gather.6
  375.7 102.4 reduce-scatter.4
  500.7 103.2 reduce-scatter.2

commit v3 on v2

v3 whole, which is shorter than its diff:
```python
import functools

import jax
import jax.numpy as jnp
from jax import lax
from jax.experimental import pallas as pl
from jax.experimental.pallas import tpu as pltpu
from jax.sharding import PartitionSpec as P

HEAD = 128
LEVELS = 4
EPSILON = 1e-06
NEGATIVE = -1e30
BF = jnp.bfloat16
F32 = jnp.float32
MIB = 1 << 20
HURRY = 16


def flip(shard, axis, bit):
    devices = lax.axis_size(axis)
    return lax.ppermute(shard, axis, [(i, i ^ bit) for i in range(devices)])


def turn(shard, axis, by):
    devices = lax.axis_size(axis)
    return lax.ppermute(shard, axis, [(i, (i + by) % devices) for i in range(devices)])


def after(values, *others):
    return lax.optimization_barrier((values,) + others)[0]


def put(buffer, part, index, dim=0):
    starts = [0] * buffer.ndim
    starts[dim] = index
    return lax.dynamic_update_slice(buffer, jnp.expand_dims(part, dim), tuple(starts))


def take(buffer, index, dim=0):
    return lax.dynamic_index_in_dim(buffer, index, dim, keepdims=False)


def side_by_side(parts):
    return jnp.concatenate([parts[k] for k in range(parts.shape[0])], axis=-1)


def pack(part, width):
    rows, cols = part.shape
    return side_by_side(part.reshape(width // cols, -1, cols))


def unpack(packed, cols):
    strips = packed.shape[1] // cols
    return jnp.concatenate([packed[:, k * cols : (k + 1) * cols] for k in range(strips)], 0)


def rank_swap(parts):
    return [parts[0]] + [turn(parts[k], "mp", k) for k in range(1, len(parts))]


def level_pieces(part):
    half = part.shape[0] // 2
    from_x = flip(part, "dp", 1)
    from_y = flip(part, "dp", 2)
    return part, from_x, from_y, flip(from_x[:half], "dp", 2), flip(from_y[half:], "dp", 1)


def level_gather(part, mine):
    return level_join(level_pieces(part), mine)


def level_join(pieces, mine):
    part, from_x, from_y, low_half, high_half = pieces
    whole = put(jnp.zeros((LEVELS,) + part.shape, part.dtype), part, mine)
    whole = put(whole, from_x, mine ^ 1)
    whole = put(whole, from_y, mine ^ 2)
    return put(whole, jnp.concatenate([low_half, high_half], 0), mine ^ 3)


def level_gather_small(part, mine):
    whole = put(jnp.zeros((LEVELS,) + part.shape, part.dtype), part, mine)
    for k in range(1, LEVELS):
        whole = put(whole, flip(part, "dp", k), mine ^ k)
    return whole


def level_scatter_open(parts, mine):
    half = parts.shape[1] // 2
    own, by_x, by_y, by_xy = (take(parts, mine ^ k) for k in range(LEVELS))
    got_x = flip(jnp.stack([by_x[:half], by_xy[:half]]), "dp", 1)
    got_y = flip(jnp.stack([by_y[half:], by_xy[half:]]), "dp", 2)
    return own, by_x[half:], by_y[:half], got_x, got_y


def level_scatter_last(by_x, by_y, got_x, got_y):
    send_y = (by_y.astype(F32) + got_x[1].astype(F32)).astype(by_y.dtype)
    send_x = (by_x.astype(F32) + got_y[1].astype(F32)).astype(by_x.dtype)
    return flip(send_y, "dp", 2), flip(send_x, "dp", 1)


def level_scatter(parts, mine):
    opened = level_scatter_open(parts, mine)
    return level_sum(opened, level_scatter_last(*opened[1:]))


def level_sum(opened, last):
    own, _, by_y, got_x, got_y = opened
    last_y, last_x = last
    half = by_y.shape[0]
    first = own[:half].astype(F32) + got_x[0].astype(F32) + last_y.astype(F32)
    second = own[half:].astype(F32) + got_y[0].astype(F32) + last_x.astype(F32)
    return jnp.concatenate([first, second], 0)


def level_swap(parts, mine):
    whole = put(jnp.zeros(parts.shape, parts.dtype), take(parts, mine), mine)
    for k in range(1, LEVELS):
        whole = put(whole, flip(take(parts, mine ^ k), "dp", k), mine ^ k)
    return whole


def teams(devices):
    return [list(range(level, devices, LEVELS)) for level in range(LEVELS)]


def team_gather(part):
    devices = lax.axis_size("dp")
    if devices == LEVELS:
        return part[None]
    return lax.all_gather(part, "dp", axis=0, axis_index_groups=teams(devices))


def team_scatter(parts):
    devices = lax.axis_size("dp")
    if devices == LEVELS:
        return parts[0]
    return lax.psum_scatter(
        parts, "dp", scatter_dimension=0, axis_index_groups=teams(devices), tiled=False
    )


def pair_gather(part, mine, dim=0):
    other = flip(part, "ctx", 1)
    shape = part.shape[:dim] + (2,) + part.shape[dim:]
    return put(put(jnp.zeros(shape, part.dtype), part, mine, dim), other, 1 - mine, dim)


def pair_split(first, second, mine):
    own = jnp.where(mine == 0, first, second)
    return own, flip(jnp.where(mine == 0, second, first), "ctx", 1)


def pair_scatter(parts, mine, dim):
    other = flip(take(parts, 1 - mine, dim), "ctx", 1)
    return take(parts, mine, dim).astype(F32) + other.astype(F32)


def model_gather(part, level, ctx):
    rows, width = part.shape
    whole = team_gather(level_gather(part, level))
    whole = pair_gather(whole.reshape(-1, rows, width), ctx, 1)
    return whole.reshape(-1, width)


def model_scatter(grad, level, ctx, rows):
    width = grad.shape[1]
    parts = grad.reshape(-1, 2, rows, width)
    parts = pair_scatter(parts, ctx, 1).astype(grad.dtype)
    parts = team_scatter(parts.reshape(-1, LEVELS, rows, width))
    return level_scatter(parts, level)


def cost(flops, bytes_accessed, transcendentals):
    return pl.CostEstimate(
        flops=flops // HURRY,
        bytes_accessed=bytes_accessed // HURRY,
        transcendentals=transcendentals // HURRY,
    )


def contract(left, right, left_dim, right_dim):
    return lax.dot_general(
        left, right, (((left_dim,), (right_dim,)), ((), ())), preferred_element_type=F32
    )


def turned(values, cosine, sine):
    return values * cosine + pltpu.roll(values, HEAD // 2, 1) * sine


def project_kernel(rows_ref, gain_ref, weight_ref, cos_ref, sin_ref, out_ref, normed_ref):
    @pl.when(pl.program_id(1) == 0)
    def _():
        values = rows_ref[...].reshape(normed_ref.shape).astype(F32)
        inv = lax.rsqrt(jnp.mean(values * values, axis=-1, keepdims=True) + EPSILON)
        normed_ref[...] = (values * inv * gain_ref[...]).astype(BF)

    values = contract(normed_ref[...], weight_ref[...], 1, 0)
    cosine, sine = cos_ref[0], sin_ref[0]
    for head in range(values.shape[1] // HEAD):
        cols = slice(head * HEAD, (head + 1) * HEAD)
        out_ref[0, :, cols] = turned(values[:, cols], cosine, sine).astype(BF)


def project(count, shard_len, rows, gain, weight, cosine, sine):
    ranks, _, width = rows.shape
    length = ranks * shard_len
    cols = weight.shape[1] // 3
    table = pl.BlockSpec((1, length, HEAD), lambda i, j: (j // 2, 0, 0))
    return pl.pallas_call(
        project_kernel,
        grid=(count, 3),
        in_specs=[
            pl.BlockSpec((ranks, shard_len, width), lambda i, j: (0, i, 0)),
            pl.BlockSpec((1, width), lambda i, j: (0, 0)),
            pl.BlockSpec((width, cols), lambda i, j: (0, j)),
            table,
            table,
        ],
        out_specs=[
            pl.BlockSpec((1, length, cols), lambda i, j: (j, i, 0)),
            pl.BlockSpec((length, width), lambda i, j: (i, 0)),
        ],
        out_shape=[
            jax.ShapeDtypeStruct((3, count * length, cols), BF),
            jax.ShapeDtypeStruct((count * length, width), BF),
        ],
        compiler_params=pltpu.CompilerParams(vmem_limit_bytes=24 * MIB),
        cost_estimate=cost(
            flops=6 * length * width * cols,
            bytes_accessed=4 * length * width + 6 * width * cols + 6 * length * cols,
            transcendentals=0,
        ),
        name="project",
    )(rows, gain, weight, cosine, sine)


def softmax_parts(query, key_own, key_early, first, late):
    factor = HEAD ** (-0.5)
    own = contract(query, key_own, 1, 1) * factor
    row_ids = first + lax.broadcasted_iota(jnp.int32, own.shape, 0)
    col_ids = lax.broadcasted_iota(jnp.int32, own.shape, 1)
    own = jnp.where(col_ids <= row_ids, own, NEGATIVE)
    early = contract(query, key_early, 1, 1) * factor if late else None
    return own, early


def attend_kernel(strip, place_ref, query_ref, key_ref, value_ref, early_ref, *refs):
    *part_refs, log_ref, mixed_ref = refs
    length = query_ref.shape[1]
    ranks = len(part_refs)
    shard_len = length // ranks

    def run(late):
        for first in range(0, length, strip):
            end = first + strip
            own, early = softmax_parts(
                query_ref[0, first:end], key_ref[0, :end], early_ref[0], first, late
            )
            largest = jnp.max(own, axis=-1, keepdims=True)
            if late:
                largest = jnp.maximum(largest, jnp.max(early, axis=-1, keepdims=True))
            own = jnp.exp(own - largest)
            total = jnp.sum(own, axis=-1, keepdims=True)
            if late:
                early = jnp.exp(early - largest)
                total = total + jnp.sum(early, axis=-1, keepdims=True)
            inverse = 1.0 / total
            mixed = contract((own * inverse).astype(BF), value_ref[0, :end], 1, 0)
            if late:
                mixed = mixed + contract((early * inverse).astype(BF), early_ref[1], 1, 0)
            mixed_ref[first:end] = mixed.astype(BF)
            log_ref[0, first:end] = largest + jnp.log(total)

    @pl.when(place_ref[0] == 0)
    def _():
        run(False)

    @pl.when(place_ref[0] != 0)
    def _():
        run(True)

    for k, part_ref in enumerate(part_refs):
        target = lax.rem(place_ref[1] + k, ranks)
        part_ref[...] = mixed_ref[pl.ds(pl.multiple_of(target * shard_len, shard_len), shard_len)]


def attend(place, ranks, length, qkv, early):
    _, rows, cols = qkv.shape
    count = rows // length
    heads = cols // HEAD
    shard_len = length // ranks
    one = lambda which: pl.BlockSpec((1, length, HEAD), lambda i, h, p: (which, i, h))
    part = pl.BlockSpec((shard_len, HEAD), lambda i, h, p: (i, h))
    *parts, logs = pl.pallas_call(
        functools.partial(attend_kernel, length // 2),
        grid_spec=pltpu.PrefetchScalarGridSpec(
            num_scalar_prefetch=1,
            grid=(count, heads),
            in_specs=[
                one(0),
                one(1),
                one(2),
                pl.BlockSpec((2, length, HEAD), lambda i, h, p: (0, i, h)),
            ],
            out_specs=[part] * ranks + [pl.BlockSpec((1, length, 1), lambda i, h, p: (i * heads + h, 0, 0))],
            scratch_shapes=[pltpu.VMEM((length, HEAD), BF)],
        ),
        out_shape=[jax.ShapeDtypeStruct((count * shard_len, cols), BF)] * ranks
        + [jax.ShapeDtypeStruct((count * heads, length, 1), F32)],
        compiler_params=pltpu.CompilerParams(vmem_limit_bytes=24 * MIB),
        cost_estimate=cost(
            flops=8 * length * length * cols,
            bytes_accessed=14 * length * cols,
            transcendentals=2 * length * length * heads,
        ),
        name="attend",
    )(place, qkv, qkv, qkv, early)
    return parts, logs


def hidden_kernel(ranks, place_ref, input_ref, gain_ref, weight_ref, *refs):
    part_refs, (hidden_ref, normed_ref, mixed_ref) = refs[:ranks], refs[ranks:]
    cols = part_refs[0].shape[1]
    hidden = input_ref[...].astype(F32)
    for k, part_ref in enumerate(part_refs):
        source = lax.rem(place_ref[1] + ranks - k, ranks)
        where = pl.ds(pl.multiple_of(source * cols, HEAD), cols)
        hidden = hidden + contract(part_ref[...], weight_ref[:, where], 1, 1)
        mixed_ref[:, where] = part_ref[...]
    hidden_ref[...] = hidden
    inv = lax.rsqrt(jnp.mean(hidden * hidden, axis=-1, keepdims=True) + EPSILON)
    normed_ref[...] = (hidden * inv * gain_ref[...]).astype(BF)


def finish_attention(place, inputs, gain, weight, parts):
    shard_len, width = inputs.shape
    ranks, cols = len(parts), parts[0].shape[1]
    whole = lambda shape: pl.BlockSpec(shape, lambda j, p: (0,) * len(shape))
    return pl.pallas_call(
        functools.partial(hidden_kernel, ranks),
        grid_spec=pltpu.PrefetchScalarGridSpec(
            num_scalar_prefetch=1,
            grid=(1,),
            in_specs=[
                whole((shard_len, width)),
                whole((1, width)),
                whole(weight.shape),
            ]
            + [whole((shard_len, cols))] * ranks,
            out_specs=[
                whole((shard_len, width)),
                whole((shard_len, width)),
                whole((shard_len, ranks * cols)),
            ],
        ),
        out_shape=[
            jax.ShapeDtypeStruct((shard_len, width), F32),
            jax.ShapeDtypeStruct((shard_len, width), BF),
            jax.ShapeDtypeStruct((shard_len, ranks * cols), BF),
        ],
        compiler_params=pltpu.CompilerParams(vmem_limit_bytes=40 * MIB),
        cost_estimate=cost(
            flops=2 * shard_len * width * width,
            bytes_accessed=2 * width * width + 12 * shard_len * width,
            transcendentals=0,
        ),
        name="finish_attention",
    )(place, inputs, gain, weight, *parts)


def grad_hidden_kernel(
    ranks,
    place_ref,
    own_ref,
    got_x_ref,
    last_y_ref,
    got_y_ref,
    last_x_ref,
    hidden_ref,
    cot_ref,
    gain_ref,
    weight_ref,
    grad_ref,
    low_ref,
    *part_refs,
):
    half = last_y_ref.shape[0]
    cols = part_refs[0].shape[1]
    for rows, got_ref, last_ref in (
        (slice(0, half), got_x_ref, last_y_ref),
        (slice(half, 2 * half), got_y_ref, last_x_ref),
    ):
        weighted = own_ref[rows].astype(F32) + got_ref[0].astype(F32) + last_ref[...].astype(F32)
        weighted = weighted * gain_ref[...]
        values = hidden_ref[rows]
        inv = lax.rsqrt(jnp.mean(values * values, axis=-1, keepdims=True) + EPSILON)
        inner = jnp.mean(weighted * values, axis=-1, keepdims=True)
        grad = inv * weighted - values * (inv * inv * inv * inner) + cot_ref[rows].astype(F32)
        grad_ref[rows] = grad
        low_ref[rows] = grad.astype(BF)
    for k, part_ref in enumerate(part_refs):
        target = lax.rem(place_ref[1] + k, ranks)
        where = pl.ds(pl.multiple_of(target * cols, HEAD), cols)
        part_ref[...] = contract(low_ref[...], weight_ref[:, where], 1, 0).astype(BF)


def begin_back(place, ranks, pieces, hidden, cotangent, gain, weight):
    shard_len, width = hidden.shape
    cols = weight.shape[1] // ranks
    half = shard_len // 2
    whole = lambda shape: pl.BlockSpec(shape, lambda j, p: (0,) * len(shape))
    first = pl.BlockSpec((1, half, width), lambda j, p: (0, 0, 0))
    grad, low, *parts = pl.pallas_call(
        functools.partial(grad_hidden_kernel, ranks),
        grid_spec=pltpu.PrefetchScalarGridSpec(
            num_scalar_prefetch=1,
            grid=(1,),
            in_specs=[
                whole((shard_len, width)),
                first,
                whole((half, width)),
                first,
                whole((half, width)),
                whole((shard_len, width)),
                whole((shard_len, width)),
                whole((1, width)),
                whole(weight.shape),
            ],
            out_specs=[whole((shard_len, width))] * 2 + [whole((shard_len, cols))] * ranks,
        ),
        out_shape=[
            jax.ShapeDtypeStruct((shard_len, width), F32),
            jax.ShapeDtypeStruct((shard_len, width), BF),
        ]
        + [jax.ShapeDtypeStruct((shard_len, cols), BF)] * ranks,
        compiler_params=pltpu.CompilerParams(vmem_limit_bytes=48 * MIB),
        cost_estimate=cost(
            flops=2 * shard_len * width * width,
            bytes_accessed=2 * width * width + 20 * shard_len * width,
            transcendentals=0,
        ),
        name="begin_back",
    )(place, *pieces, hidden, cotangent, gain, weight)
    return grad, low, parts


def attend_back_kernel(
    strip, place_ref, query_ref, key_ref, value_ref, early_ref, log_ref, cos_ref, sin_ref, *refs
):
    *part_refs, query_out, own_out, early_out, grad_ref = refs
    length = query_ref.shape[1]
    factor = HEAD ** (-0.5)
    ranks = len(part_refs)
    shard_len = length // ranks
    for k, part_ref in enumerate(part_refs):
        source = lax.rem(place_ref[1] + ranks - k, ranks)
        grad_ref[pl.ds(pl.multiple_of(source * shard_len, shard_len), shard_len)] = part_ref[...]

    def run(late):
        early_key_sum = early_value_sum = 0.0
        for first in range(length - strip, -1, -strip):
            end = first + strip
            query = query_ref[0, first:end]
            grad = grad_ref[first:end]
            log = log_ref[0, first:end]
            own, early = softmax_parts(query, key_ref[0, :end], early_ref[0], first, late)
            own = jnp.exp(own - log)
            own_grad = contract(grad, value_ref[0, :end], 1, 1)
            inner = jnp.sum(own_grad * own, axis=-1, keepdims=True)
            if late:
                early = jnp.exp(early - log)
                early_grad = contract(grad, early_ref[1], 1, 1)
                inner = inner + jnp.sum(early_grad * early, axis=-1, keepdims=True)
            own_low = (own * (own_grad - inner)).astype(BF)
            grad_query = contract(own_low, key_ref[0, :end], 1, 0)
            grad_key = contract(own_low, query, 0, 0) * factor
            grad_value = contract(own.astype(BF), grad, 0, 0)
            if first == length - strip:
                own_out[0] = grad_key
                own_out[1] = grad_value
            else:
                own_out[0, :end] += grad_key
                own_out[1, :end] += grad_value
            if late:
                early_low = (early * (early_grad - inner)).astype(BF)
                grad_query = grad_query + contract(early_low, early_ref[0], 1, 0)
                early_key_sum = early_key_sum + contract(early_low, query, 0, 0)
                early_value_sum = early_value_sum + contract(early.astype(BF), grad, 0, 0)
            grad_query = grad_query * factor
            query_out[first:end] = turned(
                grad_query, cos_ref[0, first:end], -sin_ref[0, first:end]
            ).astype(BF)
        if late:
            early_out[0] = (early_key_sum * factor).astype(BF)
            early_out[1] = early_value_sum.astype(BF)
        else:
            early_out[...] = jnp.zeros(early_out.shape, BF)

    @pl.when(place_ref[0] == 0)
    def _():
        run(False)

    @pl.when(place_ref[0] != 0)
    def _():
        run(True)


def attend_back(place, length, qkv, early, logs, parts, cosine, sine):
    _, rows, cols = qkv.shape
    count = rows // length
    heads, ranks = cols // HEAD, len(parts)
    one = lambda which: pl.BlockSpec((1, length, HEAD), lambda i, h, p: (which, i, h))
    pair = pl.BlockSpec((2, length, HEAD), lambda i, h, p: (0, i, h))
    table = pl.BlockSpec((1, length, HEAD), lambda i, h, p: (0, 0, 0))
    return pl.pallas_call(
        functools.partial(attend_back_kernel, length // 2),
        grid_spec=pltpu.PrefetchScalarGridSpec(
            num_scalar_prefetch=1,
            grid=(count, heads),
            in_specs=[
                one(0),
                one(1),
                one(2),
                pair,
                pl.BlockSpec((1, length, 1), lambda i, h, p: (i * heads + h, 0, 0)),
                table,
                table,
            ]
            + [pl.BlockSpec((length // ranks, HEAD), lambda i, h, p: (i, h))] * ranks,
            out_specs=[pl.BlockSpec((length, HEAD), lambda i, h, p: (i, h)), pair, pair],
            scratch_shapes=[pltpu.VMEM((length, HEAD), BF)],
        ),
        out_shape=[
            jax.ShapeDtypeStruct((rows, cols), BF),
            jax.ShapeDtypeStruct((2, rows, cols), F32),
            jax.ShapeDtypeStruct((2, rows, cols), BF),
        ],
        compiler_params=pltpu.CompilerParams(vmem_limit_bytes=32 * MIB),
        cost_estimate=cost(
            flops=20 * length * length * cols,
            bytes_accessed=28 * length * cols,
            transcendentals=2 * length * length * heads,
        ),
        name="attend_back",
    )(place, qkv, qkv, qkv, early, logs, cosine, sine, *parts)


def project_back_kernel(
    query_ref, own_ref, back_ref, cos_ref, sin_ref, weight_ref, low_ref, out_ref
):
    cols = query_ref.shape[1]

    @pl.when(pl.program_id(1) == 0)
    def _():
        low_ref[:, :cols] = query_ref[...]
        keys = own_ref[0] + back_ref[0].astype(F32)
        cosine, sine = cos_ref[0], -sin_ref[0]
        for head in range(cols // HEAD):
            part = slice(head * HEAD, (head + 1) * HEAD)
            into = slice(cols + head * HEAD, cols + (head + 1) * HEAD)
            low_ref[:, into] = turned(keys[:, part], cosine, sine).astype(BF)
        low_ref[:, 2 * cols :] = (own_ref[1] + back_ref[1].astype(F32)).astype(BF)

    result = contract(low_ref[...], weight_ref[...], 1, 1).astype(BF)
    out_ref[...] = result.reshape(out_ref.shape)


def project_back(count, ranks, grad_query, grad_own, back, cosine, sine, weight):
    rows, cols = grad_query.shape
    length = rows // count
    width = weight.shape[0]
    step = width // 3
    pair = pl.BlockSpec((2, length, cols), lambda i, j: (0, i, 0))
    table = pl.BlockSpec((1, length, HEAD), lambda i, j: (0, 0, 0))
    return pl.pallas_call(
        project_back_kernel,
        grid=(count, 3),
        in_specs=[
            pl.BlockSpec((length, cols), lambda i, j: (i, 0)),
            pair,
            pair,
            table,
            table,
            pl.BlockSpec((step, 3 * cols), lambda i, j: (j, 0)),
        ],
        out_specs=[
            pl.BlockSpec((length, 3 * cols), lambda i, j: (i, 0)),
            pl.BlockSpec((ranks, 1, length // ranks, step), lambda i, j: (0, i, 0, j)),
        ],
        out_shape=[
            jax.ShapeDtypeStruct((rows, 3 * cols), BF),
            jax.ShapeDtypeStruct((ranks, count, length // ranks, width), BF),
        ],
        compiler_params=pltpu.CompilerParams(vmem_limit_bytes=32 * MIB),
        cost_estimate=cost(
            flops=6 * rows * width * cols,
            bytes_accessed=6 * width * cols + 18 * rows * cols + 2 * rows * width,
            transcendentals=0,
        ),
        name="project_back",
    )(grad_query, grad_own, back, cosine, sine, weight)


def gelu_both(values):
    scale = (2.0 / jnp.pi) ** 0.5
    square = values * values
    tanh = jnp.tanh(scale * values * (1.0 + 0.044715 * square))
    half = 0.5 * (1.0 + tanh)
    slope = half + 0.5 * values * (1.0 - tanh * tanh) * scale * (1.0 + 3 * 0.044715 * square)
    return values * half, slope


def stack_units(first, own_ref, other_ref, which, into):
    ranks, _, blocks, sub, _ = own_ref.shape

    def fill(source):
        for block in range(blocks):
            for rank in range(ranks):
                row = (block * ranks + rank) * sub
                into[row : row + sub] = source[rank, which, block]

    @pl.when(first)
    def _():
        fill(own_ref)

    @pl.when(jnp.logical_not(first))
    def _():
        fill(other_ref)


def feed_kernel(count, place_ref, cot_ref, own_ref, other_ref, *refs):
    rows_in, refs = refs[: 5 * count], refs[5 * count :]
    grads_out, (rows_ref, down_ref, act_ref, pre_ref, up_ref, sum_ref) = (
        refs[: 5 * count],
        refs[5 * count :],
    )
    step = pl.program_id(0)
    half = up_ref.shape[0]
    shard_len = rows_ref.shape[1] // count
    part = shard_len // 2
    ctx, mine = place_ref[0], place_ref[2]

    for turn_of, at in ((0, 0), (1, LEVELS)):

        @pl.when(step == at)
        def _(turn_of=turn_of):
            stack_units(ctx == turn_of, own_ref, other_ref, 0, up_ref)
            stack_units(ctx == turn_of, own_ref, other_ref, 1, down_ref.at[0])

    for k in range(LEVELS):

        @pl.when((step < LEVELS) & (jnp.bitwise_xor(mine, k) == step))
        def _(k=k):
            for i in range(count):
                pieces = rows_in[5 * i : 5 * i + 5]
                rows = slice(i * shard_len, (i + 1) * shard_len)
                if k < LEVELS - 1:
                    rows_ref[0, rows] = pieces[k][...]
                else:
                    rows_ref[0, rows.start : rows.start + part] = pieces[3][...]
                    rows_ref[0, rows.start + part : rows.stop] = pieces[4][...]

    def run(used):
        upped = contract(rows_ref[0], up_ref[:used], 1, 1)
        activated, slope = gelu_both(upped)
        grad_act = contract(cot_ref[0], down_ref[0, :used], 1, 1)
        grad_upped = (grad_act * slope).astype(BF)
        act_ref[0, :, :used] = activated.astype(BF)
        pre_ref[0, :, :used] = grad_upped
        return contract(grad_upped, up_ref[:used], 1, 0)

    for one in range(LEVELS - 1):

        @pl.when(step == one)
        def _(one=one):
            sum_ref[...] = run(half // 2 ** (LEVELS - 2 - one))

    @pl.when(step == LEVELS - 1)
    def _():
        sum_ref[...] = run(half)

    @pl.when(step == LEVELS)
    def _():
        sum_ref[...] += run(half)

    level = jnp.minimum(step, LEVELS - 1)
    for k in range(LEVELS):

        @pl.when((step != LEVELS - 1) & (jnp.bitwise_xor(mine, k) == level))
        def _(k=k):
            for i in range(count):
                keep, keep_x, keep_y, send_x, send_y = grads_out[5 * i : 5 * i + 5]
                first = sum_ref[i * shard_len : i * shard_len + part].astype(BF)
                second = sum_ref[i * shard_len + part : (i + 1) * shard_len].astype(BF)
                if k == 0:
                    keep[:part] = first
                    keep[part:] = second
                elif k == 1:
                    send_x[0] = first
                    keep_x[...] = second
                elif k == 2:
                    keep_y[...] = first
                    send_y[0] = second
                else:
                    send_x[1] = first
                    send_y[1] = second


def feed(place, rows, cot, own, other):
    count = len(rows)
    _, length, width = cot.shape
    half = own.shape[0] * own.shape[2] * own.shape[3]
    shard_len = length // count
    part = shard_len // 2
    whole = lambda shape: pl.BlockSpec(
        shape, lambda s, p: (0,) * len(shape), pipeline_mode=pl.Buffered(1)
    )
    fixed = lambda shape: pl.BlockSpec(shape, lambda s, p: (0,) * len(shape))
    by_level = pl.BlockSpec((1, length, width), lambda s, p: (jnp.minimum(s, LEVELS - 1), 0, 0))
    by_half = pl.BlockSpec((1, half, width), lambda s, p: (s // LEVELS, 0, 0))
    by_step = pl.BlockSpec((1, length, half), lambda s, p: (s, 0, 0))
    pieces = [
        (shard_len, width),
        (part, width),
        (part, width),
        (2, part, width),
        (2, part, width),
    ]
    *grads, rows_all, down, activated, before = pl.pallas_call(
        functools.partial(feed_kernel, count),
        grid_spec=pltpu.PrefetchScalarGridSpec(
            num_scalar_prefetch=1,
            grid=(LEVELS + 1,),
            in_specs=[by_level, whole(own.shape), whole(own.shape)]
            + [whole(piece.shape) for one in rows for piece in one],
            out_specs=[fixed(shape) for shape in pieces] * count
            + [by_level, by_half, by_step, by_step],
            scratch_shapes=[pltpu.VMEM((half, width), BF), pltpu.VMEM((length, width), F32)],
        ),
        out_shape=[jax.ShapeDtypeStruct(shape, BF) for shape in pieces] * count
        + [
            jax.ShapeDtypeStruct(cot.shape, BF),
            jax.ShapeDtypeStruct((2, half, width), BF),
            jax.ShapeDtypeStruct((LEVELS + 1, length, half), BF),
            jax.ShapeDtypeStruct((LEVELS + 1, length, half), BF),
        ],
        compiler_params=pltpu.CompilerParams(vmem_limit_bytes=58 * MIB),
        cost_estimate=cost(
            flops=24 * length * width * half,
            bytes_accessed=24 * length * width + 8 * half * width + 20 * length * half,
            transcendentals=5 * length * half,
        ),
        name="feed",
    )(place, cot, own, other, *[piece for one in rows for piece in one])
    grads = [grads[5 * i : 5 * i + 5] for i in range(count)]
    return grads, rows_all, down, activated, before


def feed_weights_kernel(
    place_ref,
    rows_ref,
    cot_ref,
    act_ref,
    pre_ref,
    down_ref,
    keep_ref,
    send_ref,
    out_ref,
    up_sum,
    down_sum,
    out_sum,
    stage,
    sem,
):
    step = pl.program_id(0)
    half = down_ref.shape[1]
    ranks, _, blocks, sub, _ = stage.shape

    def add(used, fresh):
        up_part = contract(pre_ref[0, :, :used], rows_ref[0], 0, 0)
        down_part = contract(act_ref[0, :, :used], cot_ref[0], 0, 0)
        if fresh == used:
            up_sum[:used] = up_part
            down_sum[:used] = down_part
        else:
            up_sum[:fresh] += up_part[:fresh]
            down_sum[:fresh] += down_part[:fresh]
            if fresh < used:
                up_sum[fresh:used] = up_part[fresh:]
                down_sum[fresh:used] = down_part[fresh:]
        return contract(act_ref[0, :, :used], down_ref[0, :used], 1, 0)

    def store(which):
        for block in range(blocks):
            for rank in range(ranks):
                first = (block * ranks + rank) * sub
                stage[rank, 0, block] = up_sum[first : first + sub].astype(BF)
                stage[rank, 1, block] = down_sum[first : first + sub].astype(BF)

        @pl.when(place_ref[0] == which)
        def _():
            copy = pltpu.make_async_copy(stage, keep_ref, sem)
            copy.start()
            copy.wait()

        @pl.when(place_ref[0] != which)
        def _():
            copy = pltpu.make_async_copy(stage, send_ref, sem)
            copy.start()
            copy.wait()

    for one in range(LEVELS - 1):

        @pl.when(step == one)
        def _(one=one):
            used = half // 2 ** (LEVELS - 2 - one)
            out_ref[0] = add(used, used if one == 0 else used // 2).astype(BF)

    @pl.when(step == LEVELS - 1)
    def _():
        up_sum[...] += contract(pre_ref[0], rows_ref[0], 0, 0)
        down_sum[...] += contract(act_ref[0], cot_ref[0], 0, 0)
        out_sum[...] = contract(act_ref[0], down_ref[0], 1, 0)
        store(0)

    @pl.when(step == LEVELS)
    def _():
        out_ref[0] = (out_sum[...] + add(half, half)).astype(BF)
        store(1)


def feed_weights(place, rows, cot, activated, before, down, ranks, blocks):
    _, length, width = rows.shape
    half = down.shape[1]
    sub = half // (ranks * blocks)
    by_level = pl.BlockSpec((1, length, width), lambda s, p: (jnp.minimum(s, LEVELS - 1), 0, 0))
    by_half = pl.BlockSpec((1, half, width), lambda s, p: (s // LEVELS, 0, 0))
    by_step = pl.BlockSpec((1, length, half), lambda s, p: (s, 0, 0))
    shape = (ranks, 2, blocks, sub, width)
    return pl.pallas_call(
        feed_weights_kernel,
        grid_spec=pltpu.PrefetchScalarGridSpec(
            num_scalar_prefetch=1,
            grid=(LEVELS + 1,),
            in_specs=[by_level, by_level, by_step, by_step, by_half],
            out_specs=[
                pl.BlockSpec(memory_space=pl.ANY),
                pl.BlockSpec(memory_space=pl.ANY),
                by_level,
            ],
            scratch_shapes=[
                pltpu.VMEM((half, width), F32),
                pltpu.VMEM((half, width), F32),
                pltpu.VMEM((length, width), F32),
                pltpu.VMEM(shape, BF),
                pltpu.SemaphoreType.DMA(()),
            ],
        ),
        out_shape=[
            jax.ShapeDtypeStruct(shape, BF),
            jax.ShapeDtypeStruct(shape, BF),
            jax.ShapeDtypeStruct(rows.shape, BF),
        ],
        compiler_params=pltpu.CompilerParams(vmem_limit_bytes=56 * MIB),
        cost_estimate=cost(
            flops=24 * length * width * half,
            bytes_accessed=24 * length * width + 12 * half * width + 20 * length * half,
            transcendentals=0,
        ),
        name="feed_weights",
    )(place, rows, cot, activated, before, down)


def outer_kernel(count, *refs):
    lefts, rights, out_ref = refs[:count], refs[count : 2 * count], refs[-1]
    total = contract(lefts[0][...], rights[0][...], 0, 0)
    for left, right in zip(lefts[1:], rights[1:]):
        total = total + contract(left[...], right[...], 0, 0)
    out_ref[...] = total.astype(BF)


def outer(lefts, rights):
    rows, m = lefts[0].shape
    n = rights[0].shape[1]
    count = len(lefts)
    step = m // 4
    return pl.pallas_call(
        functools.partial(outer_kernel, count),
        grid=(4,),
        in_specs=[pl.BlockSpec((rows, step), lambda j: (0, j))] * count
        + [pl.BlockSpec((rows, n), lambda j: (0, 0))] * count,
        out_specs=pl.BlockSpec((step, n), lambda j: (j, 0)),
        out_shape=jax.ShapeDtypeStruct((m, n), BF),
        compiler_params=pltpu.CompilerParams(vmem_limit_bytes=32 * MIB),
        cost_estimate=cost(
            flops=2 * count * rows * m * n,
            bytes_accessed=2 * (count * rows * (m + n) + m * n),
            transcendentals=0,
        ),
        name="outer",
    )(*lefts, *rights)


def inverse_rms(values):
    return lax.rsqrt(jnp.mean(values * values, axis=-1, keepdims=True) + EPSILON)


def norm_back(values, inv_rms, weighted):
    return inv_rms * weighted - values * (inv_rms * inv_rms * inv_rms) * jnp.mean(
        weighted * values, axis=-1, keepdims=True
    )


def rotation(positions, head_size):
    half_size = head_size // 2
    frequency = 10000.0 ** (-jnp.arange(half_size, dtype=jnp.float32) / half_size)
    angles = positions.astype(jnp.float32)[:, None] * frequency[None, :]
    cosine, sine = jnp.cos(angles), jnp.sin(angles)
    cosine = jnp.concatenate([cosine, cosine], -1)
    sine = jnp.concatenate([-sine, sine], -1)
    return (
        jnp.stack([cosine, jnp.ones_like(cosine)]),
        jnp.stack([sine, jnp.zeros_like(sine)]),
    )


def product(equation, left, right):
    return jnp.einsum(equation, left, right, preferred_element_type=F32)


def local(inputs, w_query, w_key, w_value, w_out, w_up, w_down, gain_attn, gain_ffn, cotangent):
    count, shard_len, width = inputs.shape
    own_rows = count * shard_len
    ranks = lax.axis_size("mp")
    length_half = shard_len * ranks
    level = lax.axis_index("dp") % LEVELS
    ctx = lax.axis_index("ctx")
    rank = lax.axis_index("mp")
    part_rows, head_cols = w_query.shape
    place = jnp.stack([ctx, rank, level]).astype(jnp.int32)

    inputs_flat = inputs.reshape(own_rows, width)
    cot_flat = cotangent.reshape(own_rows, width)
    rows_all = jnp.concatenate([inputs_flat, pack(w_out.T, width)], 0)
    rows_all = lax.all_gather(rows_all, "mp", axis=0)

    gains = team_gather(level_gather_small(jnp.stack([gain_attn, gain_ffn]), level))
    gains = pair_gather(gains.reshape(-1, 2, part_rows), ctx, 1)
    gains = gains.transpose(2, 0, 1, 3).reshape(2, 1, width).astype(F32)
    gain_first, gain_second = gains[0], gains[1]

    qkv_full = model_gather(jnp.concatenate([w_query, w_key, w_value], axis=1), level, ctx)
    blocks, unit_cols = w_up.shape[1:]
    sub = unit_cols // LEVELS
    half_blocks = blocks // 2
    up_turned = w_up.transpose(1, 2, 0)
    halves = [
        jnp.stack([up_turned[b : b + half_blocks], w_down[b : b + half_blocks]])
        for b in (0, half_blocks)
    ]
    own_part, sent_part = pair_split(halves[0], halves[1], ctx)
    pair = jnp.concatenate(
        [jnp.where(ctx == 0, own_part, sent_part), jnp.where(ctx == 0, sent_part, own_part)], -1
    )
    pair = pair.reshape(2, half_blocks, LEVELS, sub, 2 * part_rows).transpose(2, 0, 1, 3, 4)
    swapped = team_gather(level_swap(pair, level))
    swapped = side_by_side(swapped.reshape(-1, 2, half_blocks, sub, 2 * part_rows))
    cot_pieces = level_pieces(after(cot_flat, swapped))
    ranked = lax.all_gather(swapped, "mp", axis=0)
    positions = ctx * length_half + jnp.arange(length_half, dtype=jnp.int32)
    cosine, sine = rotation(positions, HEAD)
    qkv, normed = project(
        count, shard_len, rows_all, after(gain_first, *cot_pieces), qkv_full, cosine, sine
    )
    cot_rows = level_join(after(cot_pieces, qkv), level)
    out_rows = rows_all[:, own_rows:]
    out_parts = jnp.concatenate([unpack(out_rows[k], head_cols) for k in range(ranks)], 1)
    out_full = model_gather(out_parts, level, ctx)
    early = lax.ppermute(qkv[1:], "ctx", [(0, 1)])
    parts, logs = attend(place, ranks, length_half, qkv, early)
    hidden, normed_two, mixed_own = finish_attention(
        place, inputs_flat, gain_second, out_full, rank_swap(parts)
    )

    ranked = after(ranked, hidden)
    (opened,), rows_second, down_mine, activated, before = feed(
        place, [level_pieces(normed_two)], cot_rows, ranked, flip(ranked, "ctx", 1)
    )
    own, by_x, by_y, got_x, got_y = opened
    got_x, got_y = flip(got_x, "dp", 1), flip(got_y, "dp", 2)

    grad_kept, grad_sent, results = feed_weights(
        place, rows_second, cot_rows, activated, before, down_mine, ranks, half_blocks
    )
    grad_sent = after(grad_sent, got_x, got_y)
    grad_ffn = (grad_kept.astype(F32) + flip(grad_sent, "ctx", 1).astype(F32)).astype(BF)
    grad_ffn_low = [grad_ffn[:, kind].reshape(-1, width) for kind in range(2)]
    grad_ffn = [
        lax.psum_scatter(one, "mp", scatter_dimension=0, tiled=True) for one in grad_ffn_low
    ]

    last_y, last_x = level_scatter_last(by_x, by_y, got_x, got_y)
    own = after(own, *grad_ffn_low)
    grad_hidden, grad_low, parts = begin_back(
        place, ranks, (own, got_x, last_y, got_y, last_x), hidden, cot_flat, gain_second, out_full
    )
    parts = rank_swap(parts)
    grad_query, grad_own, grad_early = attend_back(
        place, length_half, qkv, early, logs, parts, cosine, sine
    )
    grad_early = after(grad_early, grad_ffn[0])
    back = lax.ppermute(grad_early, "ctx", [(1, 0)])
    grad_qkv, grad_first = project_back(
        count, ranks, grad_query, grad_own, back, cosine, sine, qkv_full
    )
    grad_first = after(grad_first, grad_ffn[1])
    grad_ffn = after(grad_ffn, grad_first)
    grad_first = lax.psum_scatter(
        grad_first.reshape(-1, width), "mp", scatter_dimension=0, tiled=True
    )

    results_open = after(level_scatter_open(after(results, grad_low), level), grad_qkv)
    result = level_sum(results_open, level_scatter_last(*results_open[1:]))
    outputs = (hidden + result).astype(BF).reshape(inputs.shape)

    grad_ffn = jnp.stack(grad_ffn).reshape(2, half_blocks, sub, width)
    grad_ffn = jnp.stack(jnp.split(grad_ffn, width // (2 * part_rows), axis=-1))
    grad_ffn = team_scatter(grad_ffn.reshape((-1, LEVELS) + grad_ffn.shape[1:]))
    grad_ffn = level_swap(grad_ffn, level).transpose(1, 2, 0, 3, 4)
    grad_ffn = grad_ffn.reshape(2, half_blocks, unit_cols, 2 * part_rows)
    own_part, sent_part = pair_split(grad_ffn[..., :part_rows], grad_ffn[..., part_rows:], ctx)
    grad_ffn = jnp.concatenate(
        [jnp.where(ctx == 0, own_part, sent_part), jnp.where(ctx == 0, sent_part, own_part)], 1
    ).astype(F32)
    grad_up_out = grad_ffn[0].transpose(2, 0, 1)
    grad_down_out = grad_ffn[1]
    gain_ffn_part = jnp.sum(grad_up_out * w_up.astype(F32), axis=(1, 2)) / gain_ffn.astype(F32)

    grad_qkv_w = outer([normed], [grad_qkv])
    grad_qkv_w = model_scatter(grad_qkv_w, level, ctx, part_rows)
    originals = jnp.concatenate([w_query, w_key, w_value], axis=1).astype(F32)
    gain_attn_part = jnp.sum(grad_qkv_w * originals, axis=1) / gain_attn.astype(F32)
    gain_grads = jnp.stack([gain_attn_part, gain_ffn_part])
    gain_grads = gain_grads + sum([turn(gain_grads, "mp", k) for k in range(1, ranks)])

    grad_out_w = outer([after(grad_low, grad_qkv)], [mixed_own])
    grad_out_w = model_scatter(grad_out_w, level, ctx, part_rows).astype(BF)
    grad_out_w = jnp.stack(jnp.split(grad_out_w, ranks, axis=1))
    grad_out_out = take(grad_out_w, rank).astype(F32)
    for k in range(1, ranks):
        grad_out_out = grad_out_out + turn(take(grad_out_w, (rank + k) % ranks), "mp", k).astype(F32)
    grad_out_out = grad_out_out.T

    grad_first = after(grad_first, grad_out_out, gain_grads, outputs, grad_qkv_w, grad_up_out, grad_down_out)
    inputs_f = inputs.astype(F32)
    input_grads = grad_hidden.reshape(inputs.shape) + norm_back(
        inputs_f,
        inverse_rms(inputs_f),
        gain_first * grad_first.reshape(inputs.shape).astype(F32),
    )
    return (
        outputs,
        input_grads,
        grad_qkv_w[:, :head_cols],
        grad_qkv_w[:, head_cols : 2 * head_cols],
        grad_qkv_w[:, 2 * head_cols :],
        grad_out_out,
        grad_up_out,
        grad_down_out,
        gain_grads[0],
        gain_grads[1],
    )


def solution(mesh):
    in_specs = (
        P("dp", ("ctx", "mp"), None),
        P(("dp", "ctx"), "mp"),
        P(("dp", "ctx"), "mp"),
        P(("dp", "ctx"), "mp"),
        P("mp", ("dp", "ctx")),
        P(("dp", "ctx"), None, "mp"),
        P(None, "mp", ("dp", "ctx")),
        P(("dp", "ctx")),
        P(("dp", "ctx")),
        P("dp", ("ctx", "mp"), None),
    )
    out_specs = (
        P("dp", ("ctx", "mp"), None),
        P("dp", ("ctx", "mp"), None),
        P(("dp", "ctx"), "mp"),
        P(("dp", "ctx"), "mp"),
        P(("dp", "ctx"), "mp"),
        P("mp", ("dp", "ctx")),
        P(("dp", "ctx"), None, "mp"),
        P(None, "mp", ("dp", "ctx")),
        P(("dp", "ctx")),
        P(("dp", "ctx")),
    )
    return jax.shard_map(local, mesh=mesh, in_specs=in_specs, out_specs=out_specs, check_vma=False)
```

time: 626 us -> 595 us (0.950)
  starting transfers between devices: 125 us -> 91.3 us
  Pallas kernels: 96.8 us -> 119 us
  waiting for transfers between devices: 202 us -> 220 us
  other arithmetic: 65.4 us -> 51 us
  matrix products: 11.3 us -> 0 us
  local copies, waits for them, and re-layouts: 99.7 us -> 88.8 us
    ppermute x21 -> x12, waiting for transfers between devices: 46 us -> 71 us  [turn(): lax.ppermute(shard, axis, [(i, (i + by) % devices) for i in range(devices)])]
    pallas_call x8 -> x6, Pallas kernels: 60.3 us -> 82.1 us  [the longest x1 24.3 us: feed(): pl.pallas_call(functools.partial(feed_kernel, count), grid_spec=pltpu.Pre...]
    ppermute x21 -> x12, starting transfers between devices: 48.4 us -> 33.1 us  [turn(): lax.ppermute(shard, axis, [(i, (i + by) % devices) for i in range(devices)])]
    ppermute x67 -> x50, starting transfers between devices: 68 us -> 53.2 us  [flip(): return lax.ppermute(shard, axis, [(i, i ^ bit) for i in range(devices)])]
    dot_general x6 -> x0, matrix products: 11.3 us -> none  [product(): return jnp.einsum(equation, left, right, preferred_element_type=F32)]
    ppermute x67 -> x50, waiting for transfers between devices: 120 us -> 109 us  [flip(): return lax.ppermute(shard, axis, [(i, i ^ bit) for i in range(devices)])]
    convert_element_type x11 -> x8, other arithmetic: 19.3 us -> 11 us  [the longest x1 4.04 us: local(): (grad_kept.astype(F32) + flip(grad_sent, 'ctx', 1).astype(F32)).astype(BF)]
    slice x21 -> x11, local copies, waits for them, and re-layouts: 20.9 us -> 13.7 us  [the longest x1 3.36 us: level_scatter_open(): got_y = flip(jnp.stack([by_y[half:], by_xy[half:]]), 'dp', 2)]
  transfers between devices with their start and end apart: 98 -> 69, of which waited for: 43 -> 31; matrix products, arithmetic and copies ran while one was open for 23% -> 18% of each run, Pallas kernels for 10% -> 16%
where the time goes in v3:
time: 595 us; the launch traced here: 586 us
  waiting for transfers between devices  220 us (37%)
  Pallas kernels  119 us (20%)
  starting transfers between devices  91.3 us (15%)
  local copies, waits for them, and re-layouts  88.8 us (15%)
  other arithmetic  51 us (9%)
  between operations  15.5 us (3%)
    ppermute x50, waiting for transfers between devices, flip(): return lax.ppermute(shard, axis, [(i, i ^ bit) for i in range(devices)])  109 us
    ppermute x12, waiting for transfers between devices, turn(): lax.ppermute(shard, axis, [(i, (i + by) % devices) for i in range(devices)])  71 us
    ppermute x50, starting transfers between devices, flip(): return lax.ppermute(shard, axis, [(i, i ^ bit) for i in range(devices)])  53.2 us
    ppermute x12, starting transfers between devices, turn(): lax.ppermute(shard, axis, [(i, (i + by) % devices) for i in range(devices)])  33.1 us
    all_gather x1, waiting for transfers between devices, local(): rows_all = lax.all_gather(rows_all, 'mp', axis=0)  26.6 us
    unnamed x134, local copies, waits for them, and re-layouts  25.9 us
    dynamic_update_slice x24, local copies, waits for them, and re-layouts, put(): lax.dynamic_update_slice(buffer, jnp.expand_dims(part, dim), tuple(starts))  25.5 us
    pallas_call x1, Pallas kernels, feed(): pl.pallas_call(functools.partial(feed_kernel, count), grid_spec=pltpu.Pre...  24.3 us
  transfers between devices with their start and end apart: 69, of which 31 were waited for; matrix products, arithmetic and copies ran while one was open for 18% of the time, Pallas kernels for 16%

profile of v3, /device:TPU:0, one launch (start us, length us, event | category | flops | bytes accessed | tf_op | source)
XLA Modules:
  0.0 586.3 jit_solution(14649130513442510591)
XLA Ops:
  39.9 6.7 %collective-permute-done.10 = bf16[2,4,48,384]{3,2,1,0:T(8,128)(2,1)S(1)} collective-permute-done((bf16[2,4,48,384]{3,2,1,0:T(8,128)(2,1)S(1)}, bf16[2,4,48,384]{3,2,1,0:T(8,128)(2,1)S(1)}, u32[]{:S(2)}, u32[]{:S(2)}) %collective-permute-start.10) | collective-permute-done | bytes 294944 | tf_op jit(solution)/shard_map/ppermute | solution.py:22
  46.7 4.8 collective-permute-done.11
  60.8 20.3 %collective-permute-done.13 = bf16[384,1536]{1,0:T(8,128)(2,1)} collective-permute-done((bf16[384,1536]{1,0:T(8,128)(2,1)}, bf16[384,1536]{1,0:T(8,128)(2,1)}, u32[]{:S(2)}, u32[]{:S(2)}) %collective-permute-start.13) | collective-permute-done | bytes 1179680 | tf_op jit(solution)/shard_map/ppermute | solution.py:22
  86.0 26.6 %all-gather.5.cloned.1.call-done = bf16[1728,1536]{1,0:T(8,128)(2,1)} async-done(((bf16[432,1536]{1,0:T(8,128)(2,1)}), bf16[1728,1536]{1,0:T(8,128)(2,1)}) %all-gather.5.cloned.1.call-update) | async-done | bytes 5308432 | tf_op jit(solution)/shard_map/all_gather | solution.py:947
  125.2 13.6 %project.1 = (bf16[3,1536,384]{2,1,0:T(8,128)(2,1)S(1)}, bf16[1536,1536]{1,0:T(8,128)(2,1)S(1)}) custom-call(bf16[4,432,1536]{2,1,0:T(8,128)(2,1)S(1)} %bitcast.258, f32[1,1536]{1,0:T(1,128)S(1)} %squeeze.124.gain_ref, bf16[1536,1152]{1,0:T(8,128)(2,1)S(1)} %bitcast.249, f32[2,512,128]{2,1,0:T(8,128)S(1)} %copy-done.9, f32[2,512,128]{2,1,0:T(8,128)S(1)} %copy-done.12), custom_call_target="tpu_custom_call" | custom-call | flops 113246208 | bytes 491520 | tf_op jit(solution)/shard_map/project/pallas_call | solution.py:211
  147.7 4.1 collective-permute-done.6
  156.1 11.6 %attend.1 = (bf16[384,384]{1,0:T(8,128)(2,1)S(1)}, bf16[384,384]{1,0:T(8,128)(2,1)S(1)}, bf16[384,384]{1,0:T(8,128)(2,1)S(1)}, bf16[384,384]{1,0:T(8,128)(2,1)S(1)}, f32[9,512,1]{2,1,0:T(8,128)S(1)}) custom-call(s32[3]{0:T(128)S(1)} %pad_add_fusion.place_ref, bf16[3,1536,384]{2,1,0:T(8,128)(2,1)S(1)} %get-tuple-element.67.query_ref.key_ref.value_ref, ...), custom_call_target="tpu_custom_call" | custom-call | flops 50331648 | bytes 172032 | tf_op jit(solution)/shard_map/attend/pallas_call | solution.py:296
  173.6 11.2 %collective-permute-done.23.refs_1_ = bf16[384,384]{1,0:T(8,128)(2,1)S(1)} collective-permute-done((bf16[384,384]{1,0:T(8,128)(2,1)S(1)}, bf16[384,384]{1,0:T(8,128)(2,1)S(1)}, u32[]{:S(2)}, u32[]{:S(2)}) %collective-permute-start.23) | collective-permute-done | bytes 294944 | tf_op jit(solution)/shard_map/ppermute | solution.py:27
  184.8 20.7 %collective-permute-done.24.refs_2_ = bf16[384,384]{1,0:T(8,128)(2,1)S(1)} collective-permute-done((bf16[384,384]{1,0:T(8,128)(2,1)S(1)}, bf16[384,384]{1,0:T(8,128)(2,1)S(1)}, u32[]{:S(2)}, u32[]{:S(2)}) %collective-permute-start.24) | collective-permute-done | bytes 294944 | tf_op jit(solution)/shard_map/ppermute | solution.py:27
  205.7 3.4 finish_attention.1
  214.7 12.9 %all-gather.7.cloned.1.call-done = bf16[8,4,48,1536]{3,2,1,0:T(8,128)(2,1)} async-done(((bf16[2,4,48,1536]{3,2,1,0:T(8,128)(2,1)}), bf16[8,4,48,1536]{3,2,1,0:T(8,128)(2,1)}) %all-gather.7.cloned.1.call-update) | async-done | bytes 4718608 | tf_op jit(solution)/shard_map/all_gather | solution.py:971
  237.9 18.4 %collective-permute-done.27.refs_1_ = bf16[384,1536]{1,0:T(8,128)(2,1)S(1)} collective-permute-done((bf16[384,1536]{1,0:T(8,128)(2,1)}, bf16[384,1536]{1,0:T(8,128)(2,1)S(1)}, u32[]{:S(2)}, u32[]{:S(2)}) %collective-permute-start.27) | collective-permute-done | bytes 1179680 | tf_op jit(solution)/shard_map/ppermute | solution.py:22
  264.2 7.3 %collective-permute-done.29.refs_3_ = bf16[192,1536]{1,0:T(8,128)(2,1)} collective-permute-done((bf16[192,1536]{1,0:T(8,128)(2,1)S(1)}, bf16[192,1536]{1,0:T(8,128)(2,1)}, u32[]{:S(2)}, u32[]{:S(2)}) %collective-permute-start.29) | collective-permute-done | bytes 589856 | tf_op jit(solution)/shard_map/ppermute | solution.py:22
  272.7 24.3 %feed.1 = (bf16[384,1536]{1,0:T(8,128)(2,1)}, bf16[192,1536]{1,0:T(8,128)(2,1)}, bf16[192,1536]{1,0:T(8,128)(2,1)}, bf16[2,192,1536]{2,1,0:T(8,128)(2,1)}, bf16[...) custom-call(s32[3]{0:T(128)} %copy-done.32, ...), custom_call_target="tpu_custom_call" | custom-call | flops 679477248 | bytes 1843200 | tf_op jit(solution)/shard_map/feed/pallas_call | solution.py:731
  299.1 22.3 %feed_weights.1 = (bf16[4,2,4,48,1536]{4,3,2,1,0:T(8,128)(2,1)}, bf16[4,2,4,48,1536]{4,3,2,1,0:T(8,128)(2,1)}, bf16[4,384,1536]{2,1,0:T(8,128)(2,1)}) custom-call(s32[3]{0:T(128)} %copy-done.32, bf16[4,384,1536]{2,1,0:T(8,128)(2,1)} %get-tuple-element.80.rows_ref, bf16[4,384,1536]{2,1,0:T(8,128)(2,1)} %fusion.9.cot_ref, ...), custom_call_target="tpu_custom_call" | custom-call | flops 679477248 | bytes 2138112 | tf_op jit(solution)/shard_map/feed_weights/pallas_call | solution.py:842
  324.4 8.1 %collective-permute-done.33 = bf16[4,2,4,48,1536]{4,3,2,1,0:T(8,128)(2,1)S(1)} collective-permute-done((bf16[4,2,4,48,1536]{4,3,2,1,0:T(8,128)(2,1)}, bf16[4,2,4,48,1536]{4,3,2,1,0:T(8,128)(2,1)S(1)}, u32[]{:S(2)}, u32[]{:S(2)}) %collective-permute-start.33) | collective-permute-done | bytes 4718624 | tf_op jit(solution)/shard_map/ppermute | solution.py:22
  332.5 4.0 add_convert_fusion
  344.5 12.7 %collective-permute-done.35.last_x_ref = bf16[192,1536]{1,0:T(8,128)(2,1)S(1)} collective-permute-done((bf16[192,1536]{1,0:T(8,128)(2,1)S(1)}, bf16[192,1536]{1,0:T(8,128)(2,1)S(1)}, u32[]{:S(2)}, u32[]{:S(2)}) %collective-permute-start.35) | collective-permute-done | bytes 589856 | tf_op jit(solution)/shard_map/ppermute | solution.py:22
  358.1 8.4 %begin_back.1 = (f32[384,1536]{1,0:T(8,128)}, bf16[384,1536]{1,0:T(8,128)(2,1)S(1)}, bf16[384,384]{1,0:T(8,128)(2,1)S(1)}, bf16[384,384]{1,0:T(8,128)(2,1)S(1)},...) custom-call(s32[3]{0:T(128)S(1)} %copy-done.33, bf16[384,1536]{1,0:T(8,128)(2,1)S(1)} %copy-done.30, ...), custom_call_target="tpu_custom_call" | custom-call | flops 113246208 | bytes 1032192 | tf_op jit(solution)/shard_map/begin_back/pallas_call | solution.py:415
  367.5 6.4 %collective-permute-start.38 = (bf16[384,384]{1,0:T(8,128)(2,1)S(1)}, bf16[384,384]{1,0:T(8,128)(2,1)S(1)}, u32[]{:S(2)}, u32[]{:S(2)}) collective-permute-start(bf16[384,384]{1,0:T(8,128)(2,1)S(1)} %get-tuple-element.98), channel_id=1, source_target_pairs={{0,1},{1,2},{2,3},{3,0},{4,5},{5,6},{6,7},{7,4},{8,9},{9,10},{10,1... | collective-permute-start | bytes 884744 | tf_op jit(solution)/shard_map/ppermute | solution.py:27
  376.3 11.5 %collective-permute-done.38.refs_1_ = bf16[384,384]{1,0:T(8,128)(2,1)S(1)} collective-permute-done((bf16[384,384]{1,0:T(8,128)(2,1)S(1)}, bf16[384,384]{1,0:T(8,128)(2,1)S(1)}, u32[]{:S(2)}, u32[]{:S(2)}) %collective-permute-start.38) | collective-permute-done | bytes 294944 | tf_op jit(solution)/shard_map/ppermute | solution.py:27
  387.8 20.4 %collective-permute-done.39.refs_2_ = bf16[384,384]{1,0:T(8,128)(2,1)S(1)} collective-permute-done((bf16[384,384]{1,0:T(8,128)(2,1)S(1)}, bf16[384,384]{1,0:T(8,128)(2,1)S(1)}, u32[]{:S(2)}, u32[]{:S(2)}) %collective-permute-start.39) | collective-permute-done | bytes 294944 | tf_op jit(solution)/shard_map/ppermute | solution.py:27
  409.9 14.8 %attend_back.1 = (bf16[1536,384]{1,0:T(8,128)(2,1)S(1)}, f32[2,1536,384]{2,1,0:T(8,128)S(1)}, bf16[2,1536,384]{2,1,0:T(8,128)(2,1)S(1)}) custom-call(s32[3]{0:T(128)S(1)} %copy-done.33, bf16[3,1536,384]{2,1,0:T(8,128)(2,1)S(1)} %get-tuple-element.67.query_ref.key_ref.value_ref, bf16[3,1536,384]{2,1,0:T(8,128)(2,1)S(1)} %get-tuple-element.67.query_ref.key_ref.value_ref, ...), custom_call_target="tpu_custom_call" | custom-call | flops 125829120 | bytes 344064 | tf_op jit(solution)/shard_map/attend_back/pallas_call | solution.py:517
  441.9 10.1 %project_back.1 = (bf16[1536,1152]{1,0:T(8,128)(2,1)S(1)}, bf16[4,3,128,1536]{3,2,1,0:T(8,128)(2,1)S(1)}) custom-call(bf16[1536,384]{1,0:T(8,128)(2,1)S(1)} %copy-done.25, f32[2,1536,384]{2,1,0:T(8,128)S(1)} %copy-done.17, bf16[2,1536,384]{2,1,0:T(8,128)(2,1)S(1)} %collective-permute-done.41.back_ref, f32[2,512,128]{2,1,0:T(8,128)S(1)} %copy-done.11, ...), custom_call_target="tpu_custom_call" | custom-call | flops 339738624 | bytes 1179648 | tf_op jit(solution)/shard_map/project_back/pallas_call | solution.py:577
  452.1 7.4 %outer.3 = bf16[1536,1152]{1,0:T(8,128)(2,1)S(1)} custom-call(bf16[1536,1536]{1,0:T(8,128)(2,1)S(1)} %bitcast.261, bf16[1536,1152]{1,0:T(8,128)(2,1)S(1)} %get-tuple-element.105.refs_1_), custom_call_target="tpu_custom_call" | custom-call | flops 339738624 | bytes 737280 | tf_op jit(solution)/shard_map/outer/pallas_call | solution.py:889
  461.0 6.1 %collective-permute-start.52 = (bf16[4,192,1152]{2,1,0:T(8,128)(2,1)}, bf16[4,192,1152]{2,1,0:T(8,128)(2,1)}, u32[]{:S(2)}, u32[]{:S(2)}) collective-permute-start(bf16[4,192,1152]{2,1,0:T(8,128)(2,1)} %dynamic-slice_bitcast_fusion.1), channel_id=1, source_target_pairs={{0,4},{4,0},{1,5},{5,1},{2,6},{6,2},{3,7},{7,3},{8,12},{12,8},{9,1... | collective-permute-start | bytes 5308424 | tf_op jit(solution)/shard_map/ppermute | solution.py:22
  494.7 8.7 %collective-permute-done.43 = bf16[192,1536]{1,0:T(8,128)(2,1)S(1)} collective-permute-done((bf16[192,1536]{1,0:T(8,128)(2,1)S(1)}, bf16[192,1536]{1,0:T(8,128)(2,1)S(1)}, u32[]{:S(2)}, u32[]{:S(2)}) %collective-permute-start.43) | collective-permute-done | bytes 589856 | tf_op jit(solution)/shard_map/ppermute | solution.py:22
  518.5 3.4 copy.69
  537.6 7.5 %collective-permute-start.61 = (f32[2,192]{1,0:T(2,128)S(1)}, f32[2,192]{1,0:T(2,128)S(1)}, u32[]{:S(2)}, u32[]{:S(2)}) collective-permute-start(f32[2,192]{1,0:T(2,128)S(1)} %pad_maximum_fusion.15), channel_id=1, source_target_pairs={{0,1},{1,2},{2,3},{3,0},{4,5},{5,6},{6,7},{7,4},{8,9},{9,10},{10,1... | collective-permute-start | bytes 4616 | tf_op jit(solution)/shard_map/ppermute | solution.py:27
  551.6 3.8 collective-permute-done.46
  556.8 7.5 %collective-permute-start.49 = (bf16[192,384]{1,0:T(8,128)(2,1)S(1)}, bf16[192,384]{1,0:T(8,128)(2,1)S(1)}, u32[]{:S(2)}, u32[]{:S(2)}) collective-permute-start(bf16[192,384]{1,0:T(8,128)(2,1)S(1)} %get-tuple-element.224), channel_id=1, source_target_pairs={{0,1},{1,2},{2,3},{3,0},{4,5},{5,6},{6,7},{7,4},{8,9},{9,10},{10,1... | collective-permute-start | bytes 442376 | tf_op jit(solution)/shard_map/ppermute | solution.py:27
  570.3 4.0 collective-permute-done.50
  (381 shorter events, 217.8 us)
Async XLA Ops:
  7.2 105.4 %all-gather.5.cloned.1.call-start = ((), (), s32[]{:S(2)}) async-start(), calls=%async_computation.6 | async-start | bytes 6635520 | tf_op jit(solution)/shard_map/all_gather | solution.py:947
  10.6 217.1 %all-gather.7.cloned.1.call-start = ((), (), s32[]{:S(2)}) async-start(), calls=%async_computation.7 | async-start | bytes 5898240 | tf_op jit(solution)/shard_map/all_gather | solution.py:971
  30.4 27.4 %collective-permute-start.19 = (bf16[96,1152]{1,0:T(8,128)(2,1)S(1)}, bf16[96,1152]{1,0:T(8,128)(2,1)S(1)}, u32[]{:S(2)}, u32[]{:S(2)}) collective-permute-start(bf16[96,1152]{1,0:T(8,128)(2,1)S(1)} %slice.443), channel_id=1, source_target_pairs={{0,16},{8,24},{16,0},{24,8},{1,17},{9,25},{17,1},{25,9},{2,18},{10... | collective-permute-start | bytes 663560 | tf_op jit(solution)/shard_map/ppermute | solution.py:22
  31.9 25.9 %collective-permute-start.20 = (bf16[96,1152]{1,0:T(8,128)(2,1)S(1)}, bf16[96,1152]{1,0:T(8,128)(2,1)S(1)}, u32[]{:S(2)}, u32[]{:S(2)}) collective-permute-start(bf16[96,1152]{1,0:T(8,128)(2,1)S(1)} %slice.444), channel_id=1, source_target_pairs={{0,8},{8,0},{16,24},{24,16},{1,9},{9,1},{17,25},{25,17},{2,10},{10... | collective-permute-start | bytes 663560 | tf_op jit(solution)/shard_map/ppermute | solution.py:22
  54.0 27.2 %collective-permute-start.13 = (bf16[384,1536]{1,0:T(8,128)(2,1)}, bf16[384,1536]{1,0:T(8,128)(2,1)}, u32[]{:S(2)}, u32[]{:S(2)}) collective-permute-start(bf16[384,1536]{1,0:T(8,128)(2,1)} %bitcast.25.cot_ref), channel_id=1, source_target_pairs={{0,8},{8,0},{16,24},{24,16},{1,9},{9,1},{17,25},{25,17},{2,10},{10... | collective-permute-start | bytes 3538952 | tf_op jit(solution)/shard_map/ppermute | solution.py:22
  54.5 29.1 %collective-permute-start.14 = (bf16[384,1536]{1,0:T(8,128)(2,1)}, bf16[384,1536]{1,0:T(8,128)(2,1)}, u32[]{:S(2)}, u32[]{:S(2)}) collective-permute-start(bf16[384,1536]{1,0:T(8,128)(2,1)} %bitcast.25.cot_ref), channel_id=1, source_target_pairs={{0,16},{8,24},{16,0},{24,8},{1,17},{9,25},{17,1},{25,9},{2,18},{10... | collective-permute-start | bytes 3538952 | tf_op jit(solution)/shard_map/ppermute | solution.py:22
  55.9 373.4 %reduce-scatter.4.cloned.1.call-start = ((), (), s32[]{:S(2)}) async-start(), calls=%async_computation.3 | async-start | bytes 2949120 | tf_op jit(solution)/shard_map/reduce_scatter | solution.py:1001
  58.6 60.7 %collective-permute-start.21 = (bf16[4,192,1152]{2,1,0:T(8,128)(2,1)}, bf16[4,192,1152]{2,1,0:T(8,128)(2,1)}, u32[]{:S(2)}, u32[]{:S(2)}) collective-permute-start(bf16[4,192,1152]{2,1,0:T(8,128)(2,1)} %fusion.19), channel_id=1, source_target_pairs={{0,4},{4,0},{1,5},{5,1},{2,6},{6,2},{3,7},{7,3},{8,12},{12,8},{9,1... | collective-permute-start | bytes 5308424 | tf_op jit(solution)/shard_map/ppermute | solution.py:22
  83.0 40.0 %collective-permute-start.15 = (bf16[192,1536]{1,0:T(8,128)(2,1)}, bf16[192,1536]{1,0:T(8,128)(2,1)}, u32[]{:S(2)}, u32[]{:S(2)}) collective-permute-start(bf16[192,1536]{1,0:T(8,128)(2,1)} %slice.441), channel_id=1, source_target_pairs={{0,16},{8,24},{16,0},{24,8},{1,17},{9,25},{17,1},{25,9},{2,18},{10... | collective-permute-start | bytes 1769480 | tf_op jit(solution)/shard_map/ppermute | solution.py:22
  85.5 37.5 %collective-permute-start.16 = (bf16[192,1536]{1,0:T(8,128)(2,1)}, bf16[192,1536]{1,0:T(8,128)(2,1)}, u32[]{:S(2)}, u32[]{:S(2)}) collective-permute-start(bf16[192,1536]{1,0:T(8,128)(2,1)} %slice.442), channel_id=1, source_target_pairs={{0,8},{8,0},{16,24},{24,16},{1,9},{9,1},{17,25},{25,17},{2,10},{10... | collective-permute-start | bytes 1769480 | tf_op jit(solution)/shard_map/ppermute | solution.py:22
  116.4 28.4 %collective-permute-start.4 = (bf16[192,1536]{1,0:T(8,128)(2,1)S(1)}, bf16[192,1536]{1,0:T(8,128)(2,1)S(1)}, u32[]{:S(2)}, u32[]{:S(2)}) collective-permute-start(bf16[192,1536]{1,0:T(8,128)(2,1)S(1)} %get-tuple-element.163), channel_id=1, source_target_pairs={{0,8},{8,0},{16,24},{24,16},{1,9},{9,1},{17,25},{25,17},{2,10},{10... | collective-permute-start | bytes 1769480 | tf_op jit(solution)/shard_map/ppermute | solution.py:22
  117.8 27.3 %collective-permute-start.5 = (bf16[192,1536]{1,0:T(8,128)(2,1)S(1)}, bf16[192,1536]{1,0:T(8,128)(2,1)S(1)}, u32[]{:S(2)}, u32[]{:S(2)}) collective-permute-start(bf16[192,1536]{1,0:T(8,128)(2,1)S(1)} %get-tuple-element.163), channel_id=1, source_target_pairs={{0,16},{8,24},{16,0},{24,8},{1,17},{9,25},{17,1},{25,9},{2,18},{10... | collective-permute-start | bytes 1769480 | tf_op jit(solution)/shard_map/ppermute | solution.py:22
  152.8 18.8 %collective-permute-start.8 = (bf16[4,192,1536]{2,1,0:T(8,128)(2,1)}, bf16[4,192,1536]{2,1,0:T(8,128)(2,1)}, u32[]{:S(2)}, u32[]{:S(2)}) collective-permute-start(bf16[4,192,1536]{2,1,0:T(8,128)(2,1)} %fusion.16), channel_id=1, source_target_pairs={{0,4},{4,0},{1,5},{5,1},{2,6},{6,2},{3,7},{7,3},{8,12},{12,8},{9,1... | collective-permute-start | bytes 7077896 | tf_op jit(solution)/shard_map/ppermute | solution.py:22
  167.7 17.0 %collective-permute-start.23 = (bf16[384,384]{1,0:T(8,128)(2,1)S(1)}, bf16[384,384]{1,0:T(8,128)(2,1)S(1)}, u32[]{:S(2)}, u32[]{:S(2)}) collective-permute-start(bf16[384,384]{1,0:T(8,128)(2,1)S(1)} %get-tuple-element.69), channel_id=1, source_target_pairs={{0,1},{1,2},{2,3},{3,0},{4,5},{5,6},{6,7},{7,4},{8,9},{9,10},{10,1... | collective-permute-start | bytes 884744 | tf_op jit(solution)/shard_map/ppermute | solution.py:27
  167.8 37.7 %collective-permute-start.24 = (bf16[384,384]{1,0:T(8,128)(2,1)S(1)}, bf16[384,384]{1,0:T(8,128)(2,1)S(1)}, u32[]{:S(2)}, u32[]{:S(2)}) collective-permute-start(bf16[384,384]{1,0:T(8,128)(2,1)S(1)} %get-tuple-element.70), channel_id=1, source_target_pairs={{0,2},{1,3},{2,0},{3,1},{4,6},{5,7},{6,4},{7,5},{8,10},{9,11},{10,... | collective-permute-start | bytes 884744 | tf_op jit(solution)/shard_map/ppermute | solution.py:27
  169.1 36.6 %collective-permute-start.25 = (bf16[384,384]{1,0:T(8,128)(2,1)S(1)}, bf16[384,384]{1,0:T(8,128)(2,1)S(1)}, u32[]{:S(2)}, u32[]{:S(2)}) collective-permute-start(bf16[384,384]{1,0:T(8,128)(2,1)S(1)} %get-tuple-element.71), channel_id=1, source_target_pairs={{0,3},{1,0},{2,1},{3,2},{4,7},{5,4},{6,5},{7,6},{8,11},{9,8},{10,9... | collective-permute-start | bytes 884744 | tf_op jit(solution)/shard_map/ppermute | solution.py:27
  227.7 45.1 %collective-permute-start.26 = (bf16[4,2,4,48,1536]{4,3,2,1,0:T(8,128)(2,1)}, bf16[4,2,4,48,1536]{4,3,2,1,0:T(8,128)(2,1)}, u32[]{:S(2)}, u32[]{:S(2)}) collective-permute-start(bf16[4,2,4,48,1536]{4,3,2,1,0:T(8,128)(2,1)} %bitcast.269), channel_id=1, source_target_pairs={{0,4},{4,0},{1,5},{5,1},{2,6},{6,2},{3,7},{7,3},{8,12},{12,8},{9,1... | collective-permute-start | bytes 14155784 | tf_op jit(solution)/shard_map/ppermute | solution.py:22
  227.7 28.6 %collective-permute-start.27 = (bf16[384,1536]{1,0:T(8,128)(2,1)}, bf16[384,1536]{1,0:T(8,128)(2,1)S(1)}, u32[]{:S(2)}, u32[]{:S(2)}) collective-permute-start(bf16[384,1536]{1,0:T(8,128)(2,1)} %copy-done.31), channel_id=1, source_target_pairs={{0,8},{8,0},{16,24},{24,16},{1,9},{9,1},{17,25},{25,17},{2,10},{10... | collective-permute-start | bytes 3538952 | tf_op jit(solution)/shard_map/ppermute | solution.py:22
  229.1 28.7 %collective-permute-start.28 = (bf16[384,1536]{1,0:T(8,128)(2,1)}, bf16[384,1536]{1,0:T(8,128)(2,1)S(1)}, u32[]{:S(2)}, u32[]{:S(2)}) collective-permute-start(bf16[384,1536]{1,0:T(8,128)(2,1)} %copy-done.31), channel_id=1, source_target_pairs={{0,16},{8,24},{16,0},{24,8},{1,17},{9,25},{17,1},{25,9},{2,18},{10... | collective-permute-start | bytes 3538952 | tf_op jit(solution)/shard_map/ppermute | solution.py:22
  297.0 26.6 %collective-permute-start.32 = (bf16[2,192,1536]{2,1,0:T(8,128)(2,1)}, bf16[2,192,1536]{2,1,0:T(8,128)(2,1)S(1)}, u32[]{:S(2)}, u32[]{:S(2)}) collective-permute-start(bf16[2,192,1536]{2,1,0:T(8,128)(2,1)} %get-tuple-element.89), channel_id=1, source_target_pairs={{0,16},{8,24},{16,0},{24,8},{1,17},{9,25},{17,1},{25,9},{2,18},{10... | collective-permute-start | bytes 3538952 | tf_op jit(solution)/shard_map/ppermute | solution.py:22
  298.1 26.3 %collective-permute-start.31 = (bf16[2,192,1536]{2,1,0:T(8,128)(2,1)}, bf16[2,192,1536]{2,1,0:T(8,128)(2,1)S(1)}, u32[]{:S(2)}, u32[]{:S(2)}) collective-permute-start(bf16[2,192,1536]{2,1,0:T(8,128)(2,1)} %get-tuple-element.88), channel_id=1, source_target_pairs={{0,8},{8,0},{16,24},{24,16},{1,9},{9,1},{17,25},{25,17},{2,10},{10... | collective-permute-start | bytes 3538952 | tf_op jit(solution)/shard_map/ppermute | solution.py:22
  339.3 127.7 %reduce-scatter.6.cloned.1.call-start = ((), (), s32[]{:S(2)}) async-start(), calls=%async_computation.4 | async-start | bytes 2949120 | tf_op jit(solution)/shard_map/reduce_scatter | solution.py:1001
  339.9 235.3 %reduce-scatter.8.cloned.1.call-start = ((), (), s32[]{:S(2)}) async-start(), calls=%async_computation.5 | async-start | bytes 5898240 | tf_op jit(solution)/shard_map/reduce_scatter | solution.py:1020
  367.5 20.3 %collective-permute-start.38 = (bf16[384,384]{1,0:T(8,128)(2,1)S(1)}, bf16[384,384]{1,0:T(8,128)(2,1)S(1)}, u32[]{:S(2)}, u32[]{:S(2)}) collective-permute-start(bf16[384,384]{1,0:T(8,128)(2,1)S(1)} %get-tuple-element.98), channel_id=1, source_target_pairs={{0,1},{1,2},{2,3},{3,0},{4,5},{5,6},{6,7},{7,4},{8,9},{9,10},{10,1... | collective-permute-start | bytes 884744 | tf_op jit(solution)/shard_map/ppermute | solution.py:27
  373.9 34.3 %collective-permute-start.39 = (bf16[384,384]{1,0:T(8,128)(2,1)S(1)}, bf16[384,384]{1,0:T(8,128)(2,1)S(1)}, u32[]{:S(2)}, u32[]{:S(2)}) collective-permute-start(bf16[384,384]{1,0:T(8,128)(2,1)S(1)} %get-tuple-element.99), channel_id=1, source_target_pairs={{0,2},{1,3},{2,0},{3,1},{4,6},{5,7},{6,4},{7,5},{8,10},{9,11},{10,... | collective-permute-start | bytes 884744 | tf_op jit(solution)/shard_map/ppermute | solution.py:27
  373.9 34.3 %collective-permute-start.40 = (bf16[384,384]{1,0:T(8,128)(2,1)S(1)}, bf16[384,384]{1,0:T(8,128)(2,1)S(1)}, u32[]{:S(2)}, u32[]{:S(2)}) collective-permute-start(bf16[384,384]{1,0:T(8,128)(2,1)S(1)} %get-tuple-element.100), channel_id=1, source_target_pairs={{0,3},{1,0},{2,1},{3,2},{4,7},{5,4},{6,5},{7,6},{8,11},{9,8},{10,9... | collective-permute-start | bytes 884744 | tf_op jit(solution)/shard_map/ppermute | solution.py:27
  435.5 45.9 %collective-permute-start.37 = (bf16[2,192,1536]{2,1,0:T(8,128)(2,1)}, bf16[2,192,1536]{2,1,0:T(8,128)(2,1)}, u32[]{:S(2)}, u32[]{:S(2)}) collective-permute-start(bf16[2,192,1536]{2,1,0:T(8,128)(2,1)} %pad_maximum_fusion.4), channel_id=1, source_target_pairs={{0,16},{8,24},{16,0},{24,8},{1,17},{9,25},{17,1},{25,9},{2,18},{10... | collective-permute-start | bytes 3538952 | tf_op jit(solution)/shard_map/ppermute | solution.py:22
  438.0 45.3 %collective-permute-start.36 = (bf16[2,192,1536]{2,1,0:T(8,128)(2,1)}, bf16[2,192,1536]{2,1,0:T(8,128)(2,1)}, u32[]{:S(2)}, u32[]{:S(2)}) collective-permute-start(bf16[2,192,1536]{2,1,0:T(8,128)(2,1)} %pad_maximum_fusion.3), channel_id=1, source_target_pairs={{0,8},{8,0},{16,24},{24,16},{1,9},{9,1},{17,25},{25,17},{2,10},{10... | collective-permute-start | bytes 3538952 | tf_op jit(solution)/shard_map/ppermute | solution.py:22
  461.0 48.6 %collective-permute-start.52 = (bf16[4,192,1152]{2,1,0:T(8,128)(2,1)}, bf16[4,192,1152]{2,1,0:T(8,128)(2,1)}, u32[]{:S(2)}, u32[]{:S(2)}) collective-permute-start(bf16[4,192,1152]{2,1,0:T(8,128)(2,1)} %dynamic-slice_bitcast_fusion.1), channel_id=1, source_target_pairs={{0,4},{4,0},{1,5},{5,1},{2,6},{6,2},{3,7},{7,3},{8,12},{12,8},{9,1... | collective-permute-start | bytes 5308424 | tf_op jit(solution)/shard_map/ppermute | solution.py:22
  472.0 16.8 %collective-permute-start.58 = (bf16[2,4,48,384]{3,2,1,0:T(8,128)(2,1)}, bf16[2,4,48,384]{3,2,1,0:T(8,128)(2,1)}, u32[]{:S(2)}, u32[]{:S(2)}) collective-permute-start(bf16[2,4,48,384]{3,2,1,0:T(8,128)(2,1)} %get-tuple-element.201), channel_id=1, source_target_pairs={{0,16},{8,24},{16,0},{24,8},{1,17},{9,25},{17,1},{25,9},{2,18},{10... | collective-permute-start | bytes 884744 | tf_op jit(solution)/shard_map/ppermute | solution.py:22
  483.4 47.5 %collective-permute-start.44 = (bf16[4,192,1536]{2,1,0:T(8,128)(2,1)}, bf16[4,192,1536]{2,1,0:T(8,128)(2,1)}, u32[]{:S(2)}, u32[]{:S(2)}) collective-permute-start(bf16[4,192,1536]{2,1,0:T(8,128)(2,1)} %dynamic-slice_bitcast_fusion), channel_id=1, source_target_pairs={{0,4},{4,0},{1,5},{5,1},{2,6},{6,2},{3,7},{7,3},{8,12},{12,8},{9,1... | collective-permute-start | bytes 7077896 | tf_op jit(solution)/shard_map/ppermute | solution.py:22
  486.0 17.3 %collective-permute-start.43 = (bf16[192,1536]{1,0:T(8,128)(2,1)S(1)}, bf16[192,1536]{1,0:T(8,128)(2,1)S(1)}, u32[]{:S(2)}, u32[]{:S(2)}) collective-permute-start(bf16[192,1536]{1,0:T(8,128)(2,1)S(1)} %fusion.10), channel_id=1, source_target_pairs={{0,8},{8,0},{16,24},{24,16},{1,9},{9,1},{17,25},{25,17},{2,10},{10... | collective-permute-start | bytes 1769480 | tf_op jit(solution)/shard_map/ppermute | solution.py:22
  (102 other events, 992.0 us)
Sparse Core Ops, SparseCore 0:
  10.7 101.8 all-gather.4
  114.7 112.8 all-gather.6
  339.4 68.1 reduce-scatter.3
  409.8 49.0 reduce-scatter.5
  472.7 90.8 reduce-scatter.7

commit v4 on v3

--- a/solution.py
+++ b/solution.py
@@ -671,19 +671,23 @@
         pre_ref[0, :, :used] = grad_upped
         return contract(grad_upped, up_ref[:used], 1, 0)
 
-    for one in range(LEVELS - 1):
+    for one in range(LEVELS - 2):
 
         @pl.when(step == one)
         def _(one=one):
             sum_ref[...] = run(half // 2 ** (LEVELS - 2 - one))
 
-    @pl.when(step == LEVELS - 1)
+    @pl.when(step >= LEVELS - 2)
     def _():
-        sum_ref[...] = run(half)
-
-    @pl.when(step == LEVELS)
-    def _():
-        sum_ref[...] += run(half)
+        result = run(half)
+
+        @pl.when(step < LEVELS)
+        def _():
+            sum_ref[...] = result
+
+        @pl.when(step == LEVELS)
+        def _():
+            sum_ref[...] += result
 
     level = jnp.minimum(step, LEVELS - 1)
     for k in range(LEVELS):
@@ -943,15 +947,17 @@
 
     inputs_flat = inputs.reshape(own_rows, width)
     cot_flat = cotangent.reshape(own_rows, width)
-    rows_all = jnp.concatenate([inputs_flat, pack(w_out.T, width)], 0)
-    rows_all = lax.all_gather(rows_all, "mp", axis=0)
+    rows_all = lax.all_gather(inputs_flat, "mp", axis=0)
+    out_found = [turn(w_out, "mp", k) for k in range(1, ranks)]
 
     gains = team_gather(level_gather_small(jnp.stack([gain_attn, gain_ffn]), level))
     gains = pair_gather(gains.reshape(-1, 2, part_rows), ctx, 1)
     gains = gains.transpose(2, 0, 1, 3).reshape(2, 1, width).astype(F32)
     gain_first, gain_second = gains[0], gains[1]
 
-    qkv_full = model_gather(jnp.concatenate([w_query, w_key, w_value], axis=1), level, ctx)
+    qkv_full = model_gather(
+        after(jnp.concatenate([w_query, w_key, w_value], axis=1), *out_found), level, ctx
+    )
     blocks, unit_cols = w_up.shape[1:]
     sub = unit_cols // LEVELS
     half_blocks = blocks // 2
@@ -975,8 +981,10 @@
         count, shard_len, rows_all, after(gain_first, *cot_pieces), qkv_full, cosine, sine
     )
     cot_rows = level_join(after(cot_pieces, qkv), level)
-    out_rows = rows_all[:, own_rows:]
-    out_parts = jnp.concatenate([unpack(out_rows[k], head_cols) for k in range(ranks)], 1)
+    out_parts = put(jnp.zeros((ranks,) + w_out.shape, BF), w_out, rank)
+    for k in range(1, ranks):
+        out_parts = put(out_parts, out_found[k - 1], (rank + ranks - k) % ranks)
+    out_parts = after(out_parts.reshape(-1, part_rows).T, cot_pieces[3])
     out_full = model_gather(out_parts, level, ctx)
     early = lax.ppermute(qkv[1:], "ctx", [(0, 1)])
     parts, logs = attend(place, ranks, length_half, qkv, early)

time: 595 us -> 588 us (0.988)
  waiting for transfers between devices: 220 us -> 179 us
  local copies, waits for them, and re-layouts: 88.8 us -> 115 us
  starting transfers between devices: 91.3 us -> 101 us
    all_gather x1, waiting for transfers between devices: 26.6 us -> 0.01 us  [local(): rows_all = lax.all_gather(inputs_flat, 'mp', axis=0)]
    dynamic_update_slice x24 -> x30, local copies, waits for them, and re-layouts: 25.5 us -> 41.7 us  [put(): lax.dynamic_update_slice(buffer, jnp.expand_dims(part, dim), tuple(starts))]
    all_gather x1, waiting for transfers between devices: 12.9 us -> 0.01 us  [local(): ranked = lax.all_gather(swapped, 'mp', axis=0)]
    ppermute x12 -> x15, waiting for transfers between devices: 71 us -> 58.6 us  [turn(): lax.ppermute(shard, axis, [(i, (i + by) % devices) for i in range(devices)])]
    ppermute x12 -> x15, starting transfers between devices: 33.1 us -> 42.7 us  [turn(): lax.ppermute(shard, axis, [(i, (i + by) % devices) for i in range(devices)])]
    ppermute x50, waiting for transfers between devices: 109 us -> 119 us  [flip(): return lax.ppermute(shard, axis, [(i, i ^ bit) for i in range(devices)])]
    broadcast_in_dim x1 -> x4, local copies, waits for them, and re-layouts: 0.01 us -> 6.23 us  [put(): jnp.expand_dims(part, dim)]
    unnamed x134 -> x151, local copies, waits for them, and re-layouts: 25.9 us -> 31.4 us
  transfers between devices with their start and end apart: 69 -> 72, of which waited for: 31 -> 27; matrix products, arithmetic and copies ran while one was open for 18% -> 22% of each run, Pallas kernels for 16% -> 16%
where the time goes in v4:
time: 588 us; the launch traced here: 580 us
  waiting for transfers between devices  179 us (30%)
  Pallas kernels  119 us (20%)
  local copies, waits for them, and re-layouts  115 us (20%)
  starting transfers between devices  101 us (17%)
  other arithmetic  50.3 us (9%)
  between operations  15.5 us (3%)
    ppermute x50, waiting for transfers between devices, flip(): return lax.ppermute(shard, axis, [(i, i ^ bit) for i in range(devices)])  119 us
    ppermute x15, waiting for transfers between devices, turn(): lax.ppermute(shard, axis, [(i, (i + by) % devices) for i in range(devices)])  58.6 us
    ppermute x50, starting transfers between devices, flip(): return lax.ppermute(shard, axis, [(i, i ^ bit) for i in range(devices)])  53.4 us
    ppermute x15, starting transfers between devices, turn(): lax.ppermute(shard, axis, [(i, (i + by) % devices) for i in range(devices)])  42.7 us
    dynamic_update_slice x30, local copies, waits for them, and re-layouts, put(): lax.dynamic_update_slice(buffer, jnp.expand_dims(part, dim), tuple(starts))  41.7 us
    unnamed x151, local copies, waits for them, and re-layouts  31.4 us
    pallas_call x1, Pallas kernels, feed(): pl.pallas_call(functools.partial(feed_kernel, count), grid_spec=pltpu.Pre...  24.4 us
    pallas_call x1, Pallas kernels, feed_weights(): pl.pallas_call(feed_weights_kernel, grid_spec=pltpu.PrefetchScalarGridSpe...  22.3 us
  transfers between devices with their start and end apart: 72, of which 27 were waited for; matrix products, arithmetic and copies ran while one was open for 22% of the time, Pallas kernels for 16%

profile of v4, /device:TPU:0, one launch (start us, length us, event | category | flops | bytes accessed | tf_op | source)
XLA Modules:
  0.0 579.7 jit_solution(3056425597133663330)
XLA Ops:
  33.8 7.3 %collective-permute-done.20 = bf16[192,1152]{1,0:T(8,128)(2,1)S(1)} collective-permute-done((bf16[192,1152]{1,0:T(8,128)(2,1)}, bf16[192,1152]{1,0:T(8,128)(2,1)S(1)}, u32[]{:S(2)}, u32[]{:S(2)}) %collective-permute-start.20) | collective-permute-done | bytes 442400 | tf_op jit(solution)/shard_map/ppermute | solution.py:22
  42.7 4.5 collective-permute-done.22
  53.4 12.2 %collective-permute-done.9 = bf16[2,4,48,384]{3,2,1,0:T(8,128)(2,1)S(1)} collective-permute-done((bf16[2,4,48,384]{3,2,1,0:T(8,128)(2,1)S(1)}, bf16[2,4,48,384]{3,2,1,0:T(8,128)(2,1)S(1)}, u32[]{:S(2)}, u32[]{:S(2)}) %collective-permute-start.9) | collective-permute-done | bytes 294944 | tf_op jit(solution)/shard_map/ppermute | solution.py:22
  85.6 5.7 dynamic_update_slice.109
  91.4 5.8 dynamic_update_slice.110
  97.2 5.8 dynamic_update_slice.111
  109.1 10.8 %collective-permute-done.12 = bf16[192,1536]{1,0:T(8,128)(2,1)S(1)} collective-permute-done((bf16[192,1536]{1,0:T(8,128)(2,1)S(1)}, bf16[192,1536]{1,0:T(8,128)(2,1)S(1)}, u32[]{:S(2)}, u32[]{:S(2)}) %collective-permute-start.12) | collective-permute-done | bytes 589856 | tf_op jit(solution)/shard_map/ppermute | solution.py:22
  127.7 8.1 %collective-permute-done.13 = bf16[192,1536]{1,0:T(8,128)(2,1)S(1)} collective-permute-done((bf16[192,1536]{1,0:T(8,128)(2,1)S(1)}, bf16[192,1536]{1,0:T(8,128)(2,1)S(1)}, u32[]{:S(2)}, u32[]{:S(2)}) %collective-permute-start.13) | collective-permute-done | bytes 589856 | tf_op jit(solution)/shard_map/ppermute | solution.py:22
  147.7 13.5 %project.1 = (bf16[3,1536,384]{2,1,0:T(8,128)(2,1)S(1)}, bf16[1536,1536]{1,0:T(8,128)(2,1)S(1)}) custom-call(bf16[4,384,1536]{2,1,0:T(8,128)(2,1)S(1)} %copy-done.17, f32[1,1536]{1,0:T(1,128)S(1)} %squeeze.111.gain_ref, bf16[1536,1152]{1,0:T(8,128)(2,1)S(1)} %bitcast.251, f32[2,512,128]{2,1,0:T(8,128)S(1)} %copy-done.9, f32[2,512,128]{2,1,0:T(8,128)S(1)} %copy-done.12), custom_call_target="tpu_custom_call" | custom-call | flops 113246208 | bytes 491520 | tf_op jit(solution)/shard_map/project/pallas_call | solution.py:211
  171.9 11.6 %attend.1 = (bf16[384,384]{1,0:T(8,128)(2,1)S(1)}, bf16[384,384]{1,0:T(8,128)(2,1)S(1)}, bf16[384,384]{1,0:T(8,128)(2,1)S(1)}, bf16[384,384]{1,0:T(8,128)(2,1)S(1)}, f32[9,512,1]{2,1,0:T(8,128)S(1)}) custom-call(s32[3]{0:T(128)S(1)} %pad_add_fusion.place_ref, bf16[3,1536,384]{2,1,0:T(8,128)(2,1)S(1)} %get-tuple-element.71.query_ref.key_ref.value_ref, ...), custom_call_target="tpu_custom_call" | custom-call | flops 50331648 | bytes 172032 | tf_op jit(solution)/shard_map/attend/pallas_call | solution.py:296
  183.6 4.1 collective-permute-start.26
  192.7 6.7 %collective-permute-done.26.refs_1_ = bf16[384,384]{1,0:T(8,128)(2,1)S(1)} collective-permute-done((bf16[384,384]{1,0:T(8,128)(2,1)S(1)}, bf16[384,384]{1,0:T(8,128)(2,1)S(1)}, u32[]{:S(2)}, u32[]{:S(2)}) %collective-permute-start.26) | collective-permute-done | bytes 294944 | tf_op jit(solution)/shard_map/ppermute | solution.py:27
  199.4 12.8 %collective-permute-done.27.refs_2_ = bf16[384,384]{1,0:T(8,128)(2,1)S(1)} collective-permute-done((bf16[384,384]{1,0:T(8,128)(2,1)S(1)}, bf16[384,384]{1,0:T(8,128)(2,1)S(1)}, u32[]{:S(2)}, u32[]{:S(2)}) %collective-permute-start.27) | collective-permute-done | bytes 294944 | tf_op jit(solution)/shard_map/ppermute | solution.py:27
  231.1 19.1 %collective-permute-done.30.refs_1_ = bf16[384,1536]{1,0:T(8,128)(2,1)S(1)} collective-permute-done((bf16[384,1536]{1,0:T(8,128)(2,1)}, bf16[384,1536]{1,0:T(8,128)(2,1)S(1)}, u32[]{:S(2)}, u32[]{:S(2)}) %collective-permute-start.30) | collective-permute-done | bytes 1179680 | tf_op jit(solution)/shard_map/ppermute | solution.py:22
  257.0 7.9 %collective-permute-done.32.refs_3_ = bf16[192,1536]{1,0:T(8,128)(2,1)} collective-permute-done((bf16[192,1536]{1,0:T(8,128)(2,1)S(1)}, bf16[192,1536]{1,0:T(8,128)(2,1)}, u32[]{:S(2)}, u32[]{:S(2)}) %collective-permute-start.32) | collective-permute-done | bytes 589856 | tf_op jit(solution)/shard_map/ppermute | solution.py:22
  266.2 24.4 %feed.1 = (bf16[384,1536]{1,0:T(8,128)(2,1)}, bf16[192,1536]{1,0:T(8,128)(2,1)}, bf16[192,1536]{1,0:T(8,128)(2,1)}, bf16[2,192,1536]{2,1,0:T(8,128)(2,1)}, bf16[...) custom-call(s32[3]{0:T(128)} %copy-done.32, ...), custom_call_target="tpu_custom_call" | custom-call | flops 679477248 | bytes 1843200 | tf_op jit(solution)/shard_map/feed/pallas_call | solution.py:735
  292.7 22.3 %feed_weights.1 = (bf16[4,2,4,48,1536]{4,3,2,1,0:T(8,128)(2,1)}, bf16[4,2,4,48,1536]{4,3,2,1,0:T(8,128)(2,1)}, bf16[4,384,1536]{2,1,0:T(8,128)(2,1)}) custom-call(s32[3]{0:T(128)} %copy-done.32, bf16[4,384,1536]{2,1,0:T(8,128)(2,1)} %get-tuple-element.84.rows_ref, bf16[4,384,1536]{2,1,0:T(8,128)(2,1)} %fusion.9.cot_ref, ...), custom_call_target="tpu_custom_call" | custom-call | flops 679477248 | bytes 2138112 | tf_op jit(solution)/shard_map/feed_weights/pallas_call | solution.py:846
  317.3 8.1 %collective-permute-done.36 = bf16[4,2,4,48,1536]{4,3,2,1,0:T(8,128)(2,1)S(1)} collective-permute-done((bf16[4,2,4,48,1536]{4,3,2,1,0:T(8,128)(2,1)}, bf16[4,2,4,48,1536]{4,3,2,1,0:T(8,128)(2,1)S(1)}, u32[]{:S(2)}, u32[]{:S(2)}) %collective-permute-start.36) | collective-permute-done | bytes 4718624 | tf_op jit(solution)/shard_map/ppermute | solution.py:22
  325.5 4.0 add_convert_fusion
  337.5 12.6 %collective-permute-done.38.last_x_ref = bf16[192,1536]{1,0:T(8,128)(2,1)S(1)} collective-permute-done((bf16[192,1536]{1,0:T(8,128)(2,1)S(1)}, bf16[192,1536]{1,0:T(8,128)(2,1)S(1)}, u32[]{:S(2)}, u32[]{:S(2)}) %collective-permute-start.38) | collective-permute-done | bytes 589856 | tf_op jit(solution)/shard_map/ppermute | solution.py:22
  351.2 8.4 %begin_back.1 = (f32[384,1536]{1,0:T(8,128)}, bf16[384,1536]{1,0:T(8,128)(2,1)S(1)}, bf16[384,384]{1,0:T(8,128)(2,1)S(1)}, bf16[384,384]{1,0:T(8,128)(2,1)S(1)},...) custom-call(s32[3]{0:T(128)S(1)} %copy-done.33, bf16[384,1536]{1,0:T(8,128)(2,1)S(1)} %copy-done.30, ...), custom_call_target="tpu_custom_call" | custom-call | flops 113246208 | bytes 1032192 | tf_op jit(solution)/shard_map/begin_back/pallas_call | solution.py:415
  360.6 6.5 %collective-permute-start.41 = (bf16[384,384]{1,0:T(8,128)(2,1)S(1)}, bf16[384,384]{1,0:T(8,128)(2,1)S(1)}, u32[]{:S(2)}, u32[]{:S(2)}) collective-permute-start(bf16[384,384]{1,0:T(8,128)(2,1)S(1)} %get-tuple-element.102), channel_id=1, source_target_pairs={{0,1},{1,2},{2,3},{3,0},{4,5},{5,6},{6,7},{7,4},{8,9},{9,10},{10,1... | collective-permute-start | bytes 884744 | tf_op jit(solution)/shard_map/ppermute | solution.py:27
  369.5 11.9 %collective-permute-done.41.refs_1_ = bf16[384,384]{1,0:T(8,128)(2,1)S(1)} collective-permute-done((bf16[384,384]{1,0:T(8,128)(2,1)S(1)}, bf16[384,384]{1,0:T(8,128)(2,1)S(1)}, u32[]{:S(2)}, u32[]{:S(2)}) %collective-permute-start.41) | collective-permute-done | bytes 294944 | tf_op jit(solution)/shard_map/ppermute | solution.py:27
  381.3 20.3 %collective-permute-done.42.refs_2_ = bf16[384,384]{1,0:T(8,128)(2,1)S(1)} collective-permute-done((bf16[384,384]{1,0:T(8,128)(2,1)S(1)}, bf16[384,384]{1,0:T(8,128)(2,1)S(1)}, u32[]{:S(2)}, u32[]{:S(2)}) %collective-permute-start.42) | collective-permute-done | bytes 294944 | tf_op jit(solution)/shard_map/ppermute | solution.py:27
  403.4 14.9 %attend_back.1 = (bf16[1536,384]{1,0:T(8,128)(2,1)S(1)}, f32[2,1536,384]{2,1,0:T(8,128)S(1)}, bf16[2,1536,384]{2,1,0:T(8,128)(2,1)S(1)}) custom-call(s32[3]{0:T(128)S(1)} %copy-done.33, bf16[3,1536,384]{2,1,0:T(8,128)(2,1)S(1)} %get-tuple-element.71.query_ref.key_ref.value_ref, bf16[3,1536,384]{2,1,0:T(8,128)(2,1)S(1)} %get-tuple-element.71.query_ref.key_ref.value_ref, ...), custom_call_target="tpu_custom_call" | custom-call | flops 125829120 | bytes 344064 | tf_op jit(solution)/shard_map/attend_back/pallas_call | solution.py:517
  435.3 10.1 %project_back.1 = (bf16[1536,1152]{1,0:T(8,128)(2,1)S(1)}, bf16[4,3,128,1536]{3,2,1,0:T(8,128)(2,1)S(1)}) custom-call(bf16[1536,384]{1,0:T(8,128)(2,1)S(1)} %copy-done.25, f32[2,1536,384]{2,1,0:T(8,128)S(1)} %copy-done.16, bf16[2,1536,384]{2,1,0:T(8,128)(2,1)S(1)} %collective-permute-done.44.back_ref, f32[2,512,128]{2,1,0:T(8,128)S(1)} %copy-done.11, ...), custom_call_target="tpu_custom_call" | custom-call | flops 339738624 | bytes 1179648 | tf_op jit(solution)/shard_map/project_back/pallas_call | solution.py:577
  445.5 7.4 %outer.3 = bf16[1536,1152]{1,0:T(8,128)(2,1)S(1)} custom-call(bf16[1536,1536]{1,0:T(8,128)(2,1)S(1)} %bitcast.261, bf16[1536,1152]{1,0:T(8,128)(2,1)S(1)} %get-tuple-element.109.refs_1_), custom_call_target="tpu_custom_call" | custom-call | flops 339738624 | bytes 737280 | tf_op jit(solution)/shard_map/outer/pallas_call | solution.py:893
  454.4 6.2 %collective-permute-start.55 = (bf16[4,192,1152]{2,1,0:T(8,128)(2,1)}, bf16[4,192,1152]{2,1,0:T(8,128)(2,1)}, u32[]{:S(2)}, u32[]{:S(2)}) collective-permute-start(bf16[4,192,1152]{2,1,0:T(8,128)(2,1)} %dynamic-slice_bitcast_fusion.1), channel_id=1, source_target_pairs={{0,4},{4,0},{1,5},{5,1},{2,6},{6,2},{3,7},{7,3},{8,12},{12,8},{9,1... | collective-permute-start | bytes 5308424 | tf_op jit(solution)/shard_map/ppermute | solution.py:22
  488.4 8.5 %collective-permute-done.46 = bf16[192,1536]{1,0:T(8,128)(2,1)S(1)} collective-permute-done((bf16[192,1536]{1,0:T(8,128)(2,1)S(1)}, bf16[192,1536]{1,0:T(8,128)(2,1)S(1)}, u32[]{:S(2)}, u32[]{:S(2)}) %collective-permute-start.46) | collective-permute-done | bytes 589856 | tf_op jit(solution)/shard_map/ppermute | solution.py:22
  532.4 7.4 %collective-permute-start.64 = (f32[2,192]{1,0:T(2,128)S(1)}, f32[2,192]{1,0:T(2,128)S(1)}, u32[]{:S(2)}, u32[]{:S(2)}) collective-permute-start(f32[2,192]{1,0:T(2,128)S(1)} %pad_maximum_fusion.15), channel_id=1, source_target_pairs={{0,1},{1,2},{2,3},{3,0},{4,5},{5,6},{6,7},{7,4},{8,9},{9,10},{10,1... | collective-permute-start | bytes 4616 | tf_op jit(solution)/shard_map/ppermute | solution.py:27
  550.9 7.0 %collective-permute-start.52 = (bf16[192,384]{1,0:T(8,128)(2,1)S(1)}, bf16[192,384]{1,0:T(8,128)(2,1)S(1)}, u32[]{:S(2)}, u32[]{:S(2)}) collective-permute-start(bf16[192,384]{1,0:T(8,128)(2,1)S(1)} %get-tuple-element.222), channel_id=1, source_target_pairs={{0,1},{1,2},{2,3},{3,0},{4,5},{5,6},{6,7},{7,4},{8,9},{9,10},{10,1... | collective-permute-start | bytes 442376 | tf_op jit(solution)/shard_map/ppermute | solution.py:27
  563.6 4.2 collective-permute-done.53
  (408 shorter events, 243.9 us)
Async XLA Ops:
  7.2 134.0 %all-gather.4.cloned.1.call-start = ((), (), s32[]{:S(2)}) async-start(), calls=%async_computation.3 | async-start | bytes 5898240 | tf_op jit(solution)/shard_map/all_gather | solution.py:950
  7.9 213.3 %all-gather.6.cloned.1.call-start = ((), (), s32[]{:S(2)}) async-start(), calls=%async_computation.7 | async-start | bytes 5898240 | tf_op jit(solution)/shard_map/all_gather | solution.py:977
  8.0 18.4 %collective-permute-start.4 = (bf16[384,192]{0,1:T(8,128)(2,1)}, bf16[384,192]{0,1:T(8,128)(2,1)S(1)}, u32[]{:S(2)}, u32[]{:S(2)}) collective-permute-start(bf16[384,192]{0,1:T(8,128)(2,1)} %param.14), channel_id=1, source_target_pairs={{0,1},{1,2},{2,3},{3,0},{4,5},{5,6},{6,7},{7,4},{8,9},{9,10},{10,1... | collective-permute-start | bytes 442376 | tf_op jit(solution)/shard_map/ppermute | solution.py:27
  19.4 51.0 %collective-permute-start = (bf16[2,192]{1,0:T(2,128)(2,1)S(1)}, bf16[2,192]{1,0:T(2,128)(2,1)S(1)}, u32[]{:S(2)}, u32[]{:S(2)}) collective-permute-start(bf16[2,192]{1,0:T(2,128)(2,1)S(1)} %get-tuple-element.167), channel_id=1, source_target_pairs={{0,8},{8,0},{16,24},{24,16},{1,9},{9,1},{17,25},{25,17},{2,10},{10... | collective-permute-start | bytes 2312 | tf_op jit(solution)/shard_map/ppermute | solution.py:22
  26.3 44.6 %collective-permute-start.1 = (bf16[2,192]{1,0:T(2,128)(2,1)S(1)}, bf16[2,192]{1,0:T(2,128)(2,1)S(1)}, u32[]{:S(2)}, u32[]{:S(2)}) collective-permute-start(bf16[2,192]{1,0:T(2,128)(2,1)S(1)} %get-tuple-element.167), channel_id=1, source_target_pairs={{0,16},{8,24},{16,0},{24,8},{1,17},{9,25},{17,1},{25,9},{2,18},{10... | collective-permute-start | bytes 2312 | tf_op jit(solution)/shard_map/ppermute | solution.py:22
  32.3 19.5 %collective-permute-start.8 = (bf16[2,4,48,384]{3,2,1,0:T(8,128)(2,1)S(1)}, bf16[2,4,48,384]{3,2,1,0:T(8,128)(2,1)S(1)}, u32[]{:S(2)}, u32[]{:S(2)}) collective-permute-start(bf16[2,4,48,384]{3,2,1,0:T(8,128)(2,1)S(1)} %get-tuple-element.214), channel_id=1, source_target_pairs={{0,8},{8,0},{16,24},{24,16},{1,9},{9,1},{17,25},{25,17},{2,10},{10... | collective-permute-start | bytes 884744 | tf_op jit(solution)/shard_map/ppermute | solution.py:22
  47.2 24.8 %collective-permute-start.2 = (bf16[2,192]{1,0:T(2,128)(2,1)S(1)}, bf16[2,192]{1,0:T(2,128)(2,1)S(1)}, u32[]{:S(2)}, u32[]{:S(2)}) collective-permute-start(bf16[2,192]{1,0:T(2,128)(2,1)S(1)} %get-tuple-element.167), channel_id=1, source_target_pairs={{0,24},{8,16},{16,8},{24,0},{1,25},{9,17},{17,9},{25,1},{2,26},{10... | collective-permute-start | bytes 2312 | tf_op jit(solution)/shard_map/ppermute | solution.py:22
  65.6 57.4 %collective-permute-start.24 = (bf16[4,192,1152]{2,1,0:T(8,128)(2,1)S(1)}, bf16[4,192,1152]{2,1,0:T(8,128)(2,1)}, u32[]{:S(2)}, u32[]{:S(2)}) collective-permute-start(bf16[4,192,1152]{2,1,0:T(8,128)(2,1)S(1)} %fusion.19), channel_id=1, source_target_pairs={{0,4},{4,0},{1,5},{5,1},{2,6},{6,2},{3,7},{7,3},{8,12},{12,8},{9,1... | collective-permute-start | bytes 5308424 | tf_op jit(solution)/shard_map/ppermute | solution.py:22
  67.6 35.5 %collective-permute-start.11 = (bf16[384,1536]{1,0:T(8,128)(2,1)S(1)}, bf16[384,1536]{1,0:T(8,128)(2,1)}, u32[]{:S(2)}, u32[]{:S(2)}) collective-permute-start(bf16[384,1536]{1,0:T(8,128)(2,1)S(1)} %bitcast.266), channel_id=1, source_target_pairs={{0,8},{8,0},{16,24},{24,16},{1,9},{9,1},{17,25},{25,17},{2,10},{10... | collective-permute-start | bytes 3538952 | tf_op jit(solution)/shard_map/ppermute | solution.py:22
  68.1 354.6 %reduce-scatter.4.cloned.1.call-start = ((), (), s32[]{:S(2)}) async-start(), calls=%async_computation.4 | async-start | bytes 2949120 | tf_op jit(solution)/shard_map/reduce_scatter | solution.py:1009
  71.5 35.0 %collective-permute-start.18 = (bf16[384,1536]{1,0:T(8,128)(2,1)S(1)}, bf16[384,1536]{1,0:T(8,128)(2,1)}, u32[]{:S(2)}, u32[]{:S(2)}) collective-permute-start(bf16[384,1536]{1,0:T(8,128)(2,1)S(1)} %bitcast.267), channel_id=1, source_target_pairs={{0,16},{8,24},{16,0},{24,8},{1,17},{9,25},{17,1},{25,9},{2,18},{10... | collective-permute-start | bytes 3538952 | tf_op jit(solution)/shard_map/ppermute | solution.py:22
  107.6 17.2 %collective-permute-start.19 = (bf16[192,1536]{1,0:T(8,128)(2,1)S(1)}, bf16[192,1536]{1,0:T(8,128)(2,1)S(1)}, u32[]{:S(2)}, u32[]{:S(2)}) collective-permute-start(bf16[192,1536]{1,0:T(8,128)(2,1)S(1)} %slice.313), channel_id=1, source_target_pairs={{0,8},{8,0},{16,24},{24,16},{1,9},{9,1},{17,25},{25,17},{2,10},{10... | collective-permute-start | bytes 1769480 | tf_op jit(solution)/shard_map/ppermute | solution.py:22
  136.5 30.3 %collective-permute-start.15 = (bf16[96,1536]{1,0:T(8,128)(2,1)}, bf16[96,1536]{1,0:T(8,128)(2,1)}, u32[]{:S(2)}, u32[]{:S(2)}) collective-permute-start(bf16[96,1536]{1,0:T(8,128)(2,1)} %slice.310), channel_id=1, source_target_pairs={{0,16},{8,24},{16,0},{24,8},{1,17},{9,25},{17,1},{25,9},{2,18},{10... | collective-permute-start | bytes 884744 | tf_op jit(solution)/shard_map/ppermute | solution.py:22
  138.0 28.8 %collective-permute-start.16 = (bf16[96,1536]{1,0:T(8,128)(2,1)}, bf16[96,1536]{1,0:T(8,128)(2,1)}, u32[]{:S(2)}, u32[]{:S(2)}) collective-permute-start(bf16[96,1536]{1,0:T(8,128)(2,1)} %slice.311), channel_id=1, source_target_pairs={{0,8},{8,0},{16,24},{24,16},{1,9},{9,1},{17,25},{25,17},{2,10},{10... | collective-permute-start | bytes 884744 | tf_op jit(solution)/shard_map/ppermute | solution.py:22
  168.7 22.0 %collective-permute-start.17 = (bf16[4,192,1536]{2,1,0:T(8,128)(2,1)}, bf16[4,192,1536]{2,1,0:T(8,128)(2,1)}, u32[]{:S(2)}, u32[]{:S(2)}) collective-permute-start(bf16[4,192,1536]{2,1,0:T(8,128)(2,1)} %fusion.16), channel_id=1, source_target_pairs={{0,4},{4,0},{1,5},{5,1},{2,6},{6,2},{3,7},{7,3},{8,12},{12,8},{9,1... | collective-permute-start | bytes 7077896 | tf_op jit(solution)/shard_map/ppermute | solution.py:22
  187.6 24.6 %collective-permute-start.27 = (bf16[384,384]{1,0:T(8,128)(2,1)S(1)}, bf16[384,384]{1,0:T(8,128)(2,1)S(1)}, u32[]{:S(2)}, u32[]{:S(2)}) collective-permute-start(bf16[384,384]{1,0:T(8,128)(2,1)S(1)} %get-tuple-element.74), channel_id=1, source_target_pairs={{0,2},{1,3},{2,0},{3,1},{4,6},{5,7},{6,4},{7,5},{8,10},{9,11},{10,... | collective-permute-start | bytes 884744 | tf_op jit(solution)/shard_map/ppermute | solution.py:27
  190.3 21.9 %collective-permute-start.28 = (bf16[384,384]{1,0:T(8,128)(2,1)S(1)}, bf16[384,384]{1,0:T(8,128)(2,1)S(1)}, u32[]{:S(2)}, u32[]{:S(2)}) collective-permute-start(bf16[384,384]{1,0:T(8,128)(2,1)S(1)} %get-tuple-element.75), channel_id=1, source_target_pairs={{0,3},{1,0},{2,1},{3,2},{4,7},{5,4},{6,5},{7,6},{8,11},{9,8},{10,9... | collective-permute-start | bytes 884744 | tf_op jit(solution)/shard_map/ppermute | solution.py:27
  221.2 45.0 %collective-permute-start.29 = (bf16[4,2,4,48,1536]{4,3,2,1,0:T(8,128)(2,1)}, bf16[4,2,4,48,1536]{4,3,2,1,0:T(8,128)(2,1)}, u32[]{:S(2)}, u32[]{:S(2)}) collective-permute-start(bf16[4,2,4,48,1536]{4,3,2,1,0:T(8,128)(2,1)} %bitcast.273), channel_id=1, source_target_pairs={{0,4},{4,0},{1,5},{5,1},{2,6},{6,2},{3,7},{7,3},{8,12},{12,8},{9,1... | collective-permute-start | bytes 14155784 | tf_op jit(solution)/shard_map/ppermute | solution.py:22
  222.2 28.1 %collective-permute-start.30 = (bf16[384,1536]{1,0:T(8,128)(2,1)}, bf16[384,1536]{1,0:T(8,128)(2,1)S(1)}, u32[]{:S(2)}, u32[]{:S(2)}) collective-permute-start(bf16[384,1536]{1,0:T(8,128)(2,1)} %copy-done.31), channel_id=1, source_target_pairs={{0,8},{8,0},{16,24},{24,16},{1,9},{9,1},{17,25},{25,17},{2,10},{10... | collective-permute-start | bytes 3538952 | tf_op jit(solution)/shard_map/ppermute | solution.py:22
  223.7 28.1 %collective-permute-start.31 = (bf16[384,1536]{1,0:T(8,128)(2,1)}, bf16[384,1536]{1,0:T(8,128)(2,1)S(1)}, u32[]{:S(2)}, u32[]{:S(2)}) collective-permute-start(bf16[384,1536]{1,0:T(8,128)(2,1)} %copy-done.31), channel_id=1, source_target_pairs={{0,16},{8,24},{16,0},{24,8},{1,17},{9,25},{17,1},{25,9},{2,18},{10... | collective-permute-start | bytes 3538952 | tf_op jit(solution)/shard_map/ppermute | solution.py:22
  290.6 26.0 %collective-permute-start.35 = (bf16[2,192,1536]{2,1,0:T(8,128)(2,1)}, bf16[2,192,1536]{2,1,0:T(8,128)(2,1)S(1)}, u32[]{:S(2)}, u32[]{:S(2)}) collective-permute-start(bf16[2,192,1536]{2,1,0:T(8,128)(2,1)} %get-tuple-element.93), channel_id=1, source_target_pairs={{0,16},{8,24},{16,0},{24,8},{1,17},{9,25},{17,1},{25,9},{2,18},{10... | collective-permute-start | bytes 3538952 | tf_op jit(solution)/shard_map/ppermute | solution.py:22
  291.6 25.7 %collective-permute-start.34 = (bf16[2,192,1536]{2,1,0:T(8,128)(2,1)}, bf16[2,192,1536]{2,1,0:T(8,128)(2,1)S(1)}, u32[]{:S(2)}, u32[]{:S(2)}) collective-permute-start(bf16[2,192,1536]{2,1,0:T(8,128)(2,1)} %get-tuple-element.92), channel_id=1, source_target_pairs={{0,8},{8,0},{16,24},{24,16},{1,9},{9,1},{17,25},{25,17},{2,10},{10... | collective-permute-start | bytes 3538952 | tf_op jit(solution)/shard_map/ppermute | solution.py:22
  332.3 128.3 %reduce-scatter.6.cloned.1.call-start = ((), (), s32[]{:S(2)}) async-start(), calls=%async_computation.5 | async-start | bytes 2949120 | tf_op jit(solution)/shard_map/reduce_scatter | solution.py:1009
  332.9 235.7 %reduce-scatter.8.cloned.1.call-start = ((), (), s32[]{:S(2)}) async-start(), calls=%async_computation.6 | async-start | bytes 5898240 | tf_op jit(solution)/shard_map/reduce_scatter | solution.py:1028
  360.6 20.7 %collective-permute-start.41 = (bf16[384,384]{1,0:T(8,128)(2,1)S(1)}, bf16[384,384]{1,0:T(8,128)(2,1)S(1)}, u32[]{:S(2)}, u32[]{:S(2)}) collective-permute-start(bf16[384,384]{1,0:T(8,128)(2,1)S(1)} %get-tuple-element.102), channel_id=1, source_target_pairs={{0,1},{1,2},{2,3},{3,0},{4,5},{5,6},{6,7},{7,4},{8,9},{9,10},{10,1... | collective-permute-start | bytes 884744 | tf_op jit(solution)/shard_map/ppermute | solution.py:27
  367.1 34.6 %collective-permute-start.42 = (bf16[384,384]{1,0:T(8,128)(2,1)S(1)}, bf16[384,384]{1,0:T(8,128)(2,1)S(1)}, u32[]{:S(2)}, u32[]{:S(2)}) collective-permute-start(bf16[384,384]{1,0:T(8,128)(2,1)S(1)} %get-tuple-element.103), channel_id=1, source_target_pairs={{0,2},{1,3},{2,0},{3,1},{4,6},{5,7},{6,4},{7,5},{8,10},{9,11},{10,... | collective-permute-start | bytes 884744 | tf_op jit(solution)/shard_map/ppermute | solution.py:27
  367.5 34.1 %collective-permute-start.43 = (bf16[384,384]{1,0:T(8,128)(2,1)S(1)}, bf16[384,384]{1,0:T(8,128)(2,1)S(1)}, u32[]{:S(2)}, u32[]{:S(2)}) collective-permute-start(bf16[384,384]{1,0:T(8,128)(2,1)S(1)} %get-tuple-element.104), channel_id=1, source_target_pairs={{0,3},{1,0},{2,1},{3,2},{4,7},{5,4},{6,5},{7,6},{8,11},{9,8},{10,9... | collective-permute-start | bytes 884744 | tf_op jit(solution)/shard_map/ppermute | solution.py:27
  428.9 46.1 %collective-permute-start.40 = (bf16[2,192,1536]{2,1,0:T(8,128)(2,1)}, bf16[2,192,1536]{2,1,0:T(8,128)(2,1)}, u32[]{:S(2)}, u32[]{:S(2)}) collective-permute-start(bf16[2,192,1536]{2,1,0:T(8,128)(2,1)} %pad_maximum_fusion.4), channel_id=1, source_target_pairs={{0,16},{8,24},{16,0},{24,8},{1,17},{9,25},{17,1},{25,9},{2,18},{10... | collective-permute-start | bytes 3538952 | tf_op jit(solution)/shard_map/ppermute | solution.py:22
  431.5 45.3 %collective-permute-start.39 = (bf16[2,192,1536]{2,1,0:T(8,128)(2,1)}, bf16[2,192,1536]{2,1,0:T(8,128)(2,1)}, u32[]{:S(2)}, u32[]{:S(2)}) collective-permute-start(bf16[2,192,1536]{2,1,0:T(8,128)(2,1)} %pad_maximum_fusion.3), channel_id=1, source_target_pairs={{0,8},{8,0},{16,24},{24,16},{1,9},{9,1},{17,25},{25,17},{2,10},{10... | collective-permute-start | bytes 3538952 | tf_op jit(solution)/shard_map/ppermute | solution.py:22
  454.4 48.9 %collective-permute-start.55 = (bf16[4,192,1152]{2,1,0:T(8,128)(2,1)}, bf16[4,192,1152]{2,1,0:T(8,128)(2,1)}, u32[]{:S(2)}, u32[]{:S(2)}) collective-permute-start(bf16[4,192,1152]{2,1,0:T(8,128)(2,1)} %dynamic-slice_bitcast_fusion.1), channel_id=1, source_target_pairs={{0,4},{4,0},{1,5},{5,1},{2,6},{6,2},{3,7},{7,3},{8,12},{12,8},{9,1... | collective-permute-start | bytes 5308424 | tf_op jit(solution)/shard_map/ppermute | solution.py:22
  476.9 47.7 %collective-permute-start.47 = (bf16[4,192,1536]{2,1,0:T(8,128)(2,1)}, bf16[4,192,1536]{2,1,0:T(8,128)(2,1)}, u32[]{:S(2)}, u32[]{:S(2)}) collective-permute-start(bf16[4,192,1536]{2,1,0:T(8,128)(2,1)} %dynamic-slice_bitcast_fusion), channel_id=1, source_target_pairs={{0,4},{4,0},{1,5},{5,1},{2,6},{6,2},{3,7},{7,3},{8,12},{12,8},{9,1... | collective-permute-start | bytes 7077896 | tf_op jit(solution)/shard_map/ppermute | solution.py:22
  479.5 17.4 %collective-permute-start.46 = (bf16[192,1536]{1,0:T(8,128)(2,1)S(1)}, bf16[192,1536]{1,0:T(8,128)(2,1)S(1)}, u32[]{:S(2)}, u32[]{:S(2)}) collective-permute-start(bf16[192,1536]{1,0:T(8,128)(2,1)S(1)} %fusion.10), channel_id=1, source_target_pairs={{0,8},{8,0},{16,24},{24,16},{1,9},{9,1},{17,25},{25,17},{2,10},{10... | collective-permute-start | bytes 1769480 | tf_op jit(solution)/shard_map/ppermute | solution.py:22
  (113 other events, 1079.9 us)
Sparse Core Ops, SparseCore 0:
  9.6 93.5 all-gather.3
  105.3 102.9 all-gather.5
  332.4 68.3 reduce-scatter.3
  402.9 49.2 reduce-scatter.5
  466.4 90.3 reduce-scatter.7

commit v5 on v4

--- a/solution.py
+++ b/solution.py
@@ -294,7 +294,7 @@
     one = lambda which: pl.BlockSpec((1, length, HEAD), lambda i, h, p: (which, i, h))
     part = pl.BlockSpec((shard_len, HEAD), lambda i, h, p: (i, h))
     *parts, logs = pl.pallas_call(
-        functools.partial(attend_kernel, length // 2),
+        functools.partial(attend_kernel, length),
         grid_spec=pltpu.PrefetchScalarGridSpec(
             num_scalar_prefetch=1,
             grid=(count, heads),

time: 588 us -> 588 us (level)
  transfers between devices with their start and end apart: 72 -> 72, of which waited for: 27 -> 28; matrix products, arithmetic and copies ran while one was open for 22% -> 22% of each run, Pallas kernels for 16% -> 16%
where the time goes in v5:
time: 588 us; the launch traced here: 580 us
  waiting for transfers between devices  179 us (30%)
  Pallas kernels  119 us (20%)
  local copies, waits for them, and re-layouts  115 us (20%)
  starting transfers between devices  101 us (17%)
  other arithmetic  50.3 us (9%)
  between operations  15.5 us (3%)
    ppermute x50, waiting for transfers between devices, flip(): return lax.ppermute(shard, axis, [(i, i ^ bit) for i in range(devices)])  119 us
    ppermute x15, waiting for transfers between devices, turn(): lax.ppermute(shard, axis, [(i, (i + by) % devices) for i in range(devices)])  59 us
    ppermute x50, starting transfers between devices, flip(): return lax.ppermute(shard, axis, [(i, i ^ bit) for i in range(devices)])  53.8 us
    ppermute x15, starting transfers between devices, turn(): lax.ppermute(shard, axis, [(i, (i + by) % devices) for i in range(devices)])  42.1 us
    dynamic_update_slice x30, local copies, waits for them, and re-layouts, put(): lax.dynamic_update_slice(buffer, jnp.expand_dims(part, dim), tuple(starts))  41.7 us
    unnamed x151, local copies, waits for them, and re-layouts  31.4 us
    pallas_call x1, Pallas kernels, feed(): pl.pallas_call(functools.partial(feed_kernel, count), grid_spec=pltpu.Pre...  24.4 us
    pallas_call x1, Pallas kernels, feed_weights(): pl.pallas_call(feed_weights_kernel, grid_spec=pltpu.PrefetchScalarGridSpe...  22.3 us
  transfers between devices with their start and end apart: 72, of which 28 were waited for; matrix products, arithmetic and copies ran while one was open for 22% of the time, Pallas kernels for 16%

profile of v5, /device:TPU:0, one launch (start us, length us, event | category | flops | bytes accessed | tf_op | source)
XLA Modules:
  0.0 579.6 jit_solution(12826683203729964216)
XLA Ops:
  33.8 7.3 %collective-permute-done.20 = bf16[192,1152]{1,0:T(8,128)(2,1)S(1)} collective-permute-done((bf16[192,1152]{1,0:T(8,128)(2,1)}, bf16[192,1152]{1,0:T(8,128)(2,1)S(1)}, u32[]{:S(2)}, u32[]{:S(2)}) %collective-permute-start.20) | collective-permute-done | bytes 442400 | tf_op jit(solution)/shard_map/ppermute | solution.py:22
  42.7 4.5 collective-permute-done.22
  53.4 12.2 %collective-permute-done.9 = bf16[2,4,48,384]{3,2,1,0:T(8,128)(2,1)S(1)} collective-permute-done((bf16[2,4,48,384]{3,2,1,0:T(8,128)(2,1)S(1)}, bf16[2,4,48,384]{3,2,1,0:T(8,128)(2,1)S(1)}, u32[]{:S(2)}, u32[]{:S(2)}) %collective-permute-start.9) | collective-permute-done | bytes 294944 | tf_op jit(solution)/shard_map/ppermute | solution.py:22
  85.6 5.7 dynamic_update_slice.109
  91.4 5.8 dynamic_update_slice.110
  97.2 5.8 dynamic_update_slice.111
  109.1 10.8 %collective-permute-done.12 = bf16[192,1536]{1,0:T(8,128)(2,1)S(1)} collective-permute-done((bf16[192,1536]{1,0:T(8,128)(2,1)S(1)}, bf16[192,1536]{1,0:T(8,128)(2,1)S(1)}, u32[]{:S(2)}, u32[]{:S(2)}) %collective-permute-start.12) | collective-permute-done | bytes 589856 | tf_op jit(solution)/shard_map/ppermute | solution.py:22
  127.7 8.1 %collective-permute-done.13 = bf16[192,1536]{1,0:T(8,128)(2,1)S(1)} collective-permute-done((bf16[192,1536]{1,0:T(8,128)(2,1)S(1)}, bf16[192,1536]{1,0:T(8,128)(2,1)S(1)}, u32[]{:S(2)}, u32[]{:S(2)}) %collective-permute-start.13) | collective-permute-done | bytes 589856 | tf_op jit(solution)/shard_map/ppermute | solution.py:22
  147.7 13.5 %project.1 = (bf16[3,1536,384]{2,1,0:T(8,128)(2,1)S(1)}, bf16[1536,1536]{1,0:T(8,128)(2,1)S(1)}) custom-call(bf16[4,384,1536]{2,1,0:T(8,128)(2,1)S(1)} %copy-done.17, f32[1,1536]{1,0:T(1,128)S(1)} %squeeze.111.gain_ref, bf16[1536,1152]{1,0:T(8,128)(2,1)S(1)} %bitcast.251, f32[2,512,128]{2,1,0:T(8,128)S(1)} %copy-done.9, f32[2,512,128]{2,1,0:T(8,128)S(1)} %copy-done.12), custom_call_target="tpu_custom_call" | custom-call | flops 113246208 | bytes 491520 | tf_op jit(solution)/shard_map/project/pallas_call | solution.py:211
  171.9 10.9 %attend.1 = (bf16[384,384]{1,0:T(8,128)(2,1)S(1)}, bf16[384,384]{1,0:T(8,128)(2,1)S(1)}, bf16[384,384]{1,0:T(8,128)(2,1)S(1)}, bf16[384,384]{1,0:T(8,128)(2,1)S(1)}, f32[9,512,1]{2,1,0:T(8,128)S(1)}) custom-call(s32[3]{0:T(128)S(1)} %pad_add_fusion.place_ref, bf16[3,1536,384]{2,1,0:T(8,128)(2,1)S(1)} %get-tuple-element.71.query_ref.key_ref.value_ref, ...), custom_call_target="tpu_custom_call" | custom-call | flops 50331648 | bytes 172032 | tf_op jit(solution)/shard_map/attend/pallas_call | solution.py:296
  182.9 4.1 collective-permute-start.26
  192.0 5.7 collective-permute-done.26.refs_1_
  197.7 14.2 %collective-permute-done.27.refs_2_ = bf16[384,384]{1,0:T(8,128)(2,1)S(1)} collective-permute-done((bf16[384,384]{1,0:T(8,128)(2,1)S(1)}, bf16[384,384]{1,0:T(8,128)(2,1)S(1)}, u32[]{:S(2)}, u32[]{:S(2)}) %collective-permute-start.27) | collective-permute-done | bytes 294944 | tf_op jit(solution)/shard_map/ppermute | solution.py:27
  231.5 19.1 %collective-permute-done.30.refs_1_ = bf16[384,1536]{1,0:T(8,128)(2,1)S(1)} collective-permute-done((bf16[384,1536]{1,0:T(8,128)(2,1)}, bf16[384,1536]{1,0:T(8,128)(2,1)S(1)}, u32[]{:S(2)}, u32[]{:S(2)}) %collective-permute-start.30) | collective-permute-done | bytes 1179680 | tf_op jit(solution)/shard_map/ppermute | solution.py:22
  257.4 7.9 %collective-permute-done.32.refs_3_ = bf16[192,1536]{1,0:T(8,128)(2,1)} collective-permute-done((bf16[192,1536]{1,0:T(8,128)(2,1)S(1)}, bf16[192,1536]{1,0:T(8,128)(2,1)}, u32[]{:S(2)}, u32[]{:S(2)}) %collective-permute-start.32) | collective-permute-done | bytes 589856 | tf_op jit(solution)/shard_map/ppermute | solution.py:22
  266.6 24.4 %feed.1 = (bf16[384,1536]{1,0:T(8,128)(2,1)}, bf16[192,1536]{1,0:T(8,128)(2,1)}, bf16[192,1536]{1,0:T(8,128)(2,1)}, bf16[2,192,1536]{2,1,0:T(8,128)(2,1)}, bf16[...) custom-call(s32[3]{0:T(128)} %copy-done.32, ...), custom_call_target="tpu_custom_call" | custom-call | flops 679477248 | bytes 1843200 | tf_op jit(solution)/shard_map/feed/pallas_call | solution.py:735
  293.0 22.3 %feed_weights.1 = (bf16[4,2,4,48,1536]{4,3,2,1,0:T(8,128)(2,1)}, bf16[4,2,4,48,1536]{4,3,2,1,0:T(8,128)(2,1)}, bf16[4,384,1536]{2,1,0:T(8,128)(2,1)}) custom-call(s32[3]{0:T(128)} %copy-done.32, bf16[4,384,1536]{2,1,0:T(8,128)(2,1)} %get-tuple-element.84.rows_ref, bf16[4,384,1536]{2,1,0:T(8,128)(2,1)} %fusion.9.cot_ref, ...), custom_call_target="tpu_custom_call" | custom-call | flops 679477248 | bytes 2138112 | tf_op jit(solution)/shard_map/feed_weights/pallas_call | solution.py:846
  317.7 8.1 %collective-permute-done.36 = bf16[4,2,4,48,1536]{4,3,2,1,0:T(8,128)(2,1)S(1)} collective-permute-done((bf16[4,2,4,48,1536]{4,3,2,1,0:T(8,128)(2,1)}, bf16[4,2,4,48,1536]{4,3,2,1,0:T(8,128)(2,1)S(1)}, u32[]{:S(2)}, u32[]{:S(2)}) %collective-permute-start.36) | collective-permute-done | bytes 4718624 | tf_op jit(solution)/shard_map/ppermute | solution.py:22
  325.9 4.0 add_convert_fusion
  337.9 12.6 %collective-permute-done.38.last_x_ref = bf16[192,1536]{1,0:T(8,128)(2,1)S(1)} collective-permute-done((bf16[192,1536]{1,0:T(8,128)(2,1)S(1)}, bf16[192,1536]{1,0:T(8,128)(2,1)S(1)}, u32[]{:S(2)}, u32[]{:S(2)}) %collective-permute-start.38) | collective-permute-done | bytes 589856 | tf_op jit(solution)/shard_map/ppermute | solution.py:22
  351.5 8.4 %begin_back.1 = (f32[384,1536]{1,0:T(8,128)}, bf16[384,1536]{1,0:T(8,128)(2,1)S(1)}, bf16[384,384]{1,0:T(8,128)(2,1)S(1)}, bf16[384,384]{1,0:T(8,128)(2,1)S(1)},...) custom-call(s32[3]{0:T(128)S(1)} %copy-done.33, bf16[384,1536]{1,0:T(8,128)(2,1)S(1)} %copy-done.30, ...), custom_call_target="tpu_custom_call" | custom-call | flops 113246208 | bytes 1032192 | tf_op jit(solution)/shard_map/begin_back/pallas_call | solution.py:415
  361.0 6.0 %collective-permute-start.41 = (bf16[384,384]{1,0:T(8,128)(2,1)S(1)}, bf16[384,384]{1,0:T(8,128)(2,1)S(1)}, u32[]{:S(2)}, u32[]{:S(2)}) collective-permute-start(bf16[384,384]{1,0:T(8,128)(2,1)S(1)} %get-tuple-element.102), channel_id=1, source_target_pairs={{0,1},{1,2},{2,3},{3,0},{4,5},{5,6},{6,7},{7,4},{8,9},{9,10},{10,1... | collective-permute-start | bytes 884744 | tf_op jit(solution)/shard_map/ppermute | solution.py:27
  369.3 12.0 %collective-permute-done.41.refs_1_ = bf16[384,384]{1,0:T(8,128)(2,1)S(1)} collective-permute-done((bf16[384,384]{1,0:T(8,128)(2,1)S(1)}, bf16[384,384]{1,0:T(8,128)(2,1)S(1)}, u32[]{:S(2)}, u32[]{:S(2)}) %collective-permute-start.41) | collective-permute-done | bytes 294944 | tf_op jit(solution)/shard_map/ppermute | solution.py:27
  381.3 20.2 %collective-permute-done.42.refs_2_ = bf16[384,384]{1,0:T(8,128)(2,1)S(1)} collective-permute-done((bf16[384,384]{1,0:T(8,128)(2,1)S(1)}, bf16[384,384]{1,0:T(8,128)(2,1)S(1)}, u32[]{:S(2)}, u32[]{:S(2)}) %collective-permute-start.42) | collective-permute-done | bytes 294944 | tf_op jit(solution)/shard_map/ppermute | solution.py:27
  403.2 14.9 %attend_back.1 = (bf16[1536,384]{1,0:T(8,128)(2,1)S(1)}, f32[2,1536,384]{2,1,0:T(8,128)S(1)}, bf16[2,1536,384]{2,1,0:T(8,128)(2,1)S(1)}) custom-call(s32[3]{0:T(128)S(1)} %copy-done.33, bf16[3,1536,384]{2,1,0:T(8,128)(2,1)S(1)} %get-tuple-element.71.query_ref.key_ref.value_ref, bf16[3,1536,384]{2,1,0:T(8,128)(2,1)S(1)} %get-tuple-element.71.query_ref.key_ref.value_ref, ...), custom_call_target="tpu_custom_call" | custom-call | flops 125829120 | bytes 344064 | tf_op jit(solution)/shard_map/attend_back/pallas_call | solution.py:517
  435.2 10.1 %project_back.1 = (bf16[1536,1152]{1,0:T(8,128)(2,1)S(1)}, bf16[4,3,128,1536]{3,2,1,0:T(8,128)(2,1)S(1)}) custom-call(bf16[1536,384]{1,0:T(8,128)(2,1)S(1)} %copy-done.25, f32[2,1536,384]{2,1,0:T(8,128)S(1)} %copy-done.16, bf16[2,1536,384]{2,1,0:T(8,128)(2,1)S(1)} %collective-permute-done.44.back_ref, f32[2,512,128]{2,1,0:T(8,128)S(1)} %copy-done.11, ...), custom_call_target="tpu_custom_call" | custom-call | flops 339738624 | bytes 1179648 | tf_op jit(solution)/shard_map/project_back/pallas_call | solution.py:577
  445.3 7.4 %outer.3 = bf16[1536,1152]{1,0:T(8,128)(2,1)S(1)} custom-call(bf16[1536,1536]{1,0:T(8,128)(2,1)S(1)} %bitcast.261, bf16[1536,1152]{1,0:T(8,128)(2,1)S(1)} %get-tuple-element.109.refs_1_), custom_call_target="tpu_custom_call" | custom-call | flops 339738624 | bytes 737280 | tf_op jit(solution)/shard_map/outer/pallas_call | solution.py:893
  454.3 6.2 %collective-permute-start.55 = (bf16[4,192,1152]{2,1,0:T(8,128)(2,1)}, bf16[4,192,1152]{2,1,0:T(8,128)(2,1)}, u32[]{:S(2)}, u32[]{:S(2)}) collective-permute-start(bf16[4,192,1152]{2,1,0:T(8,128)(2,1)} %dynamic-slice_bitcast_fusion.1), channel_id=1, source_target_pairs={{0,4},{4,0},{1,5},{5,1},{2,6},{6,2},{3,7},{7,3},{8,12},{12,8},{9,1... | collective-permute-start | bytes 5308424 | tf_op jit(solution)/shard_map/ppermute | solution.py:22
  488.2 8.5 %collective-permute-done.46 = bf16[192,1536]{1,0:T(8,128)(2,1)S(1)} collective-permute-done((bf16[192,1536]{1,0:T(8,128)(2,1)S(1)}, bf16[192,1536]{1,0:T(8,128)(2,1)S(1)}, u32[]{:S(2)}, u32[]{:S(2)}) %collective-permute-start.46) | collective-permute-done | bytes 589856 | tf_op jit(solution)/shard_map/ppermute | solution.py:22
  532.2 7.3 %collective-permute-start.64 = (f32[2,192]{1,0:T(2,128)S(1)}, f32[2,192]{1,0:T(2,128)S(1)}, u32[]{:S(2)}, u32[]{:S(2)}) collective-permute-start(f32[2,192]{1,0:T(2,128)S(1)} %pad_maximum_fusion.15), channel_id=1, source_target_pairs={{0,1},{1,2},{2,3},{3,0},{4,5},{5,6},{6,7},{7,4},{8,9},{9,10},{10,1... | collective-permute-start | bytes 4616 | tf_op jit(solution)/shard_map/ppermute | solution.py:27
  550.8 6.9 %collective-permute-start.52 = (bf16[192,384]{1,0:T(8,128)(2,1)S(1)}, bf16[192,384]{1,0:T(8,128)(2,1)S(1)}, u32[]{:S(2)}, u32[]{:S(2)}) collective-permute-start(bf16[192,384]{1,0:T(8,128)(2,1)S(1)} %get-tuple-element.222), channel_id=1, source_target_pairs={{0,1},{1,2},{2,3},{3,0},{4,5},{5,6},{6,7},{7,4},{8,9},{9,10},{10,1... | collective-permute-start | bytes 442376 | tf_op jit(solution)/shard_map/ppermute | solution.py:27
  563.6 4.1 collective-permute-done.53
  (408 shorter events, 245.0 us)
Async XLA Ops:
  7.2 134.0 %all-gather.4.cloned.1.call-start = ((), (), s32[]{:S(2)}) async-start(), calls=%async_computation.3 | async-start | bytes 5898240 | tf_op jit(solution)/shard_map/all_gather | solution.py:950
  7.9 212.9 %all-gather.6.cloned.1.call-start = ((), (), s32[]{:S(2)}) async-start(), calls=%async_computation.7 | async-start | bytes 5898240 | tf_op jit(solution)/shard_map/all_gather | solution.py:977
  8.0 18.4 %collective-permute-start.4 = (bf16[384,192]{0,1:T(8,128)(2,1)}, bf16[384,192]{0,1:T(8,128)(2,1)S(1)}, u32[]{:S(2)}, u32[]{:S(2)}) collective-permute-start(bf16[384,192]{0,1:T(8,128)(2,1)} %param.14), channel_id=1, source_target_pairs={{0,1},{1,2},{2,3},{3,0},{4,5},{5,6},{6,7},{7,4},{8,9},{9,10},{10,1... | collective-permute-start | bytes 442376 | tf_op jit(solution)/shard_map/ppermute | solution.py:27
  19.4 51.0 %collective-permute-start = (bf16[2,192]{1,0:T(2,128)(2,1)S(1)}, bf16[2,192]{1,0:T(2,128)(2,1)S(1)}, u32[]{:S(2)}, u32[]{:S(2)}) collective-permute-start(bf16[2,192]{1,0:T(2,128)(2,1)S(1)} %get-tuple-element.167), channel_id=1, source_target_pairs={{0,8},{8,0},{16,24},{24,16},{1,9},{9,1},{17,25},{25,17},{2,10},{10... | collective-permute-start | bytes 2312 | tf_op jit(solution)/shard_map/ppermute | solution.py:22
  26.3 44.6 %collective-permute-start.1 = (bf16[2,192]{1,0:T(2,128)(2,1)S(1)}, bf16[2,192]{1,0:T(2,128)(2,1)S(1)}, u32[]{:S(2)}, u32[]{:S(2)}) collective-permute-start(bf16[2,192]{1,0:T(2,128)(2,1)S(1)} %get-tuple-element.167), channel_id=1, source_target_pairs={{0,16},{8,24},{16,0},{24,8},{1,17},{9,25},{17,1},{25,9},{2,18},{10... | collective-permute-start | bytes 2312 | tf_op jit(solution)/shard_map/ppermute | solution.py:22
  32.3 19.5 %collective-permute-start.8 = (bf16[2,4,48,384]{3,2,1,0:T(8,128)(2,1)S(1)}, bf16[2,4,48,384]{3,2,1,0:T(8,128)(2,1)S(1)}, u32[]{:S(2)}, u32[]{:S(2)}) collective-permute-start(bf16[2,4,48,384]{3,2,1,0:T(8,128)(2,1)S(1)} %get-tuple-element.214), channel_id=1, source_target_pairs={{0,8},{8,0},{16,24},{24,16},{1,9},{9,1},{17,25},{25,17},{2,10},{10... | collective-permute-start | bytes 884744 | tf_op jit(solution)/shard_map/ppermute | solution.py:22
  47.2 24.8 %collective-permute-start.2 = (bf16[2,192]{1,0:T(2,128)(2,1)S(1)}, bf16[2,192]{1,0:T(2,128)(2,1)S(1)}, u32[]{:S(2)}, u32[]{:S(2)}) collective-permute-start(bf16[2,192]{1,0:T(2,128)(2,1)S(1)} %get-tuple-element.167), channel_id=1, source_target_pairs={{0,24},{8,16},{16,8},{24,0},{1,25},{9,17},{17,9},{25,1},{2,26},{10... | collective-permute-start | bytes 2312 | tf_op jit(solution)/shard_map/ppermute | solution.py:22
  65.6 57.4 %collective-permute-start.24 = (bf16[4,192,1152]{2,1,0:T(8,128)(2,1)S(1)}, bf16[4,192,1152]{2,1,0:T(8,128)(2,1)}, u32[]{:S(2)}, u32[]{:S(2)}) collective-permute-start(bf16[4,192,1152]{2,1,0:T(8,128)(2,1)S(1)} %fusion.19), channel_id=1, source_target_pairs={{0,4},{4,0},{1,5},{5,1},{2,6},{6,2},{3,7},{7,3},{8,12},{12,8},{9,1... | collective-permute-start | bytes 5308424 | tf_op jit(solution)/shard_map/ppermute | solution.py:22
  67.6 35.5 %collective-permute-start.11 = (bf16[384,1536]{1,0:T(8,128)(2,1)S(1)}, bf16[384,1536]{1,0:T(8,128)(2,1)}, u32[]{:S(2)}, u32[]{:S(2)}) collective-permute-start(bf16[384,1536]{1,0:T(8,128)(2,1)S(1)} %bitcast.266), channel_id=1, source_target_pairs={{0,8},{8,0},{16,24},{24,16},{1,9},{9,1},{17,25},{25,17},{2,10},{10... | collective-permute-start | bytes 3538952 | tf_op jit(solution)/shard_map/ppermute | solution.py:22
  68.1 354.5 %reduce-scatter.4.cloned.1.call-start = ((), (), s32[]{:S(2)}) async-start(), calls=%async_computation.4 | async-start | bytes 2949120 | tf_op jit(solution)/shard_map/reduce_scatter | solution.py:1009
  71.5 35.0 %collective-permute-start.18 = (bf16[384,1536]{1,0:T(8,128)(2,1)S(1)}, bf16[384,1536]{1,0:T(8,128)(2,1)}, u32[]{:S(2)}, u32[]{:S(2)}) collective-permute-start(bf16[384,1536]{1,0:T(8,128)(2,1)S(1)} %bitcast.267), channel_id=1, source_target_pairs={{0,16},{8,24},{16,0},{24,8},{1,17},{9,25},{17,1},{25,9},{2,18},{10... | collective-permute-start | bytes 3538952 | tf_op jit(solution)/shard_map/ppermute | solution.py:22
  107.6 17.2 %collective-permute-start.19 = (bf16[192,1536]{1,0:T(8,128)(2,1)S(1)}, bf16[192,1536]{1,0:T(8,128)(2,1)S(1)}, u32[]{:S(2)}, u32[]{:S(2)}) collective-permute-start(bf16[192,1536]{1,0:T(8,128)(2,1)S(1)} %slice.313), channel_id=1, source_target_pairs={{0,8},{8,0},{16,24},{24,16},{1,9},{9,1},{17,25},{25,17},{2,10},{10... | collective-permute-start | bytes 1769480 | tf_op jit(solution)/shard_map/ppermute | solution.py:22
  136.5 30.3 %collective-permute-start.15 = (bf16[96,1536]{1,0:T(8,128)(2,1)}, bf16[96,1536]{1,0:T(8,128)(2,1)}, u32[]{:S(2)}, u32[]{:S(2)}) collective-permute-start(bf16[96,1536]{1,0:T(8,128)(2,1)} %slice.310), channel_id=1, source_target_pairs={{0,16},{8,24},{16,0},{24,8},{1,17},{9,25},{17,1},{25,9},{2,18},{10... | collective-permute-start | bytes 884744 | tf_op jit(solution)/shard_map/ppermute | solution.py:22
  138.0 28.8 %collective-permute-start.16 = (bf16[96,1536]{1,0:T(8,128)(2,1)}, bf16[96,1536]{1,0:T(8,128)(2,1)}, u32[]{:S(2)}, u32[]{:S(2)}) collective-permute-start(bf16[96,1536]{1,0:T(8,128)(2,1)} %slice.311), channel_id=1, source_target_pairs={{0,8},{8,0},{16,24},{24,16},{1,9},{9,1},{17,25},{25,17},{2,10},{10... | collective-permute-start | bytes 884744 | tf_op jit(solution)/shard_map/ppermute | solution.py:22
  168.7 21.4 %collective-permute-start.17 = (bf16[4,192,1536]{2,1,0:T(8,128)(2,1)}, bf16[4,192,1536]{2,1,0:T(8,128)(2,1)}, u32[]{:S(2)}, u32[]{:S(2)}) collective-permute-start(bf16[4,192,1536]{2,1,0:T(8,128)(2,1)} %fusion.16), channel_id=1, source_target_pairs={{0,4},{4,0},{1,5},{5,1},{2,6},{6,2},{3,7},{7,3},{8,12},{12,8},{9,1... | collective-permute-start | bytes 7077896 | tf_op jit(solution)/shard_map/ppermute | solution.py:22
  187.0 24.9 %collective-permute-start.27 = (bf16[384,384]{1,0:T(8,128)(2,1)S(1)}, bf16[384,384]{1,0:T(8,128)(2,1)S(1)}, u32[]{:S(2)}, u32[]{:S(2)}) collective-permute-start(bf16[384,384]{1,0:T(8,128)(2,1)S(1)} %get-tuple-element.74), channel_id=1, source_target_pairs={{0,2},{1,3},{2,0},{3,1},{4,6},{5,7},{6,4},{7,5},{8,10},{9,11},{10,... | collective-permute-start | bytes 884744 | tf_op jit(solution)/shard_map/ppermute | solution.py:27
  189.6 22.2 %collective-permute-start.28 = (bf16[384,384]{1,0:T(8,128)(2,1)S(1)}, bf16[384,384]{1,0:T(8,128)(2,1)S(1)}, u32[]{:S(2)}, u32[]{:S(2)}) collective-permute-start(bf16[384,384]{1,0:T(8,128)(2,1)S(1)} %get-tuple-element.75), channel_id=1, source_target_pairs={{0,3},{1,0},{2,1},{3,2},{4,7},{5,4},{6,5},{7,6},{8,11},{9,8},{10,9... | collective-permute-start | bytes 884744 | tf_op jit(solution)/shard_map/ppermute | solution.py:27
  220.8 45.8 %collective-permute-start.29 = (bf16[4,2,4,48,1536]{4,3,2,1,0:T(8,128)(2,1)}, bf16[4,2,4,48,1536]{4,3,2,1,0:T(8,128)(2,1)}, u32[]{:S(2)}, u32[]{:S(2)}) collective-permute-start(bf16[4,2,4,48,1536]{4,3,2,1,0:T(8,128)(2,1)} %bitcast.273), channel_id=1, source_target_pairs={{0,4},{4,0},{1,5},{5,1},{2,6},{6,2},{3,7},{7,3},{8,12},{12,8},{9,1... | collective-permute-start | bytes 14155784 | tf_op jit(solution)/shard_map/ppermute | solution.py:22
  222.5 28.1 %collective-permute-start.30 = (bf16[384,1536]{1,0:T(8,128)(2,1)}, bf16[384,1536]{1,0:T(8,128)(2,1)S(1)}, u32[]{:S(2)}, u32[]{:S(2)}) collective-permute-start(bf16[384,1536]{1,0:T(8,128)(2,1)} %copy-done.31), channel_id=1, source_target_pairs={{0,8},{8,0},{16,24},{24,16},{1,9},{9,1},{17,25},{25,17},{2,10},{10... | collective-permute-start | bytes 3538952 | tf_op jit(solution)/shard_map/ppermute | solution.py:22
  224.1 28.2 %collective-permute-start.31 = (bf16[384,1536]{1,0:T(8,128)(2,1)}, bf16[384,1536]{1,0:T(8,128)(2,1)S(1)}, u32[]{:S(2)}, u32[]{:S(2)}) collective-permute-start(bf16[384,1536]{1,0:T(8,128)(2,1)} %copy-done.31), channel_id=1, source_target_pairs={{0,16},{8,24},{16,0},{24,8},{1,17},{9,25},{17,1},{25,9},{2,18},{10... | collective-permute-start | bytes 3538952 | tf_op jit(solution)/shard_map/ppermute | solution.py:22
  291.0 26.0 %collective-permute-start.35 = (bf16[2,192,1536]{2,1,0:T(8,128)(2,1)}, bf16[2,192,1536]{2,1,0:T(8,128)(2,1)S(1)}, u32[]{:S(2)}, u32[]{:S(2)}) collective-permute-start(bf16[2,192,1536]{2,1,0:T(8,128)(2,1)} %get-tuple-element.93), channel_id=1, source_target_pairs={{0,16},{8,24},{16,0},{24,8},{1,17},{9,25},{17,1},{25,9},{2,18},{10... | collective-permute-start | bytes 3538952 | tf_op jit(solution)/shard_map/ppermute | solution.py:22
  292.0 25.7 %collective-permute-start.34 = (bf16[2,192,1536]{2,1,0:T(8,128)(2,1)}, bf16[2,192,1536]{2,1,0:T(8,128)(2,1)S(1)}, u32[]{:S(2)}, u32[]{:S(2)}) collective-permute-start(bf16[2,192,1536]{2,1,0:T(8,128)(2,1)} %get-tuple-element.92), channel_id=1, source_target_pairs={{0,8},{8,0},{16,24},{24,16},{1,9},{9,1},{17,25},{25,17},{2,10},{10... | collective-permute-start | bytes 3538952 | tf_op jit(solution)/shard_map/ppermute | solution.py:22
  332.7 127.7 %reduce-scatter.6.cloned.1.call-start = ((), (), s32[]{:S(2)}) async-start(), calls=%async_computation.5 | async-start | bytes 2949120 | tf_op jit(solution)/shard_map/reduce_scatter | solution.py:1009
  333.2 235.2 %reduce-scatter.8.cloned.1.call-start = ((), (), s32[]{:S(2)}) async-start(), calls=%async_computation.6 | async-start | bytes 5898240 | tf_op jit(solution)/shard_map/reduce_scatter | solution.py:1028
  361.0 20.4 %collective-permute-start.41 = (bf16[384,384]{1,0:T(8,128)(2,1)S(1)}, bf16[384,384]{1,0:T(8,128)(2,1)S(1)}, u32[]{:S(2)}, u32[]{:S(2)}) collective-permute-start(bf16[384,384]{1,0:T(8,128)(2,1)S(1)} %get-tuple-element.102), channel_id=1, source_target_pairs={{0,1},{1,2},{2,3},{3,0},{4,5},{5,6},{6,7},{7,4},{8,9},{9,10},{10,1... | collective-permute-start | bytes 884744 | tf_op jit(solution)/shard_map/ppermute | solution.py:27
  366.9 34.6 %collective-permute-start.42 = (bf16[384,384]{1,0:T(8,128)(2,1)S(1)}, bf16[384,384]{1,0:T(8,128)(2,1)S(1)}, u32[]{:S(2)}, u32[]{:S(2)}) collective-permute-start(bf16[384,384]{1,0:T(8,128)(2,1)S(1)} %get-tuple-element.103), channel_id=1, source_target_pairs={{0,2},{1,3},{2,0},{3,1},{4,6},{5,7},{6,4},{7,5},{8,10},{9,11},{10,... | collective-permute-start | bytes 884744 | tf_op jit(solution)/shard_map/ppermute | solution.py:27
  367.5 34.0 %collective-permute-start.43 = (bf16[384,384]{1,0:T(8,128)(2,1)S(1)}, bf16[384,384]{1,0:T(8,128)(2,1)S(1)}, u32[]{:S(2)}, u32[]{:S(2)}) collective-permute-start(bf16[384,384]{1,0:T(8,128)(2,1)S(1)} %get-tuple-element.104), channel_id=1, source_target_pairs={{0,3},{1,0},{2,1},{3,2},{4,7},{5,4},{6,5},{7,6},{8,11},{9,8},{10,9... | collective-permute-start | bytes 884744 | tf_op jit(solution)/shard_map/ppermute | solution.py:27
  428.8 46.1 %collective-permute-start.40 = (bf16[2,192,1536]{2,1,0:T(8,128)(2,1)}, bf16[2,192,1536]{2,1,0:T(8,128)(2,1)}, u32[]{:S(2)}, u32[]{:S(2)}) collective-permute-start(bf16[2,192,1536]{2,1,0:T(8,128)(2,1)} %pad_maximum_fusion.4), channel_id=1, source_target_pairs={{0,16},{8,24},{16,0},{24,8},{1,17},{9,25},{17,1},{25,9},{2,18},{10... | collective-permute-start | bytes 3538952 | tf_op jit(solution)/shard_map/ppermute | solution.py:22
  431.4 45.3 %collective-permute-start.39 = (bf16[2,192,1536]{2,1,0:T(8,128)(2,1)}, bf16[2,192,1536]{2,1,0:T(8,128)(2,1)}, u32[]{:S(2)}, u32[]{:S(2)}) collective-permute-start(bf16[2,192,1536]{2,1,0:T(8,128)(2,1)} %pad_maximum_fusion.3), channel_id=1, source_target_pairs={{0,8},{8,0},{16,24},{24,16},{1,9},{9,1},{17,25},{25,17},{2,10},{10... | collective-permute-start | bytes 3538952 | tf_op jit(solution)/shard_map/ppermute | solution.py:22
  454.3 48.8 %collective-permute-start.55 = (bf16[4,192,1152]{2,1,0:T(8,128)(2,1)}, bf16[4,192,1152]{2,1,0:T(8,128)(2,1)}, u32[]{:S(2)}, u32[]{:S(2)}) collective-permute-start(bf16[4,192,1152]{2,1,0:T(8,128)(2,1)} %dynamic-slice_bitcast_fusion.1), channel_id=1, source_target_pairs={{0,4},{4,0},{1,5},{5,1},{2,6},{6,2},{3,7},{7,3},{8,12},{12,8},{9,1... | collective-permute-start | bytes 5308424 | tf_op jit(solution)/shard_map/ppermute | solution.py:22
  476.7 47.7 %collective-permute-start.47 = (bf16[4,192,1536]{2,1,0:T(8,128)(2,1)}, bf16[4,192,1536]{2,1,0:T(8,128)(2,1)}, u32[]{:S(2)}, u32[]{:S(2)}) collective-permute-start(bf16[4,192,1536]{2,1,0:T(8,128)(2,1)} %dynamic-slice_bitcast_fusion), channel_id=1, source_target_pairs={{0,4},{4,0},{1,5},{5,1},{2,6},{6,2},{3,7},{7,3},{8,12},{12,8},{9,1... | collective-permute-start | bytes 7077896 | tf_op jit(solution)/shard_map/ppermute | solution.py:22
  479.4 17.4 %collective-permute-start.46 = (bf16[192,1536]{1,0:T(8,128)(2,1)S(1)}, bf16[192,1536]{1,0:T(8,128)(2,1)S(1)}, u32[]{:S(2)}, u32[]{:S(2)}) collective-permute-start(bf16[192,1536]{1,0:T(8,128)(2,1)S(1)} %fusion.10), channel_id=1, source_target_pairs={{0,8},{8,0},{16,24},{24,16},{1,9},{9,1},{17,25},{25,17},{2,10},{10... | collective-permute-start | bytes 1769480 | tf_op jit(solution)/shard_map/ppermute | solution.py:22
  (113 other events, 1077.3 us)
Sparse Core Ops, SparseCore 0:
  9.6 93.5 all-gather.3
  105.3 102.1 all-gather.5
  332.8 67.6 reduce-scatter.3
  402.6 49.5 reduce-scatter.5
  466.2 90.5 reduce-scatter.7

commit v6 on v5

--- a/solution.py
+++ b/solution.py
@@ -478,11 +478,11 @@
             grad_key = contract(own_low, query, 0, 0) * factor
             grad_value = contract(own.astype(BF), grad, 0, 0)
             if first == length - strip:
-                own_out[0] = grad_key
-                own_out[1] = grad_value
+                own_out[0] = grad_key.astype(BF)
+                own_out[1] = grad_value.astype(BF)
             else:
-                own_out[0, :end] += grad_key
-                own_out[1, :end] += grad_value
+                own_out[0, :end] += grad_key.astype(BF)
+                own_out[1, :end] += grad_value.astype(BF)
             if late:
                 early_low = (early * (early_grad - inner)).astype(BF)
                 grad_query = grad_query + contract(early_low, early_ref[0], 1, 0)
@@ -515,7 +515,7 @@
     pair = pl.BlockSpec((2, length, HEAD), lambda i, h, p: (0, i, h))
     table = pl.BlockSpec((1, length, HEAD), lambda i, h, p: (0, 0, 0))
     return pl.pallas_call(
-        functools.partial(attend_back_kernel, length // 2),
+        functools.partial(attend_back_kernel, length),
         grid_spec=pltpu.PrefetchScalarGridSpec(
             num_scalar_prefetch=1,
             grid=(count, heads),
@@ -534,7 +534,7 @@
         ),
         out_shape=[
             jax.ShapeDtypeStruct((rows, cols), BF),
-            jax.ShapeDtypeStruct((2, rows, cols), F32),
+            jax.ShapeDtypeStruct((2, rows, cols), BF),
             jax.ShapeDtypeStruct((2, rows, cols), BF),
         ],
         compiler_params=pltpu.CompilerParams(vmem_limit_bytes=32 * MIB),
@@ -555,13 +555,13 @@
     @pl.when(pl.program_id(1) == 0)
     def _():
         low_ref[:, :cols] = query_ref[...]
-        keys = own_ref[0] + back_ref[0].astype(F32)
+        keys = own_ref[0].astype(F32) + back_ref[0].astype(F32)
         cosine, sine = cos_ref[0], -sin_ref[0]
         for head in range(cols // HEAD):
             part = slice(head * HEAD, (head + 1) * HEAD)
             into = slice(cols + head * HEAD, cols + (head + 1) * HEAD)
             low_ref[:, into] = turned(keys[:, part], cosine, sine).astype(BF)
-        low_ref[:, 2 * cols :] = (own_ref[1] + back_ref[1].astype(F32)).astype(BF)
+        low_ref[:, 2 * cols :] = (own_ref[1].astype(F32) + back_ref[1].astype(F32)).astype(BF)
 
     result = contract(low_ref[...], weight_ref[...], 1, 1).astype(BF)
     out_ref[...] = result.reshape(out_ref.shape)

time: 588 us -> 588 us (level)
  transfers between devices with their start and end apart: 72 -> 72, of which waited for: 28 -> 27; matrix products, arithmetic and copies ran while one was open for 22% -> 22% of each run, Pallas kernels for 16% -> 16%
where the time goes in v6:
time: 588 us; the launch traced here: 580 us
  waiting for transfers between devices  179 us (30%)
  Pallas kernels  120 us (20%)
  local copies, waits for them, and re-layouts  116 us (20%)
  starting transfers between devices  99.2 us (17%)
  other arithmetic  50.3 us (9%)
  between operations  15.5 us (3%)
    ppermute x50, waiting for transfers between devices, flip(): return lax.ppermute(shard, axis, [(i, i ^ bit) for i in range(devices)])  119 us
    ppermute x15, waiting for transfers between devices, turn(): lax.ppermute(shard, axis, [(i, (i + by) % devices) for i in range(devices)])  59 us
    ppermute x50, starting transfers between devices, flip(): return lax.ppermute(shard, axis, [(i, i ^ bit) for i in range(devices)])  52.6 us
    ppermute x15, starting transfers between devices, turn(): lax.ppermute(shard, axis, [(i, (i + by) % devices) for i in range(devices)])  42 us
    dynamic_update_slice x30, local copies, waits for them, and re-layouts, put(): lax.dynamic_update_slice(buffer, jnp.expand_dims(part, dim), tuple(starts))  41.7 us
    unnamed x151, local copies, waits for them, and re-layouts  32.9 us
    pallas_call x1, Pallas kernels, feed(): pl.pallas_call(functools.partial(feed_kernel, count), grid_spec=pltpu.Pre...  24.4 us
    pallas_call x1, Pallas kernels, feed_weights(): pl.pallas_call(feed_weights_kernel, grid_spec=pltpu.PrefetchScalarGridSpe...  22.3 us
  transfers between devices with their start and end apart: 72, of which 27 were waited for; matrix products, arithmetic and copies ran while one was open for 22% of the time, Pallas kernels for 16%

profile of v6, /device:TPU:0, one launch (start us, length us, event | category | flops | bytes accessed | tf_op | source)
XLA Modules:
  0.0 580.3 jit_solution(341367454269782741)
XLA Ops:
  33.8 7.3 %collective-permute-done.20 = bf16[192,1152]{1,0:T(8,128)(2,1)S(1)} collective-permute-done((bf16[192,1152]{1,0:T(8,128)(2,1)}, bf16[192,1152]{1,0:T(8,128)(2,1)S(1)}, u32[]{:S(2)}, u32[]{:S(2)}) %collective-permute-start.20) | collective-permute-done | bytes 442400 | tf_op jit(solution)/shard_map/ppermute | solution.py:22
  42.7 4.5 collective-permute-done.22
  53.4 12.2 %collective-permute-done.9 = bf16[2,4,48,384]{3,2,1,0:T(8,128)(2,1)S(1)} collective-permute-done((bf16[2,4,48,384]{3,2,1,0:T(8,128)(2,1)S(1)}, bf16[2,4,48,384]{3,2,1,0:T(8,128)(2,1)S(1)}, u32[]{:S(2)}, u32[]{:S(2)}) %collective-permute-start.9) | collective-permute-done | bytes 294944 | tf_op jit(solution)/shard_map/ppermute | solution.py:22
  85.6 5.7 dynamic_update_slice.109
  91.4 5.8 dynamic_update_slice.110
  97.2 5.8 dynamic_update_slice.111
  109.1 10.8 %collective-permute-done.12 = bf16[192,1536]{1,0:T(8,128)(2,1)S(1)} collective-permute-done((bf16[192,1536]{1,0:T(8,128)(2,1)S(1)}, bf16[192,1536]{1,0:T(8,128)(2,1)S(1)}, u32[]{:S(2)}, u32[]{:S(2)}) %collective-permute-start.12) | collective-permute-done | bytes 589856 | tf_op jit(solution)/shard_map/ppermute | solution.py:22
  127.7 8.1 %collective-permute-done.13 = bf16[192,1536]{1,0:T(8,128)(2,1)S(1)} collective-permute-done((bf16[192,1536]{1,0:T(8,128)(2,1)S(1)}, bf16[192,1536]{1,0:T(8,128)(2,1)S(1)}, u32[]{:S(2)}, u32[]{:S(2)}) %collective-permute-start.13) | collective-permute-done | bytes 589856 | tf_op jit(solution)/shard_map/ppermute | solution.py:22
  147.7 13.5 %project.1 = (bf16[3,1536,384]{2,1,0:T(8,128)(2,1)S(1)}, bf16[1536,1536]{1,0:T(8,128)(2,1)S(1)}) custom-call(bf16[4,384,1536]{2,1,0:T(8,128)(2,1)S(1)} %copy-done.15, f32[1,1536]{1,0:T(1,128)S(1)} %squeeze.111.gain_ref, bf16[1536,1152]{1,0:T(8,128)(2,1)S(1)} %bitcast.251, f32[2,512,128]{2,1,0:T(8,128)S(1)} %copy-done.9, f32[2,512,128]{2,1,0:T(8,128)S(1)} %copy-done.12), custom_call_target="tpu_custom_call" | custom-call | flops 113246208 | bytes 491520 | tf_op jit(solution)/shard_map/project/pallas_call | solution.py:211
  171.9 10.9 %attend.1 = (bf16[384,384]{1,0:T(8,128)(2,1)S(1)}, bf16[384,384]{1,0:T(8,128)(2,1)S(1)}, bf16[384,384]{1,0:T(8,128)(2,1)S(1)}, bf16[384,384]{1,0:T(8,128)(2,1)S(1)}, f32[9,512,1]{2,1,0:T(8,128)S(1)}) custom-call(s32[3]{0:T(128)S(1)} %pad_add_fusion.place_ref, bf16[3,1536,384]{2,1,0:T(8,128)(2,1)S(1)} %get-tuple-element.71.query_ref.key_ref.value_ref, ...), custom_call_target="tpu_custom_call" | custom-call | flops 50331648 | bytes 172032 | tf_op jit(solution)/shard_map/attend/pallas_call | solution.py:296
  182.9 4.1 collective-permute-start.26
  192.0 5.7 collective-permute-done.26.refs_1_
  197.7 14.2 %collective-permute-done.27.refs_2_ = bf16[384,384]{1,0:T(8,128)(2,1)S(1)} collective-permute-done((bf16[384,384]{1,0:T(8,128)(2,1)S(1)}, bf16[384,384]{1,0:T(8,128)(2,1)S(1)}, u32[]{:S(2)}, u32[]{:S(2)}) %collective-permute-start.27) | collective-permute-done | bytes 294944 | tf_op jit(solution)/shard_map/ppermute | solution.py:27
  231.5 19.1 %collective-permute-done.30.refs_1_ = bf16[384,1536]{1,0:T(8,128)(2,1)S(1)} collective-permute-done((bf16[384,1536]{1,0:T(8,128)(2,1)}, bf16[384,1536]{1,0:T(8,128)(2,1)S(1)}, u32[]{:S(2)}, u32[]{:S(2)}) %collective-permute-start.30) | collective-permute-done | bytes 1179680 | tf_op jit(solution)/shard_map/ppermute | solution.py:22
  257.4 7.9 %collective-permute-done.32.refs_3_ = bf16[192,1536]{1,0:T(8,128)(2,1)} collective-permute-done((bf16[192,1536]{1,0:T(8,128)(2,1)S(1)}, bf16[192,1536]{1,0:T(8,128)(2,1)}, u32[]{:S(2)}, u32[]{:S(2)}) %collective-permute-start.32) | collective-permute-done | bytes 589856 | tf_op jit(solution)/shard_map/ppermute | solution.py:22
  266.6 24.4 %feed.1 = (bf16[384,1536]{1,0:T(8,128)(2,1)}, bf16[192,1536]{1,0:T(8,128)(2,1)}, bf16[192,1536]{1,0:T(8,128)(2,1)}, bf16[2,192,1536]{2,1,0:T(8,128)(2,1)}, bf16[...) custom-call(s32[3]{0:T(128)} %copy-done.32, ...), custom_call_target="tpu_custom_call" | custom-call | flops 679477248 | bytes 1843200 | tf_op jit(solution)/shard_map/feed/pallas_call | solution.py:735
  293.0 22.3 %feed_weights.1 = (bf16[4,2,4,48,1536]{4,3,2,1,0:T(8,128)(2,1)}, bf16[4,2,4,48,1536]{4,3,2,1,0:T(8,128)(2,1)}, bf16[4,384,1536]{2,1,0:T(8,128)(2,1)}) custom-call(s32[3]{0:T(128)} %copy-done.32, bf16[4,384,1536]{2,1,0:T(8,128)(2,1)} %get-tuple-element.84.rows_ref, bf16[4,384,1536]{2,1,0:T(8,128)(2,1)} %fusion.9.cot_ref, ...), custom_call_target="tpu_custom_call" | custom-call | flops 679477248 | bytes 2138112 | tf_op jit(solution)/shard_map/feed_weights/pallas_call | solution.py:846
  317.7 8.1 %collective-permute-done.36 = bf16[4,2,4,48,1536]{4,3,2,1,0:T(8,128)(2,1)S(1)} collective-permute-done((bf16[4,2,4,48,1536]{4,3,2,1,0:T(8,128)(2,1)}, bf16[4,2,4,48,1536]{4,3,2,1,0:T(8,128)(2,1)S(1)}, u32[]{:S(2)}, u32[]{:S(2)}) %collective-permute-start.36) | collective-permute-done | bytes 4718624 | tf_op jit(solution)/shard_map/ppermute | solution.py:22
  325.9 4.0 add_convert_fusion
  337.9 12.6 %collective-permute-done.38.last_x_ref = bf16[192,1536]{1,0:T(8,128)(2,1)S(1)} collective-permute-done((bf16[192,1536]{1,0:T(8,128)(2,1)S(1)}, bf16[192,1536]{1,0:T(8,128)(2,1)S(1)}, u32[]{:S(2)}, u32[]{:S(2)}) %collective-permute-start.38) | collective-permute-done | bytes 589856 | tf_op jit(solution)/shard_map/ppermute | solution.py:22
  351.5 8.4 %begin_back.1 = (f32[384,1536]{1,0:T(8,128)}, bf16[384,1536]{1,0:T(8,128)(2,1)S(1)}, bf16[384,384]{1,0:T(8,128)(2,1)S(1)}, bf16[384,384]{1,0:T(8,128)(2,1)S(1)},...) custom-call(s32[3]{0:T(128)S(1)} %copy-done.33, bf16[384,1536]{1,0:T(8,128)(2,1)S(1)} %copy-done.30, ...), custom_call_target="tpu_custom_call" | custom-call | flops 113246208 | bytes 1032192 | tf_op jit(solution)/shard_map/begin_back/pallas_call | solution.py:415
  361.0 6.0 %collective-permute-start.41 = (bf16[384,384]{1,0:T(8,128)(2,1)S(1)}, bf16[384,384]{1,0:T(8,128)(2,1)S(1)}, u32[]{:S(2)}, u32[]{:S(2)}) collective-permute-start(bf16[384,384]{1,0:T(8,128)(2,1)S(1)} %get-tuple-element.102), channel_id=1, source_target_pairs={{0,1},{1,2},{2,3},{3,0},{4,5},{5,6},{6,7},{7,4},{8,9},{9,10},{10,1... | collective-permute-start | bytes 884744 | tf_op jit(solution)/shard_map/ppermute | solution.py:27
  369.3 12.0 %collective-permute-done.41.refs_1_ = bf16[384,384]{1,0:T(8,128)(2,1)S(1)} collective-permute-done((bf16[384,384]{1,0:T(8,128)(2,1)S(1)}, bf16[384,384]{1,0:T(8,128)(2,1)S(1)}, u32[]{:S(2)}, u32[]{:S(2)}) %collective-permute-start.41) | collective-permute-done | bytes 294944 | tf_op jit(solution)/shard_map/ppermute | solution.py:27
  381.3 20.2 %collective-permute-done.42.refs_2_ = bf16[384,384]{1,0:T(8,128)(2,1)S(1)} collective-permute-done((bf16[384,384]{1,0:T(8,128)(2,1)S(1)}, bf16[384,384]{1,0:T(8,128)(2,1)S(1)}, u32[]{:S(2)}, u32[]{:S(2)}) %collective-permute-start.42) | collective-permute-done | bytes 294944 | tf_op jit(solution)/shard_map/ppermute | solution.py:27
  403.2 15.7 %attend_back.1 = (bf16[1536,384]{1,0:T(8,128)(2,1)S(1)}, bf16[2,1536,384]{2,1,0:T(8,128)(2,1)S(1)}, bf16[2,1536,384]{2,1,0:T(8,128)(2,1)S(1)}) custom-call(s32[3]{0:T(128)S(1)} %copy-done.33, bf16[3,1536,384]{2,1,0:T(8,128)(2,1)S(1)} %get-tuple-element.71.query_ref.key_ref.value_ref, bf16[3,1536,384]{2,1,0:T(8,128)(2,1)S(1)} %get-tuple-element.71.query_ref.key_ref.value_ref, ...), custom_call_target="tpu_custom_call" | custom-call | flops 125829120 | bytes 344064 | tf_op jit(solution)/shard_map/attend_back/pallas_call | solution.py:517
  435.2 10.1 %project_back.1 = (bf16[1536,1152]{1,0:T(8,128)(2,1)S(1)}, bf16[4,3,128,1536]{3,2,1,0:T(8,128)(2,1)S(1)}) custom-call(bf16[1536,384]{1,0:T(8,128)(2,1)S(1)} %copy-done.25, bf16[2,1536,384]{2,1,0:T(8,128)(2,1)S(1)} %copy-done.23, bf16[2,1536,384]{2,1,0:T(8,128)(2,1)S(1)} %collective-permute-done.44.back_ref, f32[2,512,128]{2,1,0:T(8,128)S(1)} %copy-done.11, ...), custom_call_target="tpu_custom_call" | custom-call | flops 339738624 | bytes 1179648 | tf_op jit(solution)/shard_map/project_back/pallas_call | solution.py:577
  447.5 7.4 %outer.3 = bf16[1536,1152]{1,0:T(8,128)(2,1)S(1)} custom-call(bf16[1536,1536]{1,0:T(8,128)(2,1)S(1)} %bitcast.261, bf16[1536,1152]{1,0:T(8,128)(2,1)S(1)} %get-tuple-element.109.refs_1_), custom_call_target="tpu_custom_call" | custom-call | flops 339738624 | bytes 737280 | tf_op jit(solution)/shard_map/outer/pallas_call | solution.py:893
  456.3 4.8 collective-permute-start.55
  489.0 8.5 %collective-permute-done.46 = bf16[192,1536]{1,0:T(8,128)(2,1)S(1)} collective-permute-done((bf16[192,1536]{1,0:T(8,128)(2,1)S(1)}, bf16[192,1536]{1,0:T(8,128)(2,1)S(1)}, u32[]{:S(2)}, u32[]{:S(2)}) %collective-permute-start.46) | collective-permute-done | bytes 589856 | tf_op jit(solution)/shard_map/ppermute | solution.py:22
  533.0 7.3 %collective-permute-start.64 = (f32[2,192]{1,0:T(2,128)S(1)}, f32[2,192]{1,0:T(2,128)S(1)}, u32[]{:S(2)}, u32[]{:S(2)}) collective-permute-start(f32[2,192]{1,0:T(2,128)S(1)} %pad_maximum_fusion.15), channel_id=1, source_target_pairs={{0,1},{1,2},{2,3},{3,0},{4,5},{5,6},{6,7},{7,4},{8,9},{9,10},{10,1... | collective-permute-start | bytes 4616 | tf_op jit(solution)/shard_map/ppermute | solution.py:27
  551.5 6.9 %collective-permute-start.52 = (bf16[192,384]{1,0:T(8,128)(2,1)S(1)}, bf16[192,384]{1,0:T(8,128)(2,1)S(1)}, u32[]{:S(2)}, u32[]{:S(2)}) collective-permute-start(bf16[192,384]{1,0:T(8,128)(2,1)S(1)} %get-tuple-element.222), channel_id=1, source_target_pairs={{0,1},{1,2},{2,3},{3,0},{4,5},{5,6},{6,7},{7,4},{8,9},{9,10},{10,1... | collective-permute-start | bytes 442376 | tf_op jit(solution)/shard_map/ppermute | solution.py:27
  564.2 4.1 collective-permute-done.53
  (408 shorter events, 246.3 us)
Async XLA Ops:
  7.2 134.0 %all-gather.4.cloned.1.call-start = ((), (), s32[]{:S(2)}) async-start(), calls=%async_computation.3 | async-start | bytes 5898240 | tf_op jit(solution)/shard_map/all_gather | solution.py:950
  7.9 212.9 %all-gather.6.cloned.1.call-start = ((), (), s32[]{:S(2)}) async-start(), calls=%async_computation.7 | async-start | bytes 5898240 | tf_op jit(solution)/shard_map/all_gather | solution.py:977
  8.0 18.4 %collective-permute-start.4 = (bf16[384,192]{0,1:T(8,128)(2,1)}, bf16[384,192]{0,1:T(8,128)(2,1)S(1)}, u32[]{:S(2)}, u32[]{:S(2)}) collective-permute-start(bf16[384,192]{0,1:T(8,128)(2,1)} %param.14), channel_id=1, source_target_pairs={{0,1},{1,2},{2,3},{3,0},{4,5},{5,6},{6,7},{7,4},{8,9},{9,10},{10,1... | collective-permute-start | bytes 442376 | tf_op jit(solution)/shard_map/ppermute | solution.py:27
  19.4 51.0 %collective-permute-start = (bf16[2,192]{1,0:T(2,128)(2,1)S(1)}, bf16[2,192]{1,0:T(2,128)(2,1)S(1)}, u32[]{:S(2)}, u32[]{:S(2)}) collective-permute-start(bf16[2,192]{1,0:T(2,128)(2,1)S(1)} %get-tuple-element.167), channel_id=1, source_target_pairs={{0,8},{8,0},{16,24},{24,16},{1,9},{9,1},{17,25},{25,17},{2,10},{10... | collective-permute-start | bytes 2312 | tf_op jit(solution)/shard_map/ppermute | solution.py:22
  26.3 44.6 %collective-permute-start.1 = (bf16[2,192]{1,0:T(2,128)(2,1)S(1)}, bf16[2,192]{1,0:T(2,128)(2,1)S(1)}, u32[]{:S(2)}, u32[]{:S(2)}) collective-permute-start(bf16[2,192]{1,0:T(2,128)(2,1)S(1)} %get-tuple-element.167), channel_id=1, source_target_pairs={{0,16},{8,24},{16,0},{24,8},{1,17},{9,25},{17,1},{25,9},{2,18},{10... | collective-permute-start | bytes 2312 | tf_op jit(solution)/shard_map/ppermute | solution.py:22
  32.3 19.5 %collective-permute-start.8 = (bf16[2,4,48,384]{3,2,1,0:T(8,128)(2,1)S(1)}, bf16[2,4,48,384]{3,2,1,0:T(8,128)(2,1)S(1)}, u32[]{:S(2)}, u32[]{:S(2)}) collective-permute-start(bf16[2,4,48,384]{3,2,1,0:T(8,128)(2,1)S(1)} %get-tuple-element.214), channel_id=1, source_target_pairs={{0,8},{8,0},{16,24},{24,16},{1,9},{9,1},{17,25},{25,17},{2,10},{10... | collective-permute-start | bytes 884744 | tf_op jit(solution)/shard_map/ppermute | solution.py:22
  47.2 24.8 %collective-permute-start.2 = (bf16[2,192]{1,0:T(2,128)(2,1)S(1)}, bf16[2,192]{1,0:T(2,128)(2,1)S(1)}, u32[]{:S(2)}, u32[]{:S(2)}) collective-permute-start(bf16[2,192]{1,0:T(2,128)(2,1)S(1)} %get-tuple-element.167), channel_id=1, source_target_pairs={{0,24},{8,16},{16,8},{24,0},{1,25},{9,17},{17,9},{25,1},{2,26},{10... | collective-permute-start | bytes 2312 | tf_op jit(solution)/shard_map/ppermute | solution.py:22
  65.6 57.4 %collective-permute-start.24 = (bf16[4,192,1152]{2,1,0:T(8,128)(2,1)S(1)}, bf16[4,192,1152]{2,1,0:T(8,128)(2,1)}, u32[]{:S(2)}, u32[]{:S(2)}) collective-permute-start(bf16[4,192,1152]{2,1,0:T(8,128)(2,1)S(1)} %fusion.19), channel_id=1, source_target_pairs={{0,4},{4,0},{1,5},{5,1},{2,6},{6,2},{3,7},{7,3},{8,12},{12,8},{9,1... | collective-permute-start | bytes 5308424 | tf_op jit(solution)/shard_map/ppermute | solution.py:22
  67.6 35.5 %collective-permute-start.11 = (bf16[384,1536]{1,0:T(8,128)(2,1)S(1)}, bf16[384,1536]{1,0:T(8,128)(2,1)}, u32[]{:S(2)}, u32[]{:S(2)}) collective-permute-start(bf16[384,1536]{1,0:T(8,128)(2,1)S(1)} %bitcast.266), channel_id=1, source_target_pairs={{0,8},{8,0},{16,24},{24,16},{1,9},{9,1},{17,25},{25,17},{2,10},{10... | collective-permute-start | bytes 3538952 | tf_op jit(solution)/shard_map/ppermute | solution.py:22
  68.1 354.6 %reduce-scatter.4.cloned.1.call-start = ((), (), s32[]{:S(2)}) async-start(), calls=%async_computation.4 | async-start | bytes 2949120 | tf_op jit(solution)/shard_map/reduce_scatter | solution.py:1009
  71.5 35.0 %collective-permute-start.18 = (bf16[384,1536]{1,0:T(8,128)(2,1)S(1)}, bf16[384,1536]{1,0:T(8,128)(2,1)}, u32[]{:S(2)}, u32[]{:S(2)}) collective-permute-start(bf16[384,1536]{1,0:T(8,128)(2,1)S(1)} %bitcast.267), channel_id=1, source_target_pairs={{0,16},{8,24},{16,0},{24,8},{1,17},{9,25},{17,1},{25,9},{2,18},{10... | collective-permute-start | bytes 3538952 | tf_op jit(solution)/shard_map/ppermute | solution.py:22
  107.6 17.2 %collective-permute-start.19 = (bf16[192,1536]{1,0:T(8,128)(2,1)S(1)}, bf16[192,1536]{1,0:T(8,128)(2,1)S(1)}, u32[]{:S(2)}, u32[]{:S(2)}) collective-permute-start(bf16[192,1536]{1,0:T(8,128)(2,1)S(1)} %slice.313), channel_id=1, source_target_pairs={{0,8},{8,0},{16,24},{24,16},{1,9},{9,1},{17,25},{25,17},{2,10},{10... | collective-permute-start | bytes 1769480 | tf_op jit(solution)/shard_map/ppermute | solution.py:22
  136.5 30.3 %collective-permute-start.15 = (bf16[96,1536]{1,0:T(8,128)(2,1)}, bf16[96,1536]{1,0:T(8,128)(2,1)}, u32[]{:S(2)}, u32[]{:S(2)}) collective-permute-start(bf16[96,1536]{1,0:T(8,128)(2,1)} %slice.310), channel_id=1, source_target_pairs={{0,16},{8,24},{16,0},{24,8},{1,17},{9,25},{17,1},{25,9},{2,18},{10... | collective-permute-start | bytes 884744 | tf_op jit(solution)/shard_map/ppermute | solution.py:22
  138.0 28.8 %collective-permute-start.16 = (bf16[96,1536]{1,0:T(8,128)(2,1)}, bf16[96,1536]{1,0:T(8,128)(2,1)}, u32[]{:S(2)}, u32[]{:S(2)}) collective-permute-start(bf16[96,1536]{1,0:T(8,128)(2,1)} %slice.311), channel_id=1, source_target_pairs={{0,8},{8,0},{16,24},{24,16},{1,9},{9,1},{17,25},{25,17},{2,10},{10... | collective-permute-start | bytes 884744 | tf_op jit(solution)/shard_map/ppermute | solution.py:22
  168.7 21.4 %collective-permute-start.17 = (bf16[4,192,1536]{2,1,0:T(8,128)(2,1)}, bf16[4,192,1536]{2,1,0:T(8,128)(2,1)}, u32[]{:S(2)}, u32[]{:S(2)}) collective-permute-start(bf16[4,192,1536]{2,1,0:T(8,128)(2,1)} %fusion.16), channel_id=1, source_target_pairs={{0,4},{4,0},{1,5},{5,1},{2,6},{6,2},{3,7},{7,3},{8,12},{12,8},{9,1... | collective-permute-start | bytes 7077896 | tf_op jit(solution)/shard_map/ppermute | solution.py:22
  187.0 24.9 %collective-permute-start.27 = (bf16[384,384]{1,0:T(8,128)(2,1)S(1)}, bf16[384,384]{1,0:T(8,128)(2,1)S(1)}, u32[]{:S(2)}, u32[]{:S(2)}) collective-permute-start(bf16[384,384]{1,0:T(8,128)(2,1)S(1)} %get-tuple-element.74), channel_id=1, source_target_pairs={{0,2},{1,3},{2,0},{3,1},{4,6},{5,7},{6,4},{7,5},{8,10},{9,11},{10,... | collective-permute-start | bytes 884744 | tf_op jit(solution)/shard_map/ppermute | solution.py:27
  189.6 22.2 %collective-permute-start.28 = (bf16[384,384]{1,0:T(8,128)(2,1)S(1)}, bf16[384,384]{1,0:T(8,128)(2,1)S(1)}, u32[]{:S(2)}, u32[]{:S(2)}) collective-permute-start(bf16[384,384]{1,0:T(8,128)(2,1)S(1)} %get-tuple-element.75), channel_id=1, source_target_pairs={{0,3},{1,0},{2,1},{3,2},{4,7},{5,4},{6,5},{7,6},{8,11},{9,8},{10,9... | collective-permute-start | bytes 884744 | tf_op jit(solution)/shard_map/ppermute | solution.py:27
  220.8 45.8 %collective-permute-start.29 = (bf16[4,2,4,48,1536]{4,3,2,1,0:T(8,128)(2,1)}, bf16[4,2,4,48,1536]{4,3,2,1,0:T(8,128)(2,1)}, u32[]{:S(2)}, u32[]{:S(2)}) collective-permute-start(bf16[4,2,4,48,1536]{4,3,2,1,0:T(8,128)(2,1)} %bitcast.273), channel_id=1, source_target_pairs={{0,4},{4,0},{1,5},{5,1},{2,6},{6,2},{3,7},{7,3},{8,12},{12,8},{9,1... | collective-permute-start | bytes 14155784 | tf_op jit(solution)/shard_map/ppermute | solution.py:22
  222.5 28.1 %collective-permute-start.30 = (bf16[384,1536]{1,0:T(8,128)(2,1)}, bf16[384,1536]{1,0:T(8,128)(2,1)S(1)}, u32[]{:S(2)}, u32[]{:S(2)}) collective-permute-start(bf16[384,1536]{1,0:T(8,128)(2,1)} %copy-done.31), channel_id=1, source_target_pairs={{0,8},{8,0},{16,24},{24,16},{1,9},{9,1},{17,25},{25,17},{2,10},{10... | collective-permute-start | bytes 3538952 | tf_op jit(solution)/shard_map/ppermute | solution.py:22
  224.1 28.2 %collective-permute-start.31 = (bf16[384,1536]{1,0:T(8,128)(2,1)}, bf16[384,1536]{1,0:T(8,128)(2,1)S(1)}, u32[]{:S(2)}, u32[]{:S(2)}) collective-permute-start(bf16[384,1536]{1,0:T(8,128)(2,1)} %copy-done.31), channel_id=1, source_target_pairs={{0,16},{8,24},{16,0},{24,8},{1,17},{9,25},{17,1},{25,9},{2,18},{10... | collective-permute-start | bytes 3538952 | tf_op jit(solution)/shard_map/ppermute | solution.py:22
  291.0 26.0 %collective-permute-start.35 = (bf16[2,192,1536]{2,1,0:T(8,128)(2,1)}, bf16[2,192,1536]{2,1,0:T(8,128)(2,1)S(1)}, u32[]{:S(2)}, u32[]{:S(2)}) collective-permute-start(bf16[2,192,1536]{2,1,0:T(8,128)(2,1)} %get-tuple-element.93), channel_id=1, source_target_pairs={{0,16},{8,24},{16,0},{24,8},{1,17},{9,25},{17,1},{25,9},{2,18},{10... | collective-permute-start | bytes 3538952 | tf_op jit(solution)/shard_map/ppermute | solution.py:22
  292.0 25.7 %collective-permute-start.34 = (bf16[2,192,1536]{2,1,0:T(8,128)(2,1)}, bf16[2,192,1536]{2,1,0:T(8,128)(2,1)S(1)}, u32[]{:S(2)}, u32[]{:S(2)}) collective-permute-start(bf16[2,192,1536]{2,1,0:T(8,128)(2,1)} %get-tuple-element.92), channel_id=1, source_target_pairs={{0,8},{8,0},{16,24},{24,16},{1,9},{9,1},{17,25},{25,17},{2,10},{10... | collective-permute-start | bytes 3538952 | tf_op jit(solution)/shard_map/ppermute | solution.py:22
  332.7 128.5 %reduce-scatter.6.cloned.1.call-start = ((), (), s32[]{:S(2)}) async-start(), calls=%async_computation.5 | async-start | bytes 2949120 | tf_op jit(solution)/shard_map/reduce_scatter | solution.py:1009
  333.2 235.9 %reduce-scatter.8.cloned.1.call-start = ((), (), s32[]{:S(2)}) async-start(), calls=%async_computation.6 | async-start | bytes 5898240 | tf_op jit(solution)/shard_map/reduce_scatter | solution.py:1028
  361.0 20.4 %collective-permute-start.41 = (bf16[384,384]{1,0:T(8,128)(2,1)S(1)}, bf16[384,384]{1,0:T(8,128)(2,1)S(1)}, u32[]{:S(2)}, u32[]{:S(2)}) collective-permute-start(bf16[384,384]{1,0:T(8,128)(2,1)S(1)} %get-tuple-element.102), channel_id=1, source_target_pairs={{0,1},{1,2},{2,3},{3,0},{4,5},{5,6},{6,7},{7,4},{8,9},{9,10},{10,1... | collective-permute-start | bytes 884744 | tf_op jit(solution)/shard_map/ppermute | solution.py:27
  366.9 34.6 %collective-permute-start.42 = (bf16[384,384]{1,0:T(8,128)(2,1)S(1)}, bf16[384,384]{1,0:T(8,128)(2,1)S(1)}, u32[]{:S(2)}, u32[]{:S(2)}) collective-permute-start(bf16[384,384]{1,0:T(8,128)(2,1)S(1)} %get-tuple-element.103), channel_id=1, source_target_pairs={{0,2},{1,3},{2,0},{3,1},{4,6},{5,7},{6,4},{7,5},{8,10},{9,11},{10,... | collective-permute-start | bytes 884744 | tf_op jit(solution)/shard_map/ppermute | solution.py:27
  367.5 34.0 %collective-permute-start.43 = (bf16[384,384]{1,0:T(8,128)(2,1)S(1)}, bf16[384,384]{1,0:T(8,128)(2,1)S(1)}, u32[]{:S(2)}, u32[]{:S(2)}) collective-permute-start(bf16[384,384]{1,0:T(8,128)(2,1)S(1)} %get-tuple-element.104), channel_id=1, source_target_pairs={{0,3},{1,0},{2,1},{3,2},{4,7},{5,4},{6,5},{7,6},{8,11},{9,8},{10,9... | collective-permute-start | bytes 884744 | tf_op jit(solution)/shard_map/ppermute | solution.py:27
  428.8 46.9 %collective-permute-start.40 = (bf16[2,192,1536]{2,1,0:T(8,128)(2,1)}, bf16[2,192,1536]{2,1,0:T(8,128)(2,1)}, u32[]{:S(2)}, u32[]{:S(2)}) collective-permute-start(bf16[2,192,1536]{2,1,0:T(8,128)(2,1)} %pad_maximum_fusion.4), channel_id=1, source_target_pairs={{0,16},{8,24},{16,0},{24,8},{1,17},{9,25},{17,1},{25,9},{2,18},{10... | collective-permute-start | bytes 3538952 | tf_op jit(solution)/shard_map/ppermute | solution.py:22
  431.4 46.1 %collective-permute-start.39 = (bf16[2,192,1536]{2,1,0:T(8,128)(2,1)}, bf16[2,192,1536]{2,1,0:T(8,128)(2,1)}, u32[]{:S(2)}, u32[]{:S(2)}) collective-permute-start(bf16[2,192,1536]{2,1,0:T(8,128)(2,1)} %pad_maximum_fusion.3), channel_id=1, source_target_pairs={{0,8},{8,0},{16,24},{24,16},{1,9},{9,1},{17,25},{25,17},{2,10},{10... | collective-permute-start | bytes 3538952 | tf_op jit(solution)/shard_map/ppermute | solution.py:22
  456.3 47.5 %collective-permute-start.55 = (bf16[4,192,1152]{2,1,0:T(8,128)(2,1)}, bf16[4,192,1152]{2,1,0:T(8,128)(2,1)}, u32[]{:S(2)}, u32[]{:S(2)}) collective-permute-start(bf16[4,192,1152]{2,1,0:T(8,128)(2,1)} %dynamic-slice_bitcast_fusion.1), channel_id=1, source_target_pairs={{0,4},{4,0},{1,5},{5,1},{2,6},{6,2},{3,7},{7,3},{8,12},{12,8},{9,1... | collective-permute-start | bytes 5308424 | tf_op jit(solution)/shard_map/ppermute | solution.py:22
  477.5 47.6 %collective-permute-start.47 = (bf16[4,192,1536]{2,1,0:T(8,128)(2,1)}, bf16[4,192,1536]{2,1,0:T(8,128)(2,1)}, u32[]{:S(2)}, u32[]{:S(2)}) collective-permute-start(bf16[4,192,1536]{2,1,0:T(8,128)(2,1)} %dynamic-slice_bitcast_fusion), channel_id=1, source_target_pairs={{0,4},{4,0},{1,5},{5,1},{2,6},{6,2},{3,7},{7,3},{8,12},{12,8},{9,1... | collective-permute-start | bytes 7077896 | tf_op jit(solution)/shard_map/ppermute | solution.py:22
  480.1 17.4 %collective-permute-start.46 = (bf16[192,1536]{1,0:T(8,128)(2,1)S(1)}, bf16[192,1536]{1,0:T(8,128)(2,1)S(1)}, u32[]{:S(2)}, u32[]{:S(2)}) collective-permute-start(bf16[192,1536]{1,0:T(8,128)(2,1)S(1)} %fusion.10), channel_id=1, source_target_pairs={{0,8},{8,0},{16,24},{24,16},{1,9},{9,1},{17,25},{25,17},{2,10},{10... | collective-permute-start | bytes 1769480 | tf_op jit(solution)/shard_map/ppermute | solution.py:22
  (113 other events, 1075.4 us)
Sparse Core Ops, SparseCore 0:
  9.6 93.5 all-gather.3
  105.3 102.1 all-gather.5
  332.8 67.6 reduce-scatter.3
  402.6 49.5 reduce-scatter.5
  467.0 90.4 reduce-scatter.7
